TPU v7x, 32 devices: a whole 2x2x4 slice. The times are simulated.
32 devices in a mesh: stream: 4 (over y, x), tile: 8 (over z, core).
Axes of the slice: x: 2, y: 2, z: 4, core: 2. Of those that a mesh axis runs over, the one named last changes fastest.
Arguments:
- concentration: bfloat16 [2, 768, 256, 128], P(None, 'stream', 'tile'), may hold values from 0.29882812 to 3
- potential: bfloat16 [768, 256, 128], P('stream', 'tile'), may hold values from -4 to 4
- diffusivity: bfloat16 [768, 256, 128], P('stream', 'tile'), may hold values from 0.5 to 2
- spacer: int32 [768, 256, 128], P('stream', 'tile'), may hold values 0 or 1
- velocity: bfloat16 [3, 768, 256, 128], P(None, 'stream', 'tile'), may hold values from -4 to 4
- balance_plan: int32 [768, 1], P(('stream', 'tile')), may hold values from 0 to 7; in each aligned block of 24 rows (0 to 23, 24 to 47, ...) at most 6 rows name the same one
Outputs:
- concentration_next: bfloat16 [2, 768, 256, 128], P(None, 'stream', 'tile')
- velocity_next: bfloat16 [3, 768, 256, 128], P(None, 'stream', 'tile')
- owned_charge: bfloat16 [1536, 32, 1024], P(('stream', 'tile'))
Inputs may be any that keep to these rules, and one draw needn't show every extreme that they name: 1 marks fluid, 0 a spacer filament. `balance_plan`: the 24 blocks of one slab tile (aligned rows of one device) name owners among the 8 tiles of the same slab; at most 6 of them name the same owner, and some slab tile has exactly 6 with one owner.
All inputs are finite; a program needn't handle non-finite values. No bound on the sum of `spacer` on one device may be relied on, other than what follows from the above.
Results may differ from a plain program's by a relative error of at most 0.011.
Values may be sent and summed in bfloat16 or wider, within the bound.
No kernel may reach another device: no remote copies, remote signals or barrier semaphores. Data moves between devices by JAX's collectives and lax.ppermute only.
A program may use at most 256 MiB of HBM per device.

v0:
```python
import functools

import jax
import jax.numpy as jnp
from jax import lax
from jax.experimental import pallas as pl
from jax.experimental.pallas import tpu as pltpu
from jax.sharding import PartitionSpec as P

BLK = 32
GRP = 16
TOP = 8
ROWS = 48

ion_step = 0.04
flow_step = 0.1
viscosity = 0.5
species_diff = (1.0, 1.5)

F32 = jnp.float32
BF16 = jnp.bfloat16


def rings(axis):
    count = lax.axis_size(axis)
    forward = [(i, (i + 1) % count) for i in range(count)]
    backward = [(target, source) for source, target in forward]
    return forward, backward


def edges(stack):
    x_fwd, x_bwd = rings("stream")
    y_fwd, y_bwd = rings("tile")
    return (
        lax.ppermute(stack(-1, None), "stream", x_fwd),
        lax.ppermute(stack(0, None), "stream", x_bwd),
        lax.ppermute(stack(None, -1), "tile", y_fwd),
        lax.ppermute(stack(None, 0), "tile", y_bwd),
    )


def pick(array, x, y):
    if x is not None:
        return array[..., x, :, :]
    return array[..., y, :]


def roll_lanes(value, shift):
    return pltpu.roll(value, shift % value.shape[-1], axis=value.ndim - 1)


def face(low, high):
    f = low[3] * high[3]
    h = f * (high[2] - low[2])
    a = f + h
    b = f - h
    return a * high[0] - b * low[0], b * high[1] - a * low[1]


def ion_kernel(
    capacity,
    plan,
    c_hbm,
    p_hbm,
    d_hbm,
    s_hbm,
    xl_hbm,
    xh_hbm,
    yl_hbm,
    yh_hbm,
    cn_hbm,
    out_hbm,
    c_v,
    p_v,
    d_v,
    s_v,
    xl_v,
    xh_v,
    yl_v,
    yh_v,
    yl_f,
    yh_f,
    fld,
    cn_v,
    chs,
    blk,
    zero,
    perm,
    lanes,
    tally,
    in_sem,
    halo_sem,
    cn_sem,
    blk_sem,
    zero_sem,
):
    nx, nz = p_hbm.shape[0], p_hbm.shape[2]
    chunks = nx // BLK
    bz = nz // BLK
    slots = out_hbm.shape[0]
    tiles = slots // capacity
    count = chunks * bz

    def loads(i):
        part = pl.ds(i * BLK, BLK)
        return (
            pltpu.make_async_copy(c_hbm.at[:, part], c_v.at[:, part], in_sem.at[0, i]),
            pltpu.make_async_copy(p_hbm.at[part], p_v.at[part], in_sem.at[1, i]),
            pltpu.make_async_copy(d_hbm.at[part], d_v.at[part], in_sem.at[2, i]),
            pltpu.make_async_copy(s_hbm.at[part], s_v.at[part], in_sem.at[3, i]),
        )

    halos = (
        pltpu.make_async_copy(xl_hbm, xl_v, halo_sem.at[0]),
        pltpu.make_async_copy(xh_hbm, xh_v, halo_sem.at[1]),
        pltpu.make_async_copy(yl_hbm, yl_v, halo_sem.at[2]),
        pltpu.make_async_copy(yh_hbm, yh_v, halo_sem.at[3]),
    )
    for copy in halos:
        copy.start()
    for i in range(chunks):
        for copy in loads(i):
            copy.start()

    zero[...] = jnp.zeros_like(zero)
    width = BLK * GRP
    r = lax.broadcasted_iota(jnp.int32, (width, width), 0)
    c = lax.broadcasted_iota(jnp.int32, (width, width), 1)
    hit = (r // GRP == c % BLK) & (r % GRP == c // BLK)
    perm[...] = jnp.where(hit, 1.0, 0.0).astype(BF16)
    wide = bz * nz
    r = lax.broadcasted_iota(jnp.int32, (wide, wide), 0)
    c = lax.broadcasted_iota(jnp.int32, (wide, wide), 1)
    hit = (r // nz == (c % nz) // BLK) & (r % nz == (c // nz) * BLK + c % BLK)
    lanes[...] = jnp.where(hit, 1.0, 0.0).astype(BF16)

    @pl.loop(0, tiles)
    def _(o):
        tally[count + o] = 0

    @pl.loop(0, count)
    def _(b):
        o = plan[b]
        rank = tally[count + o]
        tally[b] = o * capacity + rank
        tally[count + o] = rank + 1

    def blank(slot):
        return pltpu.make_async_copy(zero, out_hbm.at[slot], zero_sem.at[slot])

    @pl.loop(0, tiles)
    def _(o):
        @pl.loop(tally[count + o], capacity)
        def _(k):
            blank(o * capacity + k).start()

    for copy in halos:
        copy.wait()
    body = pl.ds(TOP, BLK)

    def root(o):
        return o * lax.rsqrt(jnp.maximum(o, 0.25))

    for plane, ref in ((0, xl_v), (nx + 1, xh_v)):
        for f in range(4):
            v = ref[f].astype(F32)
            v = v * 0.5 if f == 2 else (root(v) if f == 3 else v)
            fld[f, plane, body, :] = v
    for ref, dst in ((yl_v, yl_f), (yh_v, yh_f)):
        for f in range(4):
            v = ref[f].astype(F32)
            v = v * 0.5 if f == 2 else (root(v) if f == 3 else v)
            dst[f] = v

    def prepare(i):
        for copy in loads(i):
            copy.wait()

        @pl.loop(0, BLK)
        def _(q):
            x = i * BLK + q
            fld[0, x + 1, body, :] = c_v[0, x].astype(F32)
            fld[1, x + 1, body, :] = c_v[1, x].astype(F32)
            fld[2, x + 1, body, :] = p_v[x].astype(F32) * 0.5
            d = d_v[x].astype(F32)
            fld[3, x + 1, body, :] = jnp.where(s_v[x] > 0, d * lax.rsqrt(d), 0.0)
            for f in range(4):
                fld[f, x + 1, pl.ds(TOP - 1, 1), :] = yl_f[f, pl.ds(x, 1), :]
                fld[f, x + 1, pl.ds(TOP + BLK, 1), :] = yh_f[f, pl.ds(x, 1), :]

    def plane_of(x, rows):
        return [fld[f, x, rows, :] for f in range(4)]

    first_lane = lax.broadcasted_iota(jnp.int32, (BLK, nz), 1) == 0

    def update(i, carry):
        def step(q, carry):
            x = i * BLK + q
            mid = plane_of(x + 1, body)
            fx = face(mid, plane_of(x + 2, body))
            fy = face(
                plane_of(x + 1, pl.ds(TOP - 1, BLK + 8)), plane_of(x + 1, pl.ds(TOP, BLK + 8))
            )
            below = [roll_lanes(v, 1) for v in mid]
            below[3] = jnp.where(first_lane, 0.0, below[3])
            fz = face(below, mid)
            new = []
            for s in range(2):
                total = (fx[s] - carry[s]) + (fy[s][1 : BLK + 1] - fy[s][:BLK])
                total = total + (roll_lanes(fz[s], -1) - fz[s])
                new.append((mid[s] + (ion_step * species_diff[s]) * total).astype(BF16))
                cn_v[s, x] = new[s]
            charge = new[0].astype(F32) - new[1].astype(F32)
            chs[pl.ds(pl.multiple_of(q * BLK, BLK), BLK), :] = charge.astype(BF16)
            return fx

        return lax.fori_loop(0, BLK, step, carry)

    def saves(i):
        part = pl.ds(i * BLK, BLK)
        return pltpu.make_async_copy(cn_v.at[:, part], cn_hbm.at[:, part], cn_sem.at[i])

    def put(b):
        return pltpu.make_async_copy(blk.at[b], out_hbm.at[tally[b]], blk_sem.at[b])

    prepare(0)
    start = face(plane_of(0, body), plane_of(1, body))

    def chunk(i, carry):
        @pl.when(i + 1 < chunks)
        def _():
            prepare(i + 1)

        carry = update(i, carry)
        saves(i).start()
        for g in range(BLK // GRP):
            t = jnp.dot(perm[...], chs[g * width : (g + 1) * width, :], preferred_element_type=F32)
            t = t.astype(BF16)
            wideset = jnp.concatenate(
                [
                    jnp.concatenate(
                        [t[(j * bz + m) * GRP : (j * bz + m + 1) * GRP] for m in range(bz)], axis=1
                    )
                    for j in range(BLK // bz)
                ],
                axis=0,
            )
            res = jnp.dot(wideset, lanes[...], preferred_element_type=F32).astype(BF16)
            for k in range(bz):
                for j in range(BLK // bz):
                    blk[i * bz + k, g * GRP : (g + 1) * GRP, j * nz : (j + 1) * nz] = res[
                        j * GRP : (j + 1) * GRP, k * nz : (k + 1) * nz
                    ]
        for k in range(bz):
            put(i * bz + k).start()
        return carry

    lax.fori_loop(0, chunks, chunk, start)

    @pl.loop(0, chunks)
    def _(i):
        saves(i).wait()

    @pl.loop(0, count)
    def _(b):
        put(b).wait()

    @pl.loop(0, tiles)
    def _(o):
        @pl.loop(tally[count + o], capacity)
        def _(k):
            blank(o * capacity + k).wait()


def ion_call(plan, c, p, d, s, halo, capacity, tiles):
    _, nx, ny, nz = c.shape
    count = plan.shape[0]
    chunks = nx // BLK
    bz = nz // BLK
    anywhere = pl.BlockSpec(memory_space=pl.ANY)
    vm = pltpu.VMEM
    dma = pltpu.SemaphoreType.DMA
    return pl.pallas_call(
        functools.partial(ion_kernel, capacity),
        name="ion",
        out_shape=(
            jax.ShapeDtypeStruct(c.shape, BF16),
            jax.ShapeDtypeStruct((tiles * capacity, BLK, BLK * BLK), BF16),
        ),
        in_specs=[pl.BlockSpec(memory_space=pltpu.SMEM)] + [anywhere] * 8,
        out_specs=(anywhere, anywhere),
        scratch_shapes=[
            vm(c.shape, BF16),
            vm(p.shape, BF16),
            vm(d.shape, BF16),
            vm(s.shape, jnp.int32),
            vm((4, ny, nz), BF16),
            vm((4, ny, nz), BF16),
            vm((4, nx, nz), BF16),
            vm((4, nx, nz), BF16),
            vm((4, nx, nz), F32),
            vm((4, nx, nz), F32),
            vm((4, nx + 2, ROWS, nz), F32),
            vm(c.shape, BF16),
            vm((BLK * BLK, nz), BF16),
            vm((count, BLK, BLK * BLK), BF16),
            vm((BLK, BLK * BLK), BF16),
            vm((BLK * GRP, BLK * GRP), BF16),
            vm((bz * nz, bz * nz), BF16),
            pltpu.SMEM((count + tiles,), jnp.int32),
            dma((4, chunks)),
            dma((4,)),
            dma((chunks,)),
            dma((count,)),
            dma((tiles * capacity,)),
        ],
        compiler_params=pltpu.CompilerParams(vmem_limit_bytes=52 * 2**20),
        cost_estimate=pl.CostEstimate(
            flops=60 * p.size, bytes_accessed=20 * p.size, transcendentals=p.size
        ),
    )(plan, c, p, d, s, *halo)


def flow_kernel(
    u_hbm,
    p_hbm,
    s_hbm,
    cn_hbm,
    uxl_hbm,
    uxh_hbm,
    uyl_hbm,
    uyh_hbm,
    pxl_hbm,
    pxh_hbm,
    pyl_hbm,
    pyh_hbm,
    un_hbm,
    u_v,
    p_v,
    s_v,
    cn_v,
    uxl_v,
    uxh_v,
    uyl_v,
    uyh_v,
    pxl_v,
    pxh_v,
    pyl_v,
    pyh_v,
    yl_f,
    yh_f,
    fld,
    un_v,
    in_sem,
    halo_sem,
    un_sem,
):
    nx, nz = p_hbm.shape[0], p_hbm.shape[2]
    chunks = nx // BLK

    def loads(i):
        part = pl.ds(i * BLK, BLK)
        return (
            pltpu.make_async_copy(u_hbm.at[:, part], u_v.at[:, part], in_sem.at[0, i]),
            pltpu.make_async_copy(p_hbm.at[part], p_v.at[part], in_sem.at[1, i]),
            pltpu.make_async_copy(s_hbm.at[part], s_v.at[part], in_sem.at[2, i]),
            pltpu.make_async_copy(cn_hbm.at[:, part], cn_v.at[:, part], in_sem.at[3, i]),
        )

    pairs = (
        (uxl_hbm, uxl_v),
        (uxh_hbm, uxh_v),
        (uyl_hbm, uyl_v),
        (uyh_hbm, uyh_v),
        (pxl_hbm, pxl_v),
        (pxh_hbm, pxh_v),
        (pyl_hbm, pyl_v),
        (pyh_hbm, pyh_v),
    )
    halos = [
        pltpu.make_async_copy(src.at[2] if n > 3 else src, dst, halo_sem.at[n])
        for n, (src, dst) in enumerate(pairs)
    ]
    for copy in halos:
        copy.start()
    for i in range(chunks):
        for copy in loads(i):
            copy.start()
    for copy in halos:
        copy.wait()
    body = pl.ds(TOP, BLK)
    for plane, ref, pref in ((0, uxl_v, pxl_v), (nx + 1, uxh_v, pxh_v)):
        for f in range(3):
            fld[f, plane, body, :] = ref[f].astype(F32)
        fld[3, plane, body, :] = pref[...].astype(F32)
    for ref, pref, dst in ((uyl_v, pyl_v, yl_f), (uyh_v, pyh_v, yh_f)):
        for f in range(3):
            dst[f] = ref[f].astype(F32)
        dst[3] = pref[...].astype(F32)

    def prepare(i):
        for copy in loads(i):
            copy.wait()

        @pl.loop(0, BLK)
        def _(q):
            x = i * BLK + q
            fluid = s_v[x] > 0
            for f in range(3):
                fld[f, x + 1, body, :] = jnp.where(fluid, u_v[f, x].astype(F32), 0.0)
            fld[3, x + 1, body, :] = p_v[x].astype(F32)
            for f in range(4):
                fld[f, x + 1, pl.ds(TOP - 1, 1), :] = yl_f[f, pl.ds(x, 1), :]
                fld[f, x + 1, pl.ds(TOP + BLK, 1), :] = yh_f[f, pl.ds(x, 1), :]

    half = 16
    lane = lax.broadcasted_iota(jnp.int32, (half, nz), 1)
    first_lane = lane == 0
    last_lane = lane == nz - 1
    k_mid = flow_step * viscosity
    k_adv = flow_step * 0.5

    def below(v):
        return jnp.where(first_lane, 0.0, roll_lanes(v, 1))

    def above(v):
        return jnp.where(last_lane, 0.0, roll_lanes(v, -1))

    def update(i):
        @pl.loop(0, BLK)
        def _(q):
            x = i * BLK + q
            for y0 in range(0, BLK, half):
                at = pl.ds(TOP + y0, half)
                mid = [fld[f, x + 1, at, :] for f in range(3)]
                field = fld[3, x + 1, at, :]
                fluid = s_v[x, pl.ds(y0, half), :] > 0
                cn0 = cn_v[0, x, pl.ds(y0, half), :].astype(F32)
                cn1 = cn_v[1, x, pl.ds(y0, half), :].astype(F32)
                push = (cn0 - cn1) * k_adv
                plus = [k_mid - k_adv * u for u in mid]
                minus = [k_mid + k_adv * u for u in mid]
                for a in range(3):
                    total = mid[a] * (1.0 - 6.0 * k_mid)
                    total = total + fld[a, x + 2, at, :] * plus[0] + fld[a, x, at, :] * minus[0]
                    total = total + fld[a, x + 1, pl.ds(TOP + 1 + y0, half), :] * plus[1]
                    total = total + fld[a, x + 1, pl.ds(TOP - 1 + y0, half), :] * minus[1]
                    total = total + above(mid[a]) * plus[2] + below(mid[a]) * minus[2]
                    if a == 0:
                        rise = fld[3, x + 2, at, :] - fld[3, x, at, :]
                    elif a == 1:
                        rise = (
                            fld[3, x + 1, pl.ds(TOP + 1 + y0, half), :]
                            - fld[3, x + 1, pl.ds(TOP - 1 + y0, half), :]
                        )
                    else:
                        rise = above(field) - below(field)
                    total = jnp.where(fluid, total - push * rise, 0.0)
                    un_v[a, x, pl.ds(y0, half), :] = total.astype(BF16)

    def saves(i):
        part = pl.ds(i * BLK, BLK)
        return pltpu.make_async_copy(un_v.at[:, part], un_hbm.at[:, part], un_sem.at[i])

    prepare(0)

    @pl.loop(0, chunks)
    def _(i):
        @pl.when(i + 1 < chunks)
        def _():
            prepare(i + 1)

        update(i)
        saves(i).start()

    @pl.loop(0, chunks)
    def _(i):
        saves(i).wait()


def flow_call(u, p, s, cn, uhalo, halo):
    _, nx, ny, nz = u.shape
    chunks = nx // BLK
    anywhere = pl.BlockSpec(memory_space=pl.ANY)
    vm = pltpu.VMEM
    dma = pltpu.SemaphoreType.DMA
    return pl.pallas_call(
        flow_kernel,
        name="flow",
        out_shape=jax.ShapeDtypeStruct(u.shape, BF16),
        in_specs=[anywhere] * 12,
        out_specs=anywhere,
        scratch_shapes=[
            vm(u.shape, BF16),
            vm(p.shape, BF16),
            vm(s.shape, jnp.int32),
            vm(cn.shape, BF16),
            vm((3, ny, nz), BF16),
            vm((3, ny, nz), BF16),
            vm((3, nx, nz), BF16),
            vm((3, nx, nz), BF16),
            vm((ny, nz), BF16),
            vm((ny, nz), BF16),
            vm((nx, nz), BF16),
            vm((nx, nz), BF16),
            vm((4, nx, nz), F32),
            vm((4, nx, nz), F32),
            vm((4, nx + 2, ROWS, nz), F32),
            vm(u.shape, BF16),
            dma((4, chunks)),
            dma((8,)),
            dma((chunks,)),
        ],
        compiler_params=pltpu.CompilerParams(vmem_limit_bytes=52 * 2**20),
        cost_estimate=pl.CostEstimate(
            flops=80 * p.size, bytes_accessed=20 * p.size, transcendentals=0
        ),
    )(u, p, s, cn, *uhalo, *halo)


def per_device(concentration, potential, diffusivity, spacer, velocity, balance_plan):
    tiles = lax.axis_size("tile")
    count = balance_plan.shape[0]
    capacity = max(2, (2 * count + tiles - 1) // tiles)
    slots = tiles * capacity

    def ions(x, y):
        solid = pick(spacer, x, y) > 0
        openness = pick(diffusivity, x, y)
        openness = jnp.where(solid, openness, jnp.zeros_like(openness))
        rest = jnp.stack([pick(potential, x, y), openness])
        return jnp.concatenate([pick(concentration, x, y), rest], axis=0)

    def motion(x, y):
        moving = pick(velocity, x, y)
        return jnp.where(pick(spacer, x, y)[None] > 0, moving, jnp.zeros_like(moving))

    halo = edges(ions)
    uhalo = edges(motion)
    conc_next, outgoing = ion_call(
        balance_plan[:, 0], concentration, potential, diffusivity, spacer, halo, capacity, tiles
    )
    outgoing = outgoing.reshape(tiles, capacity, BLK, BLK * BLK)
    owned = lax.all_to_all(outgoing, "tile", split_axis=0, concat_axis=0, tiled=True)
    flow_next = flow_call(velocity, potential, spacer, conc_next, uhalo, halo)
    return conc_next, flow_next, owned.reshape(slots, BLK, BLK * BLK)


def solution(mesh):
    placed = (
        P(None, "stream", "tile", None),
        P("stream", "tile", None),
        P("stream", "tile", None),
        P("stream", "tile", None),
        P(None, "stream", "tile", None),
        P(("stream", "tile"), None),
    )
    return jax.shard_map(
        per_device,
        mesh=mesh,
        in_specs=placed,
        out_specs=(
            P(None, "stream", "tile", None),
            P(None, "stream", "tile", None),
            P(("stream", "tile"), None, None),
        ),
        check_vma=False,
    )
```

profile of v0, /device:TPU:11, one launch (start us, length us, event | category | flops | bytes accessed | tf_op | source)
XLA Modules:
  0.0 171.8 jit_solution(4756796444033316489)
XLA Ops:
  0.6 0.0 copy-start
  0.6 1.3 fusion.8
  1.9 1.3 fusion.7
  3.2 1.5 fusion.6
  4.8 1.7 fusion.5
  6.5 0.1 fusion.2
  6.6 1.9 %collective-permute-start.2 = (bf16[4,192,128]{2,1,0:T(8,128)(2,1)S(1)}, bf16[4,192,128]{2,1,0:T(8,128)(2,1)S(1)}, u32[]{:S(2)}, u32[]{:S(2)}) collective-permute-start(bf16[4,192,128]{2,1,0:T(8,128)(2,1)S(1)} %pad_maximum_fusion), channel_id=1, source_target_pairs={{0,1},{1,2},{2,3},{3,4},{4,5},{5,6},{6,7},{7,0},{8,9},{9,10},{10,1... | collective-permute-start | bytes 589832 | tf_op jit(solution)/shard_map/ppermute | solution.py:37
  8.6 0.1 collective-permute-start.3
  8.6 0.7 slice_bitcast_fusion
  9.4 0.8 slice_select_fusion
  10.2 1.3 collective-permute-start
  11.5 0.3 collective-permute-start.1
  11.7 1.3 collective-permute-done.xl_hbm.pxl_hbm
  13.0 2.3 %collective-permute-done.1.xh_hbm.pxh_hbm = bf16[4,32,128]{2,1,0:T(8,128)(2,1)S(1)} collective-permute-done((bf16[4,32,128]{2,1,0:T(8,128)(2,1)S(1)}, bf16[4,32,128]{2,1,0:T(8,128)(2,1)S(1)}, u32[]{:S(2)}, u32[]{:S(2)}) %collective-permute-start.1) | collective-permute-done | bytes 32800 | tf_op jit(solution)/shard_map/ppermute | solution.py:36
  15.3 0.0 collective-permute-done.2.yl_hbm.pyl_hbm
  15.3 0.0 collective-permute-done.3.yh_hbm.pyh_hbm
  15.3 0.0 copy-done
  15.3 45.2 %ion.1 = (bf16[2,192,32,128]{3,2,1,0:T(8,128)(2,1)}, bf16[48,32,1024]{2,1,0:T(8,128)(2,1)}) custom-call(s32[24]{0:T(128)S(1)} %bitcast.49, bf16[2,192,32,128]{3,2,1,0:T(8,128)(2,1)} %c_hbm.1, bf16[192,32,128]{2,1,0:T(8,128)(2,1)} %p_hbm.3, bf16[192,32,128]{2,1,0:T(8,128)(2,1)} %d_hbm.1, s32[192,32,128]{2,1,0:T(8,128)} %s_hbm.3, ...), custom_call_target="tpu_custom_call" | custom-call | flops 47185920 | bytes 15728640 | tf_op jit(solution)/shard_map/ion/pallas_call | solution.py:283
  60.6 8.0 %all-to-all-start = ((bf16[8,6,32,1024]{3,2,1,0:T(8,128)(2,1)}), bf16[8,6,32,1024]{3,2,1,0:T(8,128)(2,1)}, u32[]{:S(2)}, u32[]{:S(2)}) async-start(bf16[8,6,32,1024]{3,2,1,0:T(8,128)(2,1)} %bitcast.50), calls=%async_computation | async-start | bytes 6291456 | tf_op jit(solution)/shard_map/all_to_all | solution.py:544
  68.6 2.1 %fusion.4 = (bf16[3,192,1,128]{3,2,1,0:T(2,128)(2,1)S(1)}, bf16[3,192,1,128]{3,2,1,0:T(2,128)(2,1)S(1)}) fusion(bf16[3,192,32,128]{3,2,1,0:T(8,128)(2,1)} %u_hbm.1), kind=kLoop, calls=%fused_computation.26 | loop fusion | bytes 589824 | tf_op jit(solution)/shard_map/slice | solution.py:45
  70.7 1.5 collective-permute-start.6
  72.2 0.1 collective-permute-start.7
  72.3 0.8 bitcast_select_fusion
  73.1 0.0 collective-permute-start.5
  73.1 2.4 %collective-permute-start.4 = (bf16[3,32,128]{2,1,0:T(8,128)(2,1)S(1)}, bf16[3,32,128]{2,1,0:T(8,128)(2,1)S(1)}, u32[]{:S(2)}, u32[]{:S(2)}) collective-permute-start(bf16[3,32,128]{2,1,0:T(8,128)(2,1)S(1)} %get-tuple-element.18), channel_id=1, source_target_pairs={{0,8},{8,16},{16,24},{24,0},{1,9},{9,17},{17,25},{25,1},{2,10},{10... | collective-permute-start | bytes 73736 | tf_op jit(solution)/shard_map/ppermute | solution.py:35
  75.4 1.6 collective-permute-done.5.uxh_hbm
  77.1 0.0 collective-permute-done.4.uxl_hbm
  77.1 62.6 %collective-permute-done.6.uyl_hbm = bf16[3,192,128]{2,1,0:T(8,128)(2,1)S(1)} collective-permute-done((bf16[3,192,128]{2,1,0:T(8,128)(2,1)S(1)}, bf16[3,192,128]{2,1,0:T(8,128)(2,1)S(1)}, u32[]{:S(2)}, u32[]{:S(2)}) %collective-permute-start.6) | collective-permute-done | bytes 147488 | tf_op jit(solution)/shard_map/ppermute | solution.py:37
  139.7 1.8 %collective-permute-done.7.uyh_hbm = bf16[3,192,128]{2,1,0:T(8,128)(2,1)S(1)} collective-permute-done((bf16[3,192,128]{2,1,0:T(8,128)(2,1)S(1)}, bf16[3,192,128]{2,1,0:T(8,128)(2,1)S(1)}, u32[]{:S(2)}, u32[]{:S(2)}) %collective-permute-start.7) | collective-permute-done | bytes 147488 | tf_op jit(solution)/shard_map/ppermute | solution.py:38
  141.5 26.2 %flow.1 = bf16[3,192,32,128]{3,2,1,0:T(8,128)(2,1)} custom-call(bf16[3,192,32,128]{3,2,1,0:T(8,128)(2,1)} %u_hbm.1, bf16[192,32,128]{2,1,0:T(8,128)(2,1)} %p_hbm.3, s32[192,32,128]{2,1,0:T(8,128)} %s_hbm.3, bf16[2,192,32,128]{3,2,1,0:T(8,128)(2,1)} %get-tuple-element.40.cn_hbm, bf16[3,32,128]{2,1,0:T(8,128)(2,1)S(1)} %collective-permute-done.4.uxl_hbm, ...), custom_call_target="tpu_custom_call" | custom-call | flops 62914560 | bytes 15728640 | tf_op jit(solution)/shard_map/flow/pallas_call | solution.py:487
  167.7 0.0 all-to-all-done
  167.7 4.1 %copy.58 = bf16[48,32,1024]{2,1,0:T(8,128)(2,1)} copy(bf16[48,32,1024]{2,1,0:T(8,128)(2,1)} %bitcast.18) | data formatting | bytes 6291456
  (10 shorter events, 0.2 us)
Async XLA Ops:
  0.6 14.7 %copy-start = (s32[24,1]{0,1:T(1,128)S(1)}, s32[24,1]{0,1:T(1,128)}, u32[]{:S(2)}) copy-start(s32[24,1]{0,1:T(1,128)} %param.11) | copy-start | bytes 292
  6.6 8.7 %collective-permute-start.2 = (bf16[4,192,128]{2,1,0:T(8,128)(2,1)S(1)}, bf16[4,192,128]{2,1,0:T(8,128)(2,1)S(1)}, u32[]{:S(2)}, u32[]{:S(2)}) collective-permute-start(bf16[4,192,128]{2,1,0:T(8,128)(2,1)S(1)} %pad_maximum_fusion), channel_id=1, source_target_pairs={{0,1},{1,2},{2,3},{3,4},{4,5},{5,6},{6,7},{7,0},{8,9},{9,10},{10,1... | collective-permute-start | bytes 589832 | tf_op jit(solution)/shard_map/ppermute | solution.py:37
  8.6 6.8 %collective-permute-start.3 = (bf16[4,192,128]{2,1,0:T(8,128)(2,1)S(1)}, bf16[4,192,128]{2,1,0:T(8,128)(2,1)S(1)}, u32[]{:S(2)}, u32[]{:S(2)}) collective-permute-start(bf16[4,192,128]{2,1,0:T(8,128)(2,1)S(1)} %pad_maximum_fusion.1), channel_id=1, source_target_pairs={{1,0},{2,1},{3,2},{4,3},{5,4},{6,5},{7,6},{0,7},{9,8},{10,9},{11,1... | collective-permute-start | bytes 589832 | tf_op jit(solution)/shard_map/ppermute | solution.py:38
  10.2 2.8 %collective-permute-start = (bf16[4,32,128]{2,1,0:T(8,128)(2,1)S(1)}, bf16[4,32,128]{2,1,0:T(8,128)(2,1)S(1)}, u32[]{:S(2)}, u32[]{:S(2)}) collective-permute-start(bf16[4,32,128]{2,1,0:T(8,128)(2,1)S(1)} %pad_maximum_fusion.2), channel_id=1, source_target_pairs={{0,8},{8,16},{16,24},{24,0},{1,9},{9,17},{17,25},{25,1},{2,10},{10... | collective-permute-start | bytes 98312 | tf_op jit(solution)/shard_map/ppermute | solution.py:35
  11.5 3.9 %collective-permute-start.1 = (bf16[4,32,128]{2,1,0:T(8,128)(2,1)S(1)}, bf16[4,32,128]{2,1,0:T(8,128)(2,1)S(1)}, u32[]{:S(2)}, u32[]{:S(2)}) collective-permute-start(bf16[4,32,128]{2,1,0:T(8,128)(2,1)S(1)} %pad_maximum_fusion.3), channel_id=1, source_target_pairs={{8,0},{16,8},{24,16},{0,24},{9,1},{17,9},{25,17},{1,25},{10,2},{18... | collective-permute-start | bytes 98312 | tf_op jit(solution)/shard_map/ppermute | solution.py:36
  60.6 107.1 %all-to-all-start = ((bf16[8,6,32,1024]{3,2,1,0:T(8,128)(2,1)}), bf16[8,6,32,1024]{3,2,1,0:T(8,128)(2,1)}, u32[]{:S(2)}, u32[]{:S(2)}) async-start(bf16[8,6,32,1024]{3,2,1,0:T(8,128)(2,1)} %bitcast.50), calls=%async_computation | async-start | bytes 6291456 | tf_op jit(solution)/shard_map/all_to_all | solution.py:544
  70.7 69.0 %collective-permute-start.6 = (bf16[3,192,128]{2,1,0:T(8,128)(2,1)S(1)}, bf16[3,192,128]{2,1,0:T(8,128)(2,1)S(1)}, u32[]{:S(2)}, u32[]{:S(2)}) collective-permute-start(bf16[3,192,128]{2,1,0:T(8,128)(2,1)S(1)} %fusion.1), channel_id=1, source_target_pairs={{0,1},{1,2},{2,3},{3,4},{4,5},{5,6},{6,7},{7,0},{8,9},{9,10},{10,1... | collective-permute-start | bytes 442376 | tf_op jit(solution)/shard_map/ppermute | solution.py:37
  72.2 69.2 %collective-permute-start.7 = (bf16[3,192,128]{2,1,0:T(8,128)(2,1)S(1)}, bf16[3,192,128]{2,1,0:T(8,128)(2,1)S(1)}, u32[]{:S(2)}, u32[]{:S(2)}) collective-permute-start(bf16[3,192,128]{2,1,0:T(8,128)(2,1)S(1)} %fusion), channel_id=1, source_target_pairs={{1,0},{2,1},{3,2},{4,3},{5,4},{6,5},{7,6},{0,7},{9,8},{10,9},{11,1... | collective-permute-start | bytes 442376 | tf_op jit(solution)/shard_map/ppermute | solution.py:38
  73.1 4.0 %collective-permute-start.5 = (bf16[3,32,128]{2,1,0:T(8,128)(2,1)S(1)}, bf16[3,32,128]{2,1,0:T(8,128)(2,1)S(1)}, u32[]{:S(2)}, u32[]{:S(2)}) collective-permute-start(bf16[3,32,128]{2,1,0:T(8,128)(2,1)S(1)} %get-tuple-element.17), channel_id=1, source_target_pairs={{8,0},{16,8},{24,16},{0,24},{9,1},{17,9},{25,17},{1,25},{10,2},{18... | collective-permute-start | bytes 73736 | tf_op jit(solution)/shard_map/ppermute | solution.py:36
  73.1 4.0 %collective-permute-start.4 = (bf16[3,32,128]{2,1,0:T(8,128)(2,1)S(1)}, bf16[3,32,128]{2,1,0:T(8,128)(2,1)S(1)}, u32[]{:S(2)}, u32[]{:S(2)}) collective-permute-start(bf16[3,32,128]{2,1,0:T(8,128)(2,1)S(1)} %get-tuple-element.18), channel_id=1, source_target_pairs={{0,8},{8,16},{16,24},{24,0},{1,9},{9,17},{17,25},{25,1},{2,10},{10... | collective-permute-start | bytes 73736 | tf_op jit(solution)/shard_map/ppermute | solution.py:35
where the time goes:
time: 172 us
  Pallas kernels  71.4 us (42%)
  waiting for transfers between devices  69.6 us (40%)
  starting transfers between devices  15.4 us (9%)
  local copies, waits for them, and re-layouts  12.8 us (7%)
  other arithmetic  1.74 us (1%)
    ppermute x2, waiting for transfers between devices, edges(): lax.ppermute(stack(None, -1), 'tile', y_fwd)  62.6 us
    pallas_call x1, Pallas kernels, ion_call(): pl.pallas_call(functools.partial(ion_kernel, capacity), name='ion', out_s...  45.2 us
    pallas_call x1, Pallas kernels, flow_call(): pl.pallas_call(flow_kernel, name='flow', out_shape=jax.ShapeDtypeStruct(u...  26.2 us
    all_to_all x1, starting transfers between devices, per_device(): lax.all_to_all(outgoing, 'tile', split_axis=0, concat_axis=0, tiled=True)  7.99 us
    slice x5, local copies, waits for them, and re-layouts, pick(): return array[..., y, :]  7.89 us
    unnamed x7, local copies, waits for them, and re-layouts  4.15 us
    ppermute x2, waiting for transfers between devices, edges(): lax.ppermute(stack(0, None), 'stream', x_bwd)  3.92 us
    ppermute x2, starting transfers between devices, edges(): lax.ppermute(stack(-1, None), 'stream', x_fwd)  3.62 us
  transfers between devices with their start and end apart: 9, of which 5 were waited for; matrix products, arithmetic and copies ran while one was open for 3% of the time, Pallas kernels for 15%

commit v1 on v0

v1 whole, which is shorter than its diff:
```python
import functools

import jax
import jax.numpy as jnp
from jax import lax
from jax.experimental import pallas as pl
from jax.experimental.pallas import tpu as pltpu
from jax.sharding import PartitionSpec as P


BLK = 32
TOP = 8
ROWS = 48

ion_step = 0.04
flow_step = 0.1
viscosity = 0.5
species_diff = (1.0, 1.5)

F32 = jnp.float32
BF16 = jnp.bfloat16

HBM = pl.BlockSpec(memory_space=pltpu.HBM)
PARAMS = pltpu.CompilerParams(vmem_limit_bytes=60 * 2**20)


def rings(axis):
    count = lax.axis_size(axis)
    forward = [(i, (i + 1) % count) for i in range(count)]
    backward = [(target, source) for source, target in forward]
    return forward, backward


def edge_kernel(*refs):
    c_hbm, p_hbm, d_hbm, s_hbm, u_hbm, xf, xl, yf, yl = refs[:9]
    c_x, p_x, d_x, s_x, u_x, c_y, p_y, d_y, s_y, u_y, tmp, tmp_s, x_sem, y_sem = refs[9:]
    nx, ny, nz = p_hbm.shape
    cuts = y_sem.shape[2]
    step = nx // cuts
    sources = (c_hbm, p_hbm, d_hbm, s_hbm, u_hbm)

    def planes(n):
        at = 0 if n == 0 else nx - 1
        copies = []
        for j, (src, dst) in enumerate(zip(sources, (c_x, p_x, d_x, s_x, u_x))):
            part = src.at[:, at] if len(src.shape) == 4 else src.at[at]
            copies.append(pltpu.make_async_copy(part, dst.at[n], x_sem.at[n, j]))
        return copies

    def rows(n, i):
        part = pl.ds(i * step, step)
        row = pl.ds(0 if n == 0 else ny - TOP, TOP)
        copies = []
        for j, (src, dst) in enumerate(zip(sources, (c_y, p_y, d_y, s_y, u_y))):
            if len(src.shape) == 4:
                pair = src.at[:, part, row], dst.at[n, :, part]
            else:
                pair = src.at[part, row], dst.at[n, part]
            copies.append(pltpu.make_async_copy(*pair, y_sem.at[n, j, i]))
        return copies

    for i in range(cuts):
        for n in range(2):
            for copy in rows(n, i):
                copy.start()
    for n in range(2):
        for copy in planes(n):
            copy.start()
    for n, out in enumerate((xf, xl)):
        for copy in planes(n):
            copy.wait()
        solid = s_x[n] > 0
        out[0] = c_x[n, 0]
        out[1] = c_x[n, 1]
        out[2] = p_x[n]
        out[3] = jnp.where(solid, d_x[n].astype(F32), 0.0).astype(BF16)
        for f in range(3):
            out[4 + f] = jnp.where(solid, u_x[n, f].astype(F32), 0.0).astype(BF16)
    size = 16
    for i in range(cuts):
        for n, out in enumerate((yf, yl)):
            for copy in rows(n, i):
                copy.wait()
            row = 0 if n == 0 else TOP - 1

            @pl.loop(0, step // size)
            def _(q, i=i, n=n, out=out, row=row):
                at = pl.ds(pl.multiple_of(i * step + q * size, size), size)
                picked = pl.ds(row, size, stride=TOP)
                tmp_s[...] = s_y[n, at].reshape(size * TOP, nz)
                solid = tmp_s[picked, :] > 0
                loaded = [c_y[n, 0, at], c_y[n, 1, at], p_y[n, at], d_y[n, at]]
                loaded += [u_y[n, f, at] for f in range(3)]
                for f, v in enumerate(loaded):
                    tmp[f] = v.astype(F32).reshape(size * TOP, nz)
                for f in range(7):
                    v = tmp[f, picked, :]
                    if f > 2:
                        v = jnp.where(solid, v, 0.0)
                    out[f, at, :] = v.astype(BF16)


def edges(c, p, d, s, u):
    nx, ny, nz = p.shape
    vm = pltpu.VMEM
    vmem = pl.BlockSpec(memory_space=vm)
    cuts = 4

    def pieces(shape):
        return [
            vm((2,) + (2,) * two + (3,) * three + shape, jnp.int32 if whole else BF16)
            for two, three, whole in ((1, 0, 0), (0, 0, 0), (0, 0, 0), (0, 0, 1), (0, 1, 0))
        ]

    x_first, x_last, y_first, y_last = pl.pallas_call(
        edge_kernel,
        name="edges",
        out_shape=(jax.ShapeDtypeStruct((7, ny, nz), BF16),) * 2
        + (jax.ShapeDtypeStruct((7, nx, nz), BF16),) * 2,
        in_specs=[HBM] * 5,
        out_specs=(vmem,) * 4,
        scratch_shapes=pieces((ny, nz))
        + pieces((nx, TOP, nz))
        + [
            vm((7, 16 * TOP, nz), F32),
            vm((16 * TOP, nz), jnp.int32),
            pltpu.SemaphoreType.DMA((2, 5)),
            pltpu.SemaphoreType.DMA((2, 5, cuts)),
        ],
        compiler_params=PARAMS,
        cost_estimate=pl.CostEstimate(
            flops=20 * nx * nz, bytes_accessed=200 * nx * nz, transcendentals=0
        ),
    )(c, p, d, s, u)
    x_fwd, x_bwd = rings("stream")
    y_fwd, y_bwd = rings("tile")
    low_x = lax.ppermute(x_last, "stream", x_fwd)
    high_x = lax.ppermute(x_first, "stream", x_bwd)
    low_y = lax.ppermute(y_last, "tile", y_fwd)
    high_y = lax.ppermute(y_first, "tile", y_bwd)
    return low_x, high_x, low_y, high_y


def roll_lanes(value, shift):
    return pltpu.roll(value, shift % value.shape[-1], axis=value.ndim - 1)


def face(low, high):
    f = low[3] * high[3]
    h = f * (high[2] - low[2])
    a = f + h
    b = f - h
    return a * high[0] - b * low[0], b * high[1] - a * low[1]


def onehot(rows, cols, test):
    r = lax.broadcasted_iota(jnp.int32, (rows, cols), 0)
    c = lax.broadcasted_iota(jnp.int32, (rows, cols), 1)
    return jnp.where(test(r, c), 1.0, 0.0)


def ion_kernel(capacity, inner, *refs):
    refs = list(refs)
    plan, me, c_hbm, p_hbm, d_hbm, s_hbm = refs[:6]
    refs = refs[6:]
    edges_hbm = []
    if not inner:
        edges_hbm, refs = refs[:4], refs[5:]
    cn_hbm, out_hbm, c_v, p_v, d_v, s_v = refs[:6]
    refs = refs[6:]
    if not inner:
        xl_v, xh_v, yl_v, yh_v, yl_f, yh_f = refs[:6]
        refs = refs[6:]
    fld, cn_v, chs, blk, zero, perm, lanes, shift, shift2, dpot = refs[:10]
    tally, in_sem, halo_sem, cn_sem, blk_sem, zero_sem = refs[10:]
    nx, _, nz = p_hbm.shape
    chunks = nx // BLK
    bz = nz // BLK
    slots = out_hbm.shape[0]
    tiles = slots // capacity
    count = chunks * bz
    m0, m1 = TOP, BLK - TOP
    first = m0 - 1 if inner else 0
    depth = m1 + 1 - first if inner else BLK

    def loads(i):
        part = pl.ds(i * BLK + first, depth)
        return (
            pltpu.make_async_copy(c_hbm.at[:, part], c_v.at[:, part], in_sem.at[0, i]),
            pltpu.make_async_copy(p_hbm.at[part], p_v.at[part], in_sem.at[1, i]),
            pltpu.make_async_copy(d_hbm.at[part], d_v.at[part], in_sem.at[2, i]),
            pltpu.make_async_copy(s_hbm.at[part], s_v.at[part], in_sem.at[3, i]),
        )

    halos = []
    if not inner:
        for n, (src, dst) in enumerate(zip(edges_hbm, (xl_v, xh_v, yl_v, yh_v))):
            halos.append(pltpu.make_async_copy(src.at[pl.ds(0, 4)], dst, halo_sem.at[n]))
    for copy in halos:
        copy.start()
    for i in range(chunks):
        for copy in loads(i):
            copy.start()

    zero[...] = jnp.zeros_like(zero)
    width = BLK * TOP
    if not inner:
        perm[1] = onehot(
            width, width, lambda r, c: (r // BLK == c % TOP) & (r % BLK == c // TOP)
        ).astype(BF16)
    half = BLK // 2
    perm[0] = onehot(
        width,
        width,
        lambda r, c: (r // half == (c // (half * TOP)) * TOP + c % TOP)
        & (r % half == (c // TOP) % half),
    ).astype(BF16)
    wide = bz * nz
    lanes[...] = onehot(
        wide,
        wide,
        lambda r, c: (r // nz == (c % nz) // BLK) & (r % nz == (c // nz) * BLK + c % BLK),
    ).astype(BF16)
    near = onehot(
        nz, 2 * nz, lambda r, c: ((c < nz) & (r == c - 1)) | ((c >= nz) & (r == c - nz + 1))
    )
    own = onehot(nz, 2 * nz, lambda r, c: r == c % nz)
    shift[...] = near.astype(BF16)
    shift2[0:nz, :] = near.astype(BF16)
    shift2[nz : 2 * nz, :] = near.astype(BF16)
    dpot[...] = (near - own).astype(BF16)

    @pl.loop(0, tiles)
    def _(o):
        tally[count + o] = 0

    def place(o):
        return o if inner else lax.rem(o + tiles - me[0], tiles)

    @pl.loop(0, count)
    def _(b):
        o = place(plan[b])
        rank = tally[count + o]
        tally[b] = o * capacity + rank
        tally[count + o] = rank + 1

    def blank(slot):
        return pltpu.make_async_copy(zero, out_hbm.at[slot], zero_sem.at[slot])

    @pl.loop(0, tiles)
    def _(o):
        @pl.loop(tally[count + o], capacity)
        def _(k):
            blank(o * capacity + k).start()

    body = pl.ds(TOP, BLK)

    def scaled(f, v):
        v = v.astype(F32)
        if f == 2:
            return v * 0.5
        return v * lax.rsqrt(jnp.maximum(v, 0.25)) if f == 3 else v

    if not inner:
        for copy in halos:
            copy.wait()
        for plane, ref in ((0, xl_v), (nx + 1, xh_v)):
            for f in range(4):
                fld[f, plane, body, :] = scaled(f, ref[f])
        for ref, dst in ((yl_v, yl_f), (yh_v, yh_f)):
            for f in range(4):
                dst[f] = scaled(f, ref[f])

    def convert(x, number):
        at = pl.ds(x, number)
        to = pl.ds(x + 1, number)
        fld[0, to, body, :] = c_v[0, at].astype(F32)
        fld[1, to, body, :] = c_v[1, at].astype(F32)
        fld[2, to, body, :] = p_v[at].astype(F32) * 0.5
        d = d_v[at].astype(F32)
        fld[3, to, body, :] = jnp.where(s_v[at] > 0, d * lax.rsqrt(d), 0.0)

    def prepare(i):
        for copy in loads(i):
            copy.wait()
        if inner:
            convert(i * BLK + first, 1)
            convert(i * BLK + m1, 1)

            @pl.loop(m0 // 4, m1 // 4)
            def _(q):
                convert(i * BLK + q * 4, 4)

            return

        @pl.loop(0, BLK // 4)
        def _(q):
            x = i * BLK + q * 4
            convert(x, 4)
            for j in range(4):
                for f in range(4):
                    fld[f, x + 1 + j, pl.ds(TOP - 1, 1), :] = yl_f[f, pl.ds(x + j, 1), :]
                    fld[f, x + 1 + j, pl.ds(TOP + BLK, 1), :] = yh_f[f, pl.ds(x + j, 1), :]

    batch = TOP

    def planes(x, number, row, tall):
        return [fld[f, pl.ds(x + 1, number), pl.ds(TOP + row, tall), :] for f in range(4)]

    def update(x, row, tall):
        mid = planes(x, batch, row, tall)
        c0, c1, pot, s = mid
        m = batch * tall

        def flat(v):
            return v.reshape(m, nz)

        high = s.astype(BF16)
        low = (s - high.astype(F32)).astype(BF16)
        both = jnp.concatenate([flat(c0), flat(c1)], axis=0).astype(BF16)
        zc = jnp.dot(both, shift[...], preferred_element_type=F32)
        zs = jnp.dot(
            jnp.concatenate([flat(high), flat(low)], axis=1),
            shift2[...],
            preferred_element_type=F32,
        )
        zp = jnp.dot(flat(pot).astype(BF16), dpot[...], preferred_element_type=F32)
        lows = planes(x - 1, batch + 1, row, tall)
        highs = planes(x, batch + 1, row, tall)
        fx = face(lows, highs)
        total = [fx[sp][1:] - fx[sp][:batch] for sp in range(2)]
        sides = []
        for off in (-1, 1):
            n0, n1, npot, ns = planes(x, batch, row + off, tall)
            sides.append((n0, n1, npot - pot, ns))
        for part in (slice(0, nz), slice(nz, 2 * nz)):
            parts = (zc[:m, part], zc[m:, part], zp[:, part], zs[:, part])
            sides.append(tuple(v.reshape(batch, tall, nz) for v in parts))
        sum_a = sum_b = None
        for n0, n1, dp, ns in sides:
            f = s * ns
            h = f * dp
            a = f + h
            b = f - h
            total[0] = total[0] + n0 * a
            total[1] = total[1] + n1 * b
            sum_a = a if sum_a is None else sum_a + a
            sum_b = b if sum_b is None else sum_b + b
        total[0] = total[0] - c0 * sum_b
        total[1] = total[1] - c1 * sum_a
        new = []
        for sp in range(2):
            value = mid[sp] + (ion_step * species_diff[sp]) * total[sp]
            new.append(value.astype(BF16))
            cn_v[sp, pl.ds(x, batch), pl.ds(row, tall), :] = new[sp]
        return (new[0].astype(F32) - new[1].astype(F32)).astype(BF16)

    def keep(group, offset, charge):
        m = charge.shape[0] * charge.shape[1]
        at = pl.multiple_of(offset, m) if not isinstance(offset, int) else offset
        chs[group, pl.ds(at, m), :] = charge.reshape(m, nz)

    def saves(i):
        x = i * BLK
        spots = [(m0, m1 - m0, m0, m1 - m0)]
        if not inner:
            spots = [(0, BLK, 0, TOP), (0, BLK, m1, TOP), (0, m0, m0, m1 - m0)]
            spots.append((m1, TOP, m0, m1 - m0))
        copies = []
        for n, (px, number, row, tall) in enumerate(spots):
            at = (slice(None), pl.ds(x + px, number), pl.ds(row, tall))
            copies.append(pltpu.make_async_copy(cn_v.at[at], cn_hbm.at[at], cn_sem.at[n, i]))
        return copies

    def put(b):
        return pltpu.make_async_copy(blk.at[b], out_hbm.at[tally[b]], blk_sem.at[b])

    def joined(t, size):
        groups = t.shape[0] // (size * bz)
        return [
            jnp.concatenate(
                [t[(j * bz + m) * size : (j * bz + m + 1) * size] for m in range(bz)], axis=1
            )
            for j in range(groups)
        ]

    prepare(0)

    @pl.loop(0, chunks)
    def _(i):
        @pl.when(i + 1 < chunks)
        def _():
            prepare(i + 1)

        x = i * BLK
        middle = half * TOP
        if inner:

            @pl.loop(0, (m1 - m0) // batch)
            def _(q):
                charge = update(x + m0 + q * batch, m0, m1 - m0)
                for t in range(2):
                    keep(0, t * middle + q * batch * TOP, charge[:, t * TOP : (t + 1) * TOP])

        else:

            @pl.loop(0, BLK // batch)
            def _(q):
                for t, row in enumerate((0, m1)):
                    keep(1 + t, q * batch * TOP, update(x + q * batch, row, TOP))

            for q, px in enumerate((0, m1)):
                charge = update(x + px, m0, m1 - m0)
                for t in range(2):
                    keep(0, t * middle + q * batch * TOP, charge[:, t * TOP : (t + 1) * TOP])

        for copy in saves(i):
            copy.start()
        rowsets = []
        if not inner:
            for t in range(2):
                v = jnp.dot(perm[1], chs[1 + t], preferred_element_type=F32).astype(BF16)
                rowsets += joined(v, BLK)
        v = jnp.dot(perm[0], chs[0], preferred_element_type=F32).astype(BF16)
        rowsets += joined(v, half)
        res = jnp.dot(
            jnp.concatenate(rowsets, axis=0), lanes[...], preferred_element_type=F32
        ).astype(BF16)
        groups = TOP // bz
        for k in range(bz):
            row = 0
            if not inner:
                for j in range(2 * groups):
                    blk[i * bz + k, 0:BLK, j * nz : (j + 1) * nz] = res[
                        row : row + BLK, k * nz : (k + 1) * nz
                    ]
                    row += BLK
            base = 0 if inner else BLK
            for j in range(2 * groups):
                blk[i * bz + k, base : base + half, j * nz : (j + 1) * nz] = res[
                    row : row + half, k * nz : (k + 1) * nz
                ]
                row += half
            put(i * bz + k).start()

    @pl.loop(0, chunks)
    def _(i):
        for copy in saves(i):
            copy.wait()

    @pl.loop(0, count)
    def _(b):
        put(b).wait()

    @pl.loop(0, tiles)
    def _(o):
        @pl.loop(tally[count + o], capacity)
        def _(k):
            blank(o * capacity + k).wait()


def ion_call(plan, me, c, p, d, s, halo, before, capacity, tiles):
    _, nx, ny, nz = c.shape
    count = plan.shape[0]
    chunks = nx // BLK
    bz = nz // BLK
    inner = before is None
    args = [plan, me, c, p, d, s] + ([] if inner else list(halo) + [before])
    deep = BLK // 2 if inner else BLK + BLK // 2
    wide = BLK * BLK // 2
    vm = pltpu.VMEM
    dma = pltpu.SemaphoreType.DMA
    ends = [
        vm((4, ny, nz), BF16),
        vm((4, ny, nz), BF16),
        vm((4, nx, nz), BF16),
        vm((4, nx, nz), BF16),
        vm((4, nx, nz), F32),
        vm((4, nx, nz), F32),
    ]
    share = 0.25 if inner else 0.75
    return pl.pallas_call(
        functools.partial(ion_kernel, capacity, inner),
        name="ion_inner" if inner else "ion_outer",
        out_shape=(
            jax.ShapeDtypeStruct(c.shape, BF16),
            jax.ShapeDtypeStruct((tiles * capacity, deep, wide), BF16),
        ),
        in_specs=[pl.BlockSpec(memory_space=pltpu.SMEM)] * 2 + [HBM] * (len(args) - 2),
        out_specs=(HBM, HBM),
        scratch_shapes=[
            vm(c.shape, BF16),
            vm(p.shape, BF16),
            vm(p.shape, BF16),
            vm(p.shape, jnp.int32),
        ]
        + ([] if inner else ends)
        + [
            vm((4, nx + 2, ROWS, nz), F32),
            vm(c.shape, BF16),
            vm((1 if inner else 3, BLK * TOP, nz), BF16),
            vm((count, deep, wide), BF16),
            vm((deep, wide), BF16),
            vm((2, BLK * TOP, BLK * TOP), BF16),
            vm((bz * nz, bz * nz), BF16),
            vm((nz, 2 * nz), BF16),
            vm((2 * nz, 2 * nz), BF16),
            vm((nz, 2 * nz), BF16),
            pltpu.SMEM((count + tiles,), jnp.int32),
            dma((4, chunks)),
            dma((4,)),
            dma((4, chunks)),
            dma((count,)),
            dma((tiles * capacity,)),
        ],
        input_output_aliases={} if inner else {len(args) - 1: 0},
        compiler_params=PARAMS,
        cost_estimate=pl.CostEstimate(
            flops=int(100 * p.size * share),
            bytes_accessed=int(60 * p.size * share),
            transcendentals=int(p.size * share),
        ),
    )(*args)


def gather_kernel(boxes, capacity, shifts, aliased, *refs):
    me, parts, refs = refs[0], refs[1 : 1 + len(shifts)], refs[1 + len(shifts) + aliased :]
    out_hbm, sem = refs
    tiles = out_hbm.shape[0] // capacity

    def moves(n):
        base = lax.rem(me[0] + (tiles - shifts[n]), tiles) * capacity
        at = pl.ds(base, parts[n].shape[0])
        copies = []
        for m, ((r0, l0), (x0, y0), rows, width) in enumerate(boxes):
            copies.append(
                pltpu.make_async_copy(
                    parts[n].at[:, pl.ds(r0, rows), pl.ds(l0, width)],
                    out_hbm.at[at, pl.ds(x0, rows), pl.ds(y0, width)],
                    sem.at[n, m],
                )
            )
        return copies

    for n in range(len(shifts)):
        for copy in moves(n):
            copy.start()
    for n in range(len(shifts)):
        for copy in moves(n):
            copy.wait()


def gather_call(me, parts, shifts, inner, before, slots, capacity):
    q, h = BLK * BLK // 4, BLK // 2
    t = TOP
    if inner:
        boxes = (((0, 0), (t, q), h, 2 * q),)
    else:
        boxes = (
            ((0, 0), (0, 0), BLK, q),
            ((0, q), (0, 3 * q), BLK, q),
            ((BLK, 0), (0, q), t, 2 * q),
            ((BLK + t, 0), (BLK - t, q), t, 2 * q),
        )
    vmem = pl.BlockSpec(memory_space=pltpu.VMEM)
    args = [me] + list(parts) + ([] if before is None else [before])
    return pl.pallas_call(
        functools.partial(gather_kernel, boxes, capacity, shifts, before is not None),
        name="gather_inner" if inner else "gather_outer",
        out_shape=jax.ShapeDtypeStruct((slots, BLK, BLK * BLK), BF16),
        in_specs=[pl.BlockSpec(memory_space=pltpu.SMEM)]
        + [vmem] * len(parts)
        + [HBM] * (before is not None),
        out_specs=HBM,
        scratch_shapes=[pltpu.SemaphoreType.DMA((len(parts), len(boxes)))],
        input_output_aliases={} if before is None else {len(args) - 1: 0},
        compiler_params=pltpu.CompilerParams(vmem_limit_bytes=8 * 2**20),
        cost_estimate=pl.CostEstimate(
            flops=0, bytes_accessed=4 * sum(v.size for v in parts), transcendentals=0
        ),
    )(*args)


def flow_kernel(
    u_hbm,
    p_hbm,
    s_hbm,
    cn_hbm,
    xl_hbm,
    xh_hbm,
    yl_hbm,
    yh_hbm,
    un_hbm,
    u_v,
    p_v,
    s_v,
    cn_v,
    uxl_v,
    uxh_v,
    uyl_v,
    uyh_v,
    pxl_v,
    pxh_v,
    pyl_v,
    pyh_v,
    yl_f,
    yh_f,
    fld,
    un_v,
    in_sem,
    halo_sem,
    un_sem,
):
    nx, nz = p_hbm.shape[0], p_hbm.shape[2]
    chunks = nx // BLK

    def loads(i):
        part = pl.ds(i * BLK, BLK)
        return (
            pltpu.make_async_copy(u_hbm.at[:, part], u_v.at[:, part], in_sem.at[0, i]),
            pltpu.make_async_copy(p_hbm.at[part], p_v.at[part], in_sem.at[1, i]),
            pltpu.make_async_copy(s_hbm.at[part], s_v.at[part], in_sem.at[2, i]),
            pltpu.make_async_copy(cn_hbm.at[:, part], cn_v.at[:, part], in_sem.at[3, i]),
        )

    pairs = (
        (xl_hbm, uxl_v),
        (xh_hbm, uxh_v),
        (yl_hbm, uyl_v),
        (yh_hbm, uyh_v),
        (xl_hbm, pxl_v),
        (xh_hbm, pxh_v),
        (yl_hbm, pyl_v),
        (yh_hbm, pyh_v),
    )
    halos = [
        pltpu.make_async_copy(src.at[2] if n > 3 else src.at[pl.ds(4, 3)], dst, halo_sem.at[n])
        for n, (src, dst) in enumerate(pairs)
    ]
    for copy in halos:
        copy.start()
    for i in range(chunks):
        for copy in loads(i):
            copy.start()
    for copy in halos:
        copy.wait()
    body = pl.ds(TOP, BLK)
    for plane, ref, pref in ((0, uxl_v, pxl_v), (nx + 1, uxh_v, pxh_v)):
        for f in range(3):
            fld[f, plane, body, :] = ref[f].astype(F32)
        fld[3, plane, body, :] = pref[...].astype(F32)
    for ref, pref, dst in ((uyl_v, pyl_v, yl_f), (uyh_v, pyh_v, yh_f)):
        for f in range(3):
            dst[f] = ref[f].astype(F32)
        dst[3] = pref[...].astype(F32)

    def prepare(i):
        for copy in loads(i):
            copy.wait()

        @pl.loop(0, BLK)
        def _(q):
            x = i * BLK + q
            fluid = s_v[x] > 0
            for f in range(3):
                fld[f, x + 1, body, :] = jnp.where(fluid, u_v[f, x].astype(F32), 0.0)
            fld[3, x + 1, body, :] = p_v[x].astype(F32)
            for f in range(4):
                fld[f, x + 1, pl.ds(TOP - 1, 1), :] = yl_f[f, pl.ds(x, 1), :]
                fld[f, x + 1, pl.ds(TOP + BLK, 1), :] = yh_f[f, pl.ds(x, 1), :]

    half = 16
    lane = lax.broadcasted_iota(jnp.int32, (half, nz), 1)
    first_lane = lane == 0
    last_lane = lane == nz - 1
    k_mid = flow_step * viscosity
    k_adv = flow_step * 0.5

    def below(v):
        return jnp.where(first_lane, 0.0, roll_lanes(v, 1))

    def above(v):
        return jnp.where(last_lane, 0.0, roll_lanes(v, -1))

    def update(i):
        @pl.loop(0, BLK)
        def _(q):
            x = i * BLK + q
            for y0 in range(0, BLK, half):
                at = pl.ds(TOP + y0, half)
                mid = [fld[f, x + 1, at, :] for f in range(3)]
                field = fld[3, x + 1, at, :]
                fluid = s_v[x, pl.ds(y0, half), :] > 0
                cn0 = cn_v[0, x, pl.ds(y0, half), :].astype(F32)
                cn1 = cn_v[1, x, pl.ds(y0, half), :].astype(F32)
                push = (cn0 - cn1) * k_adv
                plus = [k_mid - k_adv * u for u in mid]
                minus = [k_mid + k_adv * u for u in mid]
                for a in range(3):
                    total = mid[a] * (1.0 - 6.0 * k_mid)
                    total = total + fld[a, x + 2, at, :] * plus[0] + fld[a, x, at, :] * minus[0]
                    total = total + fld[a, x + 1, pl.ds(TOP + 1 + y0, half), :] * plus[1]
                    total = total + fld[a, x + 1, pl.ds(TOP - 1 + y0, half), :] * minus[1]
                    total = total + above(mid[a]) * plus[2] + below(mid[a]) * minus[2]
                    if a == 0:
                        rise = fld[3, x + 2, at, :] - fld[3, x, at, :]
                    elif a == 1:
                        rise = (
                            fld[3, x + 1, pl.ds(TOP + 1 + y0, half), :]
                            - fld[3, x + 1, pl.ds(TOP - 1 + y0, half), :]
                        )
                    else:
                        rise = above(field) - below(field)
                    total = jnp.where(fluid, total - push * rise, 0.0)
                    un_v[a, x, pl.ds(y0, half), :] = total.astype(BF16)

    def saves(i):
        part = pl.ds(i * BLK, BLK)
        return pltpu.make_async_copy(un_v.at[:, part], un_hbm.at[:, part], un_sem.at[i])

    prepare(0)

    @pl.loop(0, chunks)
    def _(i):
        @pl.when(i + 1 < chunks)
        def _():
            prepare(i + 1)

        update(i)
        saves(i).start()

    @pl.loop(0, chunks)
    def _(i):
        saves(i).wait()


def flow_call(u, p, s, cn, halo):
    _, nx, ny, nz = u.shape
    chunks = nx // BLK
    vm = pltpu.VMEM
    dma = pltpu.SemaphoreType.DMA
    return pl.pallas_call(
        flow_kernel,
        name="flow",
        out_shape=jax.ShapeDtypeStruct(u.shape, BF16),
        in_specs=[HBM] * 8,
        out_specs=HBM,
        scratch_shapes=[
            vm(u.shape, BF16),
            vm(p.shape, BF16),
            vm(s.shape, jnp.int32),
            vm(cn.shape, BF16),
            vm((3, ny, nz), BF16),
            vm((3, ny, nz), BF16),
            vm((3, nx, nz), BF16),
            vm((3, nx, nz), BF16),
            vm((ny, nz), BF16),
            vm((ny, nz), BF16),
            vm((nx, nz), BF16),
            vm((nx, nz), BF16),
            vm((4, nx, nz), F32),
            vm((4, nx, nz), F32),
            vm((4, nx + 2, ROWS, nz), F32),
            vm(u.shape, BF16),
            dma((4, chunks)),
            dma((8,)),
            dma((chunks,)),
        ],
        compiler_params=PARAMS,
        cost_estimate=pl.CostEstimate(
            flops=80 * p.size, bytes_accessed=20 * p.size, transcendentals=0
        ),
    )(u, p, s, cn, *halo)


def per_device(concentration, potential, diffusivity, spacer, velocity, balance_plan):
    tiles = lax.axis_size("tile")
    count = balance_plan.shape[0]
    capacity = max(2, (2 * count + tiles - 1) // tiles)
    slots = tiles * capacity

    me = lax.axis_index("tile").astype(jnp.int32)[None]

    def exchange(part):
        part = part.reshape((tiles, capacity) + part.shape[1:])
        part = lax.all_to_all(part, "tile", split_axis=0, concat_axis=0, tiled=True)
        return part.reshape((slots,) + part.shape[2:])

    def pass_on(part, shift):
        piece = part[shift * capacity : (shift + 1) * capacity]
        if shift == 0:
            return piece
        return lax.ppermute(piece, "tile", [(i, (i + shift) % tiles) for i in range(tiles)])

    halo = edges(concentration, potential, diffusivity, spacer, velocity)
    given = (balance_plan[:, 0], me, concentration, potential, diffusivity, spacer)
    conc, first = ion_call(*given, None, None, capacity, tiles)
    first = exchange(first)
    conc_next, second = ion_call(*given, halo, conc, capacity, tiles)
    order = sorted(range(1, tiles), key=lambda d: -min(d, tiles - d)) + [0]
    pieces = [pass_on(second, d) for d in order]
    flow_next = flow_call(velocity, potential, spacer, conc_next, halo)
    owned = gather_call(jnp.zeros_like(me), [first], (0,), True, None, slots, capacity)
    owned = gather_call(me, pieces, tuple(order), False, owned, slots, capacity)
    return conc_next, flow_next, owned


def solution(mesh):
    placed = (
        P(None, "stream", "tile", None),
        P("stream", "tile", None),
        P("stream", "tile", None),
        P("stream", "tile", None),
        P(None, "stream", "tile", None),
        P(("stream", "tile"), None),
    )
    return jax.shard_map(
        per_device,
        mesh=mesh,
        in_specs=placed,
        out_specs=(
            P(None, "stream", "tile", None),
            P(None, "stream", "tile", None),
            P(("stream", "tile"), None, None),
        ),
        check_vma=False,
    )
```

time: 172 us -> 123 us (0.72)
  the two profiles are of different devices: /device:TPU:11 before, /device:TPU:1 now
where the time goes in v1:
time: 123 us
  Pallas kernels  67.3 us (55%)
  starting transfers between devices  32.1 us (26%)
  waiting for transfers between devices  19.2 us (16%)
  local copies, waits for them, and re-layouts  3.61 us (3%)
    pallas_call x2, Pallas kernels, ion_call(): pl.pallas_call(functools.partial(ion_kernel, capacity, inner), name='ion_...  30.4 us
    pallas_call x1, Pallas kernels, flow_call(): pl.pallas_call(flow_kernel, name='flow', out_shape=jax.ShapeDtypeStruct(u...  28.5 us
    ppermute x7, starting transfers between devices, pass_on(): lax.ppermute(piece, 'tile', [(i, (i + shift) % tiles) for i in range(tile...  21.7 us
    ppermute x7, waiting for transfers between devices, pass_on(): lax.ppermute(piece, 'tile', [(i, (i + shift) % tiles) for i in range(tile...  8.38 us
    ppermute x1, waiting for transfers between devices, edges(): low_y = lax.ppermute(y_last, 'tile', y_fwd)  8.09 us
    all_to_all x1, starting transfers between devices, exchange(): part = lax.all_to_all(part, 'tile', split_axis=0, concat_axis=0, tiled=True)  6.38 us
    pallas_call x1, Pallas kernels, edges(): pl.pallas_call(edge_kernel, name='edges', out_shape=(jax.ShapeDtypeStruct...  5.82 us
    slice x1, local copies, waits for them, and re-layouts, pass_on(): piece = part[shift * capacity:(shift + 1) * capacity]  2.72 us
  transfers between devices with their start and end apart: 12, of which 5 were waited for; matrix products, arithmetic and copies ran while one was open for 2% of the time, Pallas kernels for 45%

profile of v1, /device:TPU:1, one launch (start us, length us, event | category | flops | bytes accessed | tf_op | source)
XLA Modules:
  0.0 122.9 jit_solution(7660098397270967651)
XLA Ops:
  0.6 10.1 %ion_inner.1 = (bf16[2,192,32,128]{3,2,1,0:T(8,128)(2,1)}, bf16[48,16,512]{2,1,0:T(8,128)(2,1)}) custom-call(s32[24]{0:T(128)} %bitcast.6, s32[1]{0:T(128)} %bitcast.1.refs_1_.refs_0_, bf16[2,192,32,128]{3,2,1,0:T(8,128)(2,1)} %refs_2_.5, bf16[192,32,128]{2,1,0:T(8,128)(2,1)} %p_hbm.1, bf16[192,32,128]{2,1,0:T(8,128)(2,1)} %refs_4_.5, s32[192,32,128]{2,1,0:T(8,128)} %s_hbm.1), custom_call_target="tpu_custom_call" | custom-call | flops 19660800 | bytes 11796480 | tf_op jit(solution)/shard_map/ion_inner/pallas_call | solution.py:482
  10.7 6.4 %all-to-all-start = ((bf16[8,6,16,512]{3,2,1,0:T(8,128)(2,1)}), bf16[8,6,16,512]{3,2,1,0:T(8,128)(2,1)S(1)}, u32[]{:S(2)}, u32[]{:S(2)}) async-start(bf16[8,6,16,512]{3,2,1,0:T(8,128)(2,1)} %bitcast.5), calls=%async_computation | async-start | bytes 1572864 | tf_op jit(solution)/shard_map/all_to_all | solution.py:786
  17.1 5.8 %edges.1 = (bf16[7,32,128]{2,1,0:T(8,128)(2,1)}, bf16[7,32,128]{2,1,0:T(8,128)(2,1)}, bf16[7,192,128]{2,1,0:T(8,128)(2,1)}, bf16[7,192,128]{2,1,0:T(8,128)(2,1)}) custom-call(bf16[2,192,32,128]{3,2,1,0:T(8,128)(2,1)} %refs_2_.5, bf16[192,32,128]{2,1,0:T(8,128)(2,1)} %p_hbm.1, bf16[192,32,128]{2,1,0:T(8,128)(2,1)} %refs_4_.5, s32[192,32,128]{2,1,0:T(8,128)} %s_hbm.1, ...), custom_call_target="tpu_custom_call" | custom-call | flops 491520 | bytes 4915200 | tf_op jit(solution)/shard_map/edges/pallas_call | solution.py:115
  22.9 1.7 %collective-permute-start.2 = (bf16[7,192,128]{2,1,0:T(8,128)(2,1)}, bf16[7,192,128]{2,1,0:T(8,128)(2,1)S(1)}, u32[]{:S(2)}, u32[]{:S(2)}) collective-permute-start(bf16[7,192,128]{2,1,0:T(8,128)(2,1)} %get-tuple-element.13), channel_id=1, source_target_pairs={{0,1},{1,2},{2,3},{3,4},{4,5},{5,6},{6,7},{7,0},{8,9},{9,10},{10,1... | collective-permute-start | bytes 1032200 | tf_op jit(solution)/shard_map/ppermute | solution.py:139
  24.6 0.0 collective-permute-start.3
  24.6 1.2 collective-permute-start
  25.8 1.2 collective-permute-start.1
  27.0 2.1 %collective-permute-done.refs_6_.xl_hbm = bf16[7,32,128]{2,1,0:T(8,128)(2,1)S(1)} collective-permute-done((bf16[7,32,128]{2,1,0:T(8,128)(2,1)}, bf16[7,32,128]{2,1,0:T(8,128)(2,1)S(1)}, u32[]{:S(2)}, u32[]{:S(2)}) %collective-permute-start) | collective-permute-done | bytes 57376 | tf_op jit(solution)/shard_map/ppermute | solution.py:137
  29.0 0.0 copy-start.2
  29.0 0.6 collective-permute-done.1.refs_7_.xh_hbm
  29.7 0.0 copy-start.3
  29.7 8.1 %collective-permute-done.2.refs_8_.yl_hbm = bf16[7,192,128]{2,1,0:T(8,128)(2,1)S(1)} collective-permute-done((bf16[7,192,128]{2,1,0:T(8,128)(2,1)}, bf16[7,192,128]{2,1,0:T(8,128)(2,1)S(1)}, u32[]{:S(2)}, u32[]{:S(2)}) %collective-permute-start.2) | collective-permute-done | bytes 344096 | tf_op jit(solution)/shard_map/ppermute | solution.py:139
  37.8 0.0 copy-start
  37.8 0.0 collective-permute-done.3.refs_9_.yh_hbm
  37.8 0.0 copy-start.1
  37.8 0.0 copy-done.2
  37.8 0.0 copy-done.3
  37.8 0.7 copy-done
  38.5 0.2 copy-done.1
  38.7 20.3 %ion_outer.1 = (bf16[2,192,32,128]{3,2,1,0:T(8,128)(2,1)}, bf16[48,48,512]{2,1,0:T(8,128)(2,1)}) custom-call(s32[24]{0:T(128)} %bitcast.7, s32[1]{0:T(128)} %bitcast.1.refs_1_.refs_0_, bf16[2,192,32,128]{3,2,1,0:T(8,128)(2,1)} %refs_2_.5, bf16[192,32,128]{2,1,0:T(8,128)(2,1)} %p_hbm.1, ...), custom_call_target="tpu_custom_call", output_to_operand_aliasing={{0}: (10, {})} | custom-call | flops 58982400 | bytes 35389440 | tf_op jit(solution)/shard_map/ion_outer/pallas_call | solution.py:482
  59.0 2.7 %fusion = (bf16[6,48,512]{2,1,0:T(8,128)(2,1)S(1)}, bf16[6,48,512]{2,1,0:T(8,128)(2,1)S(1)}, bf16[6,48,512]{2,1,0:T(8,128)(2,1)S(1)}, bf16[6,48,512]{2,1,0:T(8,1...) fusion(bf16[48,48,512]{2,1,0:T(8,128)(2,1)} %get-tuple-element.17), kind=kLoop, calls=%fused_computation | loop fusion | bytes 4718592 | tf_op jit(solution)/shard_map/slice | solution.py:790
  61.7 3.8 %collective-permute-start.10 = (bf16[6,48,512]{2,1,0:T(8,128)(2,1)S(1)}, bf16[6,48,512]{2,1,0:T(8,128)(2,1)S(1)}, u32[]{:S(2)}, u32[]{:S(2)}) collective-permute-start(bf16[6,48,512]{2,1,0:T(8,128)(2,1)S(1)} %get-tuple-element.20), channel_id=1, source_target_pairs={{0,7},{1,0},{2,1},{3,2},{4,3},{5,4},{6,5},{7,6},{8,15},{9,8},{10,9... | collective-permute-start | bytes 884744 | tf_op jit(solution)/shard_map/ppermute | solution.py:793
  65.6 0.0 collective-permute-start.9
  65.6 3.3 %collective-permute-start.8 = (bf16[6,48,512]{2,1,0:T(8,128)(2,1)}, bf16[6,48,512]{2,1,0:T(8,128)(2,1)S(1)}, u32[]{:S(2)}, u32[]{:S(2)}) collective-permute-start(bf16[6,48,512]{2,1,0:T(8,128)(2,1)} %get-tuple-element.22), channel_id=1, source_target_pairs={{0,6},{1,7},{2,0},{3,1},{4,2},{5,3},{6,4},{7,5},{8,14},{9,15},{10,... | collective-permute-start | bytes 884744 | tf_op jit(solution)/shard_map/ppermute | solution.py:793
  68.9 1.6 %collective-permute-start.7 = (bf16[6,48,512]{2,1,0:T(8,128)(2,1)}, bf16[6,48,512]{2,1,0:T(8,128)(2,1)S(1)}, u32[]{:S(2)}, u32[]{:S(2)}) collective-permute-start(bf16[6,48,512]{2,1,0:T(8,128)(2,1)} %get-tuple-element.23), channel_id=1, source_target_pairs={{0,2},{1,3},{2,4},{3,5},{4,6},{5,7},{6,0},{7,1},{8,10},{9,11},{10,... | collective-permute-start | bytes 884744 | tf_op jit(solution)/shard_map/ppermute | solution.py:793
  70.6 1.2 collective-permute-start.6
  71.7 0.0 collective-permute-done.10.refs_7_
  71.7 7.6 %collective-permute-start.5 = (bf16[6,48,512]{2,1,0:T(8,128)(2,1)}, bf16[6,48,512]{2,1,0:T(8,128)(2,1)S(1)}, u32[]{:S(2)}, u32[]{:S(2)}) collective-permute-start(bf16[6,48,512]{2,1,0:T(8,128)(2,1)} %get-tuple-element.25), channel_id=1, source_target_pairs={{0,3},{1,4},{2,5},{3,6},{4,7},{5,0},{6,1},{7,2},{8,11},{9,12},{10,... | collective-permute-start | bytes 884744 | tf_op jit(solution)/shard_map/ppermute | solution.py:793
  79.3 0.0 collective-permute-done.9.refs_6_
  79.3 4.1 %collective-permute-start.4 = (bf16[6,48,512]{2,1,0:T(8,128)(2,1)S(1)}, bf16[6,48,512]{2,1,0:T(8,128)(2,1)S(1)}, u32[]{:S(2)}, u32[]{:S(2)}) collective-permute-start(bf16[6,48,512]{2,1,0:T(8,128)(2,1)S(1)} %get-tuple-element.26), channel_id=1, source_target_pairs={{0,4},{1,5},{2,6},{3,7},{4,0},{5,1},{6,2},{7,3},{8,12},{9,13},{10,... | collective-permute-start | bytes 884744 | tf_op jit(solution)/shard_map/ppermute | solution.py:793
  83.4 28.5 %flow.1 = bf16[3,192,32,128]{3,2,1,0:T(8,128)(2,1)} custom-call(bf16[3,192,32,128]{3,2,1,0:T(8,128)(2,1)} %u_hbm.1, bf16[192,32,128]{2,1,0:T(8,128)(2,1)} %p_hbm.1, s32[192,32,128]{2,1,0:T(8,128)} %s_hbm.1, bf16[2,192,32,128]{3,2,1,0:T(8,128)(2,1)} %get-tuple-element.8.cn_hbm, bf16[7,32,128]{2,1,0:T(8,128)(2,1)} %copy-done.2, bf16[7,32,128]{2,1,0:T(8,128)(2,1)} %copy-done.3, ...), custom_call_target="tpu_custom_call" | custom-call | flops 62914560 | bytes 15728640 | tf_op jit(solution)/shard_map/flow/pallas_call | solution.py:742
  111.9 0.0 all-to-all-done
  112.0 0.9 gather_inner.1.refs_9_
  112.9 0.0 collective-permute-done.8.refs_5_
  112.9 0.0 collective-permute-done.7.refs_4_
  112.9 1.6 %collective-permute-done.6.refs_3_ = bf16[6,48,512]{2,1,0:T(8,128)(2,1)S(1)} collective-permute-done((bf16[6,48,512]{2,1,0:T(8,128)(2,1)}, bf16[6,48,512]{2,1,0:T(8,128)(2,1)S(1)}, u32[]{:S(2)}, u32[]{:S(2)}) %collective-permute-start.6) | collective-permute-done | bytes 294944 | tf_op jit(solution)/shard_map/ppermute | solution.py:793
  114.5 0.0 collective-permute-done.5.refs_2_
  114.5 6.7 %collective-permute-done.4.refs_1_ = bf16[6,48,512]{2,1,0:T(8,128)(2,1)S(1)} collective-permute-done((bf16[6,48,512]{2,1,0:T(8,128)(2,1)S(1)}, bf16[6,48,512]{2,1,0:T(8,128)(2,1)S(1)}, u32[]{:S(2)}, u32[]{:S(2)}) %collective-permute-start.4) | collective-permute-done | bytes 294944 | tf_op jit(solution)/shard_map/ppermute | solution.py:793
  121.2 1.7 %gather_outer.1 = bf16[48,32,1024]{2,1,0:T(8,128)(2,1)} custom-call(s32[1]{0:T(128)} %bitcast.1.refs_1_.refs_0_, bf16[6,48,512]{2,1,0:T(8,128)(2,1)S(1)} %collective-permute-done.4.refs_1_, bf16[6,48,512]{2,1,0:T(8,128)(2,1)S(1)} %collective-permute-done.5.refs_2_, ...), custom_call_target="tpu_custom_call", output_to_operand_aliasing={{}: (9, {})} | custom-call | bytes 4718592 | tf_op jit(solution)/shard_map/gather_outer/pallas_call | solution.py:567
Async XLA Ops:
  10.7 101.3 %all-to-all-start = ((bf16[8,6,16,512]{3,2,1,0:T(8,128)(2,1)}), bf16[8,6,16,512]{3,2,1,0:T(8,128)(2,1)S(1)}, u32[]{:S(2)}, u32[]{:S(2)}) async-start(bf16[8,6,16,512]{3,2,1,0:T(8,128)(2,1)} %bitcast.5), calls=%async_computation | async-start | bytes 1572864 | tf_op jit(solution)/shard_map/all_to_all | solution.py:786
  22.9 14.9 %collective-permute-start.2 = (bf16[7,192,128]{2,1,0:T(8,128)(2,1)}, bf16[7,192,128]{2,1,0:T(8,128)(2,1)S(1)}, u32[]{:S(2)}, u32[]{:S(2)}) collective-permute-start(bf16[7,192,128]{2,1,0:T(8,128)(2,1)} %get-tuple-element.13), channel_id=1, source_target_pairs={{0,1},{1,2},{2,3},{3,4},{4,5},{5,6},{6,7},{7,0},{8,9},{9,10},{10,1... | collective-permute-start | bytes 1032200 | tf_op jit(solution)/shard_map/ppermute | solution.py:139
  24.6 13.2 %collective-permute-start.3 = (bf16[7,192,128]{2,1,0:T(8,128)(2,1)}, bf16[7,192,128]{2,1,0:T(8,128)(2,1)S(1)}, u32[]{:S(2)}, u32[]{:S(2)}) collective-permute-start(bf16[7,192,128]{2,1,0:T(8,128)(2,1)} %get-tuple-element.14), channel_id=1, source_target_pairs={{1,0},{2,1},{3,2},{4,3},{5,4},{6,5},{7,6},{0,7},{9,8},{10,9},{11,1... | collective-permute-start | bytes 1032200 | tf_op jit(solution)/shard_map/ppermute | solution.py:140
  24.6 4.4 %collective-permute-start = (bf16[7,32,128]{2,1,0:T(8,128)(2,1)}, bf16[7,32,128]{2,1,0:T(8,128)(2,1)S(1)}, u32[]{:S(2)}, u32[]{:S(2)}) collective-permute-start(bf16[7,32,128]{2,1,0:T(8,128)(2,1)} %get-tuple-element.11), channel_id=1, source_target_pairs={{0,8},{8,16},{16,24},{24,0},{1,9},{9,17},{17,25},{25,1},{2,10},{10... | collective-permute-start | bytes 172040 | tf_op jit(solution)/shard_map/ppermute | solution.py:137
  25.8 3.9 %collective-permute-start.1 = (bf16[7,32,128]{2,1,0:T(8,128)(2,1)}, bf16[7,32,128]{2,1,0:T(8,128)(2,1)S(1)}, u32[]{:S(2)}, u32[]{:S(2)}) collective-permute-start(bf16[7,32,128]{2,1,0:T(8,128)(2,1)} %get-tuple-element.12), channel_id=1, source_target_pairs={{8,0},{16,8},{24,16},{0,24},{9,1},{17,9},{25,17},{1,25},{10,2},{18... | collective-permute-start | bytes 172040 | tf_op jit(solution)/shard_map/ppermute | solution.py:138
  29.0 8.8 %copy-start.2 = (bf16[7,32,128]{2,1,0:T(8,128)(2,1)}, bf16[7,32,128]{2,1,0:T(8,128)(2,1)S(1)}, u32[]{:S(2)}) copy-start(bf16[7,32,128]{2,1,0:T(8,128)(2,1)S(1)} %collective-permute-done.refs_6_.xl_hbm) | copy-start | bytes 172036
  29.7 8.1 %copy-start.3 = (bf16[7,32,128]{2,1,0:T(8,128)(2,1)}, bf16[7,32,128]{2,1,0:T(8,128)(2,1)S(1)}, u32[]{:S(2)}) copy-start(bf16[7,32,128]{2,1,0:T(8,128)(2,1)S(1)} %collective-permute-done.1.refs_7_.xh_hbm) | copy-start | bytes 172036
  37.8 0.7 copy-start
  37.8 0.9 copy-start.1
  61.7 10.0 %collective-permute-start.10 = (bf16[6,48,512]{2,1,0:T(8,128)(2,1)S(1)}, bf16[6,48,512]{2,1,0:T(8,128)(2,1)S(1)}, u32[]{:S(2)}, u32[]{:S(2)}) collective-permute-start(bf16[6,48,512]{2,1,0:T(8,128)(2,1)S(1)} %get-tuple-element.20), channel_id=1, source_target_pairs={{0,7},{1,0},{2,1},{3,2},{4,3},{5,4},{6,5},{7,6},{8,15},{9,8},{10,9... | collective-permute-start | bytes 884744 | tf_op jit(solution)/shard_map/ppermute | solution.py:793
  65.6 13.7 %collective-permute-start.9 = (bf16[6,48,512]{2,1,0:T(8,128)(2,1)S(1)}, bf16[6,48,512]{2,1,0:T(8,128)(2,1)S(1)}, u32[]{:S(2)}, u32[]{:S(2)}) collective-permute-start(bf16[6,48,512]{2,1,0:T(8,128)(2,1)S(1)} %get-tuple-element.21), channel_id=1, source_target_pairs={{0,1},{1,2},{2,3},{3,4},{4,5},{5,6},{6,7},{7,0},{8,9},{9,10},{10,1... | collective-permute-start | bytes 884744 | tf_op jit(solution)/shard_map/ppermute | solution.py:793
  65.6 47.3 %collective-permute-start.8 = (bf16[6,48,512]{2,1,0:T(8,128)(2,1)}, bf16[6,48,512]{2,1,0:T(8,128)(2,1)S(1)}, u32[]{:S(2)}, u32[]{:S(2)}) collective-permute-start(bf16[6,48,512]{2,1,0:T(8,128)(2,1)} %get-tuple-element.22), channel_id=1, source_target_pairs={{0,6},{1,7},{2,0},{3,1},{4,2},{5,3},{6,4},{7,5},{8,14},{9,15},{10,... | collective-permute-start | bytes 884744 | tf_op jit(solution)/shard_map/ppermute | solution.py:793
  68.9 44.0 %collective-permute-start.7 = (bf16[6,48,512]{2,1,0:T(8,128)(2,1)}, bf16[6,48,512]{2,1,0:T(8,128)(2,1)S(1)}, u32[]{:S(2)}, u32[]{:S(2)}) collective-permute-start(bf16[6,48,512]{2,1,0:T(8,128)(2,1)} %get-tuple-element.23), channel_id=1, source_target_pairs={{0,2},{1,3},{2,4},{3,5},{4,6},{5,7},{6,0},{7,1},{8,10},{9,11},{10,... | collective-permute-start | bytes 884744 | tf_op jit(solution)/shard_map/ppermute | solution.py:793
  70.6 44.0 %collective-permute-start.6 = (bf16[6,48,512]{2,1,0:T(8,128)(2,1)}, bf16[6,48,512]{2,1,0:T(8,128)(2,1)S(1)}, u32[]{:S(2)}, u32[]{:S(2)}) collective-permute-start(bf16[6,48,512]{2,1,0:T(8,128)(2,1)} %get-tuple-element.24), channel_id=1, source_target_pairs={{0,5},{1,6},{2,7},{3,0},{4,1},{5,2},{6,3},{7,4},{8,13},{9,14},{10,... | collective-permute-start | bytes 884744 | tf_op jit(solution)/shard_map/ppermute | solution.py:793
  71.7 42.8 %collective-permute-start.5 = (bf16[6,48,512]{2,1,0:T(8,128)(2,1)}, bf16[6,48,512]{2,1,0:T(8,128)(2,1)S(1)}, u32[]{:S(2)}, u32[]{:S(2)}) collective-permute-start(bf16[6,48,512]{2,1,0:T(8,128)(2,1)} %get-tuple-element.25), channel_id=1, source_target_pairs={{0,3},{1,4},{2,5},{3,6},{4,7},{5,0},{6,1},{7,2},{8,11},{9,12},{10,... | collective-permute-start | bytes 884744 | tf_op jit(solution)/shard_map/ppermute | solution.py:793
  79.3 41.9 %collective-permute-start.4 = (bf16[6,48,512]{2,1,0:T(8,128)(2,1)S(1)}, bf16[6,48,512]{2,1,0:T(8,128)(2,1)S(1)}, u32[]{:S(2)}, u32[]{:S(2)}) collective-permute-start(bf16[6,48,512]{2,1,0:T(8,128)(2,1)S(1)} %get-tuple-element.26), channel_id=1, source_target_pairs={{0,4},{1,5},{2,6},{3,7},{4,0},{5,1},{6,2},{7,3},{8,12},{9,13},{10,... | collective-permute-start | bytes 884744 | tf_op jit(solution)/shard_map/ppermute | solution.py:793

commit v2 on v1

--- a/solution.py
+++ b/solution.py
@@ -21,6 +21,8 @@
 BF16 = jnp.bfloat16
 
 HBM = pl.BlockSpec(memory_space=pltpu.HBM)
+VMEM = pl.BlockSpec(memory_space=pltpu.VMEM)
+SMEM = pl.BlockSpec(memory_space=pltpu.SMEM)
 PARAMS = pltpu.CompilerParams(vmem_limit_bytes=60 * 2**20)
 
 
@@ -32,26 +34,18 @@
 
 
 def edge_kernel(*refs):
-    c_hbm, p_hbm, d_hbm, s_hbm, u_hbm, xf, xl, yf, yl = refs[:9]
-    c_x, p_x, d_x, s_x, u_x, c_y, p_y, d_y, s_y, u_y, tmp, tmp_s, x_sem, y_sem = refs[9:]
+    c_hbm, p_hbm, d_hbm, s_hbm, u_hbm, first, last = refs[:7]
+    c_y, p_y, d_y, s_y, u_y, tmp, tmp_s, y_sem = refs[7:]
     nx, ny, nz = p_hbm.shape
     cuts = y_sem.shape[2]
     step = nx // cuts
-    sources = (c_hbm, p_hbm, d_hbm, s_hbm, u_hbm)
-
-    def planes(n):
-        at = 0 if n == 0 else nx - 1
-        copies = []
-        for j, (src, dst) in enumerate(zip(sources, (c_x, p_x, d_x, s_x, u_x))):
-            part = src.at[:, at] if len(src.shape) == 4 else src.at[at]
-            copies.append(pltpu.make_async_copy(part, dst.at[n], x_sem.at[n, j]))
-        return copies
 
     def rows(n, i):
         part = pl.ds(i * step, step)
         row = pl.ds(0 if n == 0 else ny - TOP, TOP)
         copies = []
-        for j, (src, dst) in enumerate(zip(sources, (c_y, p_y, d_y, s_y, u_y))):
+        pairs = zip((c_hbm, p_hbm, d_hbm, s_hbm, u_hbm), (c_y, p_y, d_y, s_y, u_y))
+        for j, (src, dst) in enumerate(pairs):
             if len(src.shape) == 4:
                 pair = src.at[:, part, row], dst.at[n, :, part]
             else:
@@ -63,22 +57,9 @@
         for n in range(2):
             for copy in rows(n, i):
                 copy.start()
-    for n in range(2):
-        for copy in planes(n):
-            copy.start()
-    for n, out in enumerate((xf, xl)):
-        for copy in planes(n):
-            copy.wait()
-        solid = s_x[n] > 0
-        out[0] = c_x[n, 0]
-        out[1] = c_x[n, 1]
-        out[2] = p_x[n]
-        out[3] = jnp.where(solid, d_x[n].astype(F32), 0.0).astype(BF16)
-        for f in range(3):
-            out[4 + f] = jnp.where(solid, u_x[n, f].astype(F32), 0.0).astype(BF16)
     size = 16
     for i in range(cuts):
-        for n, out in enumerate((yf, yl)):
+        for n, out in enumerate((first, last)):
             for copy in rows(n, i):
                 copy.wait()
             row = 0 if n == 0 else TOP - 1
@@ -100,31 +81,25 @@
                     out[f, at, :] = v.astype(BF16)
 
 
-def edges(c, p, d, s, u):
-    nx, ny, nz = p.shape
-    vm = pltpu.VMEM
-    vmem = pl.BlockSpec(memory_space=vm)
+def field_scratch(shape):
+    leads = ((2, 2), (2,), (2,), (2,), (2, 3))
+    kinds = (BF16, BF16, BF16, jnp.int32, BF16)
+    return [pltpu.VMEM(lead + shape, kind) for lead, kind in zip(leads, kinds)]
+
+
+def edge_call(c, p, d, s, u):
+    nx, _, nz = p.shape
     cuts = 4
-
-    def pieces(shape):
-        return [
-            vm((2,) + (2,) * two + (3,) * three + shape, jnp.int32 if whole else BF16)
-            for two, three, whole in ((1, 0, 0), (0, 0, 0), (0, 0, 0), (0, 0, 1), (0, 1, 0))
-        ]
-
-    x_first, x_last, y_first, y_last = pl.pallas_call(
+    return pl.pallas_call(
         edge_kernel,
         name="edges",
-        out_shape=(jax.ShapeDtypeStruct((7, ny, nz), BF16),) * 2
-        + (jax.ShapeDtypeStruct((7, nx, nz), BF16),) * 2,
+        out_shape=(jax.ShapeDtypeStruct((7, nx, nz), BF16),) * 2,
         in_specs=[HBM] * 5,
-        out_specs=(vmem,) * 4,
-        scratch_shapes=pieces((ny, nz))
-        + pieces((nx, TOP, nz))
+        out_specs=(VMEM,) * 2,
+        scratch_shapes=field_scratch((nx, TOP, nz))
         + [
-            vm((7, 16 * TOP, nz), F32),
-            vm((16 * TOP, nz), jnp.int32),
-            pltpu.SemaphoreType.DMA((2, 5)),
+            pltpu.VMEM((7, 16 * TOP, nz), F32),
+            pltpu.VMEM((16 * TOP, nz), jnp.int32),
             pltpu.SemaphoreType.DMA((2, 5, cuts)),
         ],
         compiler_params=PARAMS,
@@ -132,17 +107,11 @@
             flops=20 * nx * nz, bytes_accessed=200 * nx * nz, transcendentals=0
         ),
     )(c, p, d, s, u)
-    x_fwd, x_bwd = rings("stream")
-    y_fwd, y_bwd = rings("tile")
-    low_x = lax.ppermute(x_last, "stream", x_fwd)
-    high_x = lax.ppermute(x_first, "stream", x_bwd)
-    low_y = lax.ppermute(y_last, "tile", y_fwd)
-    high_y = lax.ppermute(y_first, "tile", y_bwd)
-    return low_x, high_x, low_y, high_y
-
-
-def roll_lanes(value, shift):
-    return pltpu.roll(value, shift % value.shape[-1], axis=value.ndim - 1)
+
+
+def swap_ends(first, last, axis):
+    forward, backward = rings(axis)
+    return lax.ppermute(last, axis, forward), lax.ppermute(first, axis, backward)
 
 
 def face(low, high):
@@ -159,26 +128,33 @@
     return jnp.where(test(r, c), 1.0, 0.0)
 
 
-def ion_kernel(capacity, inner, *refs):
+def ion_kernel(capacity, mode, spread, *refs):
+    inner, mid, outer = mode == "inner", mode == "mid", mode == "outer"
     refs = list(refs)
-    plan, me, c_hbm, p_hbm, d_hbm, s_hbm = refs[:6]
-    refs = refs[6:]
-    edges_hbm = []
-    if not inner:
-        edges_hbm, refs = refs[:4], refs[5:]
-    cn_hbm, out_hbm, c_v, p_v, d_v, s_v = refs[:6]
-    refs = refs[6:]
-    if not inner:
-        xl_v, xh_v, yl_v, yh_v, yl_f, yh_f = refs[:6]
-        refs = refs[6:]
-    fld, cn_v, chs, blk, zero, perm, lanes, shift, shift2, dpot = refs[:10]
-    tally, in_sem, halo_sem, cn_sem, blk_sem, zero_sem = refs[10:]
+
+    def take(number):
+        taken = refs[:number]
+        del refs[:number]
+        return taken
+
+    plan, me, c_hbm, p_hbm, d_hbm, s_hbm = take(6)
     nx, _, nz = p_hbm.shape
     chunks = nx // BLK
     bz = nz // BLK
-    slots = out_hbm.shape[0]
-    tiles = slots // capacity
     count = chunks * bz
+    u_hbm = take(1)[0] if inner else None
+    edges_hbm = [] if inner else take(4 if outer else 2)
+    take(0 if inner else 1)
+    cn_hbm = take(1)[0]
+    outs = take(spread)
+    ends = take(2 if inner else 0)
+    c_v, p_v, d_v, s_v = take(4)
+    raw = take(5 if inner else 0)
+    edges_v = take(len(edges_hbm))
+    edges_f = take(2 if outer else 0)
+    fld, cn_v, chs, blk, zero, perm, lanes, shift, shift2, dpot = take(10)
+    tally, in_sem, halo_sem, cn_sem, blk_sem, zero_sem = refs
+    tiles = zero_sem.shape[0] // capacity
     m0, m1 = TOP, BLK - TOP
     first = m0 - 1 if inner else 0
     depth = m1 + 1 - first if inner else BLK
@@ -192,29 +168,40 @@
             pltpu.make_async_copy(s_hbm.at[part], s_v.at[part], in_sem.at[3, i]),
         )
 
-    halos = []
-    if not inner:
-        for n, (src, dst) in enumerate(zip(edges_hbm, (xl_v, xh_v, yl_v, yh_v))):
-            halos.append(pltpu.make_async_copy(src.at[pl.ds(0, 4)], dst, halo_sem.at[n]))
-    for copy in halos:
-        copy.start()
+    halos = [
+        pltpu.make_async_copy(src.at[pl.ds(0, 4)], dst, halo_sem.at[n])
+        for n, (src, dst) in enumerate(zip(edges_hbm, edges_v))
+    ]
+    if inner:
+        for j, (src, dst) in enumerate(zip((c_hbm, p_hbm, d_hbm, s_hbm, u_hbm), raw)):
+            for n in range(2):
+                at = n * (nx - 1)
+                part = src.at[:, at] if len(src.shape) == 4 else src.at[at]
+                halos.append(pltpu.make_async_copy(part, dst.at[n], halo_sem.at[2 * j + n]))
+    else:
+        for copy in halos:
+            copy.start()
     for i in range(chunks):
         for copy in loads(i):
             copy.start()
+    if inner:
+        for copy in halos:
+            copy.start()
 
     zero[...] = jnp.zeros_like(zero)
     width = BLK * TOP
-    if not inner:
-        perm[1] = onehot(
+    if outer:
+        perm[0] = onehot(
             width, width, lambda r, c: (r // BLK == c % TOP) & (r % BLK == c // TOP)
         ).astype(BF16)
     half = BLK // 2
-    perm[0] = onehot(
-        width,
-        width,
-        lambda r, c: (r // half == (c // (half * TOP)) * TOP + c % TOP)
-        & (r % half == (c // TOP) % half),
-    ).astype(BF16)
+    if not outer:
+        perm[0] = onehot(
+            width,
+            width,
+            lambda r, c: (r // half == (c // (half * TOP)) * TOP + c % TOP)
+            & (r % half == (c // TOP) % half),
+        ).astype(BF16)
     wide = bz * nz
     lanes[...] = onehot(
         wide,
@@ -235,23 +222,39 @@
         tally[count + o] = 0
 
     def place(o):
-        return o if inner else lax.rem(o + tiles - me[0], tiles)
+        return o if spread == 1 else lax.rem(o + tiles - me[0], tiles)
 
     @pl.loop(0, count)
     def _(b):
         o = place(plan[b])
         rank = tally[count + o]
-        tally[b] = o * capacity + rank
+        tally[b] = rank if spread > 1 else o * capacity + rank
         tally[count + o] = rank + 1
 
-    def blank(slot):
-        return pltpu.make_async_copy(zero, out_hbm.at[slot], zero_sem.at[slot])
-
-    @pl.loop(0, tiles)
-    def _(o):
-        @pl.loop(tally[count + o], capacity)
-        def _(k):
-            blank(o * capacity + k).start()
+    def blank(o, k, ref=None):
+        if spread == 1:
+            return pltpu.make_async_copy(
+                zero, outs[0].at[o * capacity + k], zero_sem.at[o * capacity + k]
+            )
+        return pltpu.make_async_copy(zero, ref.at[k], zero_sem.at[o * capacity + k])
+
+    def blanks(act):
+        if spread == 1:
+
+            @pl.loop(0, tiles)
+            def _(o):
+                @pl.loop(tally[count + o], capacity)
+                def _(k):
+                    act(blank(o, k))
+
+            return
+        for o in range(tiles):
+
+            @pl.loop(tally[count + o], capacity)
+            def _(k, o=o):
+                act(blank(o, k, outs[o]))
+
+    blanks(lambda copy: copy.start())
 
     body = pl.ds(TOP, BLK)
 
@@ -264,10 +267,10 @@
     if not inner:
         for copy in halos:
             copy.wait()
-        for plane, ref in ((0, xl_v), (nx + 1, xh_v)):
+        for plane, ref in zip((0, nx + 1), edges_v):
             for f in range(4):
                 fld[f, plane, body, :] = scaled(f, ref[f])
-        for ref, dst in ((yl_v, yl_f), (yh_v, yh_f)):
+        for ref, dst in zip(edges_v[2:], edges_f):
             for f in range(4):
                 dst[f] = scaled(f, ref[f])
 
@@ -283,13 +286,16 @@
     def prepare(i):
         for copy in loads(i):
             copy.wait()
-        if inner:
-            convert(i * BLK + first, 1)
+        if not outer:
+            convert(i * BLK + m0 - 1, 1)
+            convert(i * BLK + m0, 1) if mid else None
+            convert(i * BLK + m1 - 1, 1) if mid else None
             convert(i * BLK + m1, 1)
 
-            @pl.loop(m0 // 4, m1 // 4)
+            @pl.loop(0, 4)
             def _(q):
-                convert(i * BLK + q * 4, 4)
+                shifted = q * 4 + (m0 if inner else jnp.where(q >= 2, m1 - m0, 0))
+                convert(i * BLK + shifted, 4)
 
             return
 
@@ -299,8 +305,8 @@
             convert(x, 4)
             for j in range(4):
                 for f in range(4):
-                    fld[f, x + 1 + j, pl.ds(TOP - 1, 1), :] = yl_f[f, pl.ds(x + j, 1), :]
-                    fld[f, x + 1 + j, pl.ds(TOP + BLK, 1), :] = yh_f[f, pl.ds(x + j, 1), :]
+                    for n, row in enumerate((TOP - 1, TOP + BLK)):
+                        fld[f, x + 1 + j, pl.ds(row, 1), :] = edges_f[n][f, pl.ds(x + j, 1), :]
 
     batch = TOP
 
@@ -363,17 +369,29 @@
     def saves(i):
         x = i * BLK
         spots = [(m0, m1 - m0, m0, m1 - m0)]
-        if not inner:
-            spots = [(0, BLK, 0, TOP), (0, BLK, m1, TOP), (0, m0, m0, m1 - m0)]
-            spots.append((m1, TOP, m0, m1 - m0))
+        if mid:
+            spots = [(0, m0, m0, m1 - m0), (m1, TOP, m0, m1 - m0)]
+        if outer:
+            spots = [(0, BLK, 0, TOP), (0, BLK, m1, TOP)]
         copies = []
         for n, (px, number, row, tall) in enumerate(spots):
             at = (slice(None), pl.ds(x + px, number), pl.ds(row, tall))
             copies.append(pltpu.make_async_copy(cn_v.at[at], cn_hbm.at[at], cn_sem.at[n, i]))
         return copies
 
-    def put(b):
-        return pltpu.make_async_copy(blk.at[b], out_hbm.at[tally[b]], blk_sem.at[b])
+    def put(b, n=0):
+        return pltpu.make_async_copy(blk.at[b], outs[n].at[tally[b]], blk_sem.at[b])
+
+    def send(b):
+        if spread == 1:
+            put(b).start()
+            return
+        shift = place(plan[b])
+        for n in range(tiles):
+
+            @pl.when(shift == n)
+            def _(n=n):
+                put(b, n).start()
 
     def joined(t, size):
         groups = t.shape[0] // (size * bz)
@@ -402,46 +420,50 @@
                 for t in range(2):
                     keep(0, t * middle + q * batch * TOP, charge[:, t * TOP : (t + 1) * TOP])
 
-        else:
+        if mid:
+
+            @pl.loop(0, 2)
+            def _(q):
+                charge = update(x + q * m1, m0, m1 - m0)
+                for t in range(2):
+                    keep(0, t * middle + q * batch * TOP, charge[:, t * TOP : (t + 1) * TOP])
+
+        if outer:
 
             @pl.loop(0, BLK // batch)
             def _(q):
                 for t, row in enumerate((0, m1)):
-                    keep(1 + t, q * batch * TOP, update(x + q * batch, row, TOP))
-
-            for q, px in enumerate((0, m1)):
-                charge = update(x + px, m0, m1 - m0)
-                for t in range(2):
-                    keep(0, t * middle + q * batch * TOP, charge[:, t * TOP : (t + 1) * TOP])
+                    keep(t, q * batch * TOP, update(x + q * batch, row, TOP))
 
         for copy in saves(i):
             copy.start()
+        size = BLK if outer else half
         rowsets = []
-        if not inner:
-            for t in range(2):
-                v = jnp.dot(perm[1], chs[1 + t], preferred_element_type=F32).astype(BF16)
-                rowsets += joined(v, BLK)
-        v = jnp.dot(perm[0], chs[0], preferred_element_type=F32).astype(BF16)
-        rowsets += joined(v, half)
+        for t in range(2 if outer else 1):
+            v = jnp.dot(perm[0], chs[t], preferred_element_type=F32).astype(BF16)
+            rowsets += joined(v, size)
         res = jnp.dot(
             jnp.concatenate(rowsets, axis=0), lanes[...], preferred_element_type=F32
         ).astype(BF16)
-        groups = TOP // bz
         for k in range(bz):
-            row = 0
-            if not inner:
-                for j in range(2 * groups):
-                    blk[i * bz + k, 0:BLK, j * nz : (j + 1) * nz] = res[
-                        row : row + BLK, k * nz : (k + 1) * nz
-                    ]
-                    row += BLK
-            base = 0 if inner else BLK
-            for j in range(2 * groups):
-                blk[i * bz + k, base : base + half, j * nz : (j + 1) * nz] = res[
-                    row : row + half, k * nz : (k + 1) * nz
+            for j in range(len(rowsets)):
+                blk[i * bz + k, :, j * nz : (j + 1) * nz] = res[
+                    j * size : (j + 1) * size, k * nz : (k + 1) * nz
                 ]
-                row += half
-            put(i * bz + k).start()
+            send(i * bz + k)
+
+    if inner:
+        for copy in halos:
+            copy.wait()
+        c_x, p_x, d_x, s_x, u_x = raw
+        for n, out in enumerate(ends):
+            solid = s_x[n] > 0
+            out[0] = c_x[n, 0]
+            out[1] = c_x[n, 1]
+            out[2] = p_x[n]
+            out[3] = jnp.where(solid, d_x[n].astype(F32), 0.0).astype(BF16)
+            for f in range(3):
+                out[4 + f] = jnp.where(solid, u_x[n, f].astype(F32), 0.0).astype(BF16)
 
     @pl.loop(0, chunks)
     def _(i):
@@ -452,64 +474,54 @@
     def _(b):
         put(b).wait()
 
-    @pl.loop(0, tiles)
-    def _(o):
-        @pl.loop(tally[count + o], capacity)
-        def _(k):
-            blank(o * capacity + k).wait()
-
-
-def ion_call(plan, me, c, p, d, s, halo, before, capacity, tiles):
+    blanks(lambda copy: copy.wait())
+
+
+def ion_call(mode, plan, me, c, p, d, s, u, halo, before, capacity, tiles):
     _, nx, ny, nz = c.shape
     count = plan.shape[0]
     chunks = nx // BLK
     bz = nz // BLK
-    inner = before is None
-    args = [plan, me, c, p, d, s] + ([] if inner else list(halo) + [before])
-    deep = BLK // 2 if inner else BLK + BLK // 2
+    inner, outer = mode == "inner", mode == "outer"
+    args = [plan, me, c, p, d, s] + ([u] if inner else list(halo) + [before])
+    deep = BLK if outer else BLK // 2
     wide = BLK * BLK // 2
+    spread = tiles if outer else 1
     vm = pltpu.VMEM
     dma = pltpu.SemaphoreType.DMA
-    ends = [
-        vm((4, ny, nz), BF16),
-        vm((4, ny, nz), BF16),
-        vm((4, nx, nz), BF16),
-        vm((4, nx, nz), BF16),
-        vm((4, nx, nz), F32),
-        vm((4, nx, nz), F32),
-    ]
-    share = 0.25 if inner else 0.75
+    extra = field_scratch((ny, nz)) if inner else [vm((4, ny, nz), BF16)] * 2
+    if outer:
+        extra += [vm((4, nx, nz), BF16)] * 2 + [vm((4, nx, nz), F32)] * 2
+    share = 0.5 if outer else 0.25
+    part = jax.ShapeDtypeStruct((tiles * capacity // spread, deep, wide), BF16)
+    end = jax.ShapeDtypeStruct((7, ny, nz), BF16)
     return pl.pallas_call(
-        functools.partial(ion_kernel, capacity, inner),
-        name="ion_inner" if inner else "ion_outer",
-        out_shape=(
-            jax.ShapeDtypeStruct(c.shape, BF16),
-            jax.ShapeDtypeStruct((tiles * capacity, deep, wide), BF16),
-        ),
-        in_specs=[pl.BlockSpec(memory_space=pltpu.SMEM)] * 2 + [HBM] * (len(args) - 2),
-        out_specs=(HBM, HBM),
+        functools.partial(ion_kernel, capacity, mode, spread),
+        out_shape=[jax.ShapeDtypeStruct(c.shape, BF16)] + [part] * spread + [end] * (2 * inner),
+        in_specs=[SMEM] * 2 + [HBM] * (len(args) - 2),
+        out_specs=[HBM] * (1 + spread) + [VMEM] * (2 * inner),
         scratch_shapes=[
             vm(c.shape, BF16),
             vm(p.shape, BF16),
             vm(p.shape, BF16),
             vm(p.shape, jnp.int32),
         ]
-        + ([] if inner else ends)
+        + extra
         + [
             vm((4, nx + 2, ROWS, nz), F32),
             vm(c.shape, BF16),
-            vm((1 if inner else 3, BLK * TOP, nz), BF16),
+            vm((2 if outer else 1, BLK * TOP, nz), BF16),
             vm((count, deep, wide), BF16),
             vm((deep, wide), BF16),
-            vm((2, BLK * TOP, BLK * TOP), BF16),
+            vm((1, BLK * TOP, BLK * TOP), BF16),
             vm((bz * nz, bz * nz), BF16),
             vm((nz, 2 * nz), BF16),
             vm((2 * nz, 2 * nz), BF16),
             vm((nz, 2 * nz), BF16),
             pltpu.SMEM((count + tiles,), jnp.int32),
             dma((4, chunks)),
-            dma((4,)),
-            dma((4, chunks)),
+            dma((10,)),
+            dma((2, chunks)),
             dma((count,)),
             dma((tiles * capacity,)),
         ],
@@ -550,26 +562,20 @@
             copy.wait()
 
 
-def gather_call(me, parts, shifts, inner, before, slots, capacity):
+def gather_call(mode, me, parts, shifts, before, slots, capacity):
     q, h = BLK * BLK // 4, BLK // 2
     t = TOP
-    if inner:
-        boxes = (((0, 0), (t, q), h, 2 * q),)
-    else:
-        boxes = (
-            ((0, 0), (0, 0), BLK, q),
-            ((0, q), (0, 3 * q), BLK, q),
-            ((BLK, 0), (0, q), t, 2 * q),
-            ((BLK + t, 0), (BLK - t, q), t, 2 * q),
-        )
-    vmem = pl.BlockSpec(memory_space=pltpu.VMEM)
+    boxes = {
+        "inner": (((0, 0), (t, q), h, 2 * q),),
+        "mid": (((0, 0), (0, q), t, 2 * q), ((t, 0), (BLK - t, q), t, 2 * q)),
+        "outer": (((0, 0), (0, 0), BLK, q), ((0, q), (0, 3 * q), BLK, q)),
+    }[mode]
     args = [me] + list(parts) + ([] if before is None else [before])
     return pl.pallas_call(
         functools.partial(gather_kernel, boxes, capacity, shifts, before is not None),
-        name="gather_inner" if inner else "gather_outer",
         out_shape=jax.ShapeDtypeStruct((slots, BLK, BLK * BLK), BF16),
-        in_specs=[pl.BlockSpec(memory_space=pltpu.SMEM)]
-        + [vmem] * len(parts)
+        in_specs=[SMEM]
+        + [VMEM] * len(parts)
         + [HBM] * (before is not None),
         out_specs=HBM,
         scratch_shapes=[pltpu.SemaphoreType.DMA((len(parts), len(boxes)))],
@@ -607,6 +613,7 @@
     yh_f,
     fld,
     un_v,
+    mix,
     in_sem,
     halo_sem,
     un_sem,
@@ -669,50 +676,48 @@
                 fld[f, x + 1, pl.ds(TOP - 1, 1), :] = yl_f[f, pl.ds(x, 1), :]
                 fld[f, x + 1, pl.ds(TOP + BLK, 1), :] = yh_f[f, pl.ds(x, 1), :]
 
-    half = 16
-    lane = lax.broadcasted_iota(jnp.int32, (half, nz), 1)
-    first_lane = lane == 0
-    last_lane = lane == nz - 1
-    k_mid = flow_step * viscosity
-    k_adv = flow_step * 0.5
-
-    def below(v):
-        return jnp.where(first_lane, 0.0, roll_lanes(v, 1))
-
-    def above(v):
-        return jnp.where(last_lane, 0.0, roll_lanes(v, -1))
+    up = onehot(nz, nz, lambda r, c: r == c + 1)
+    down = onehot(nz, nz, lambda r, c: r == c - 1)
+    mix[:, 0:nz] = ((up + down) * viscosity).astype(BF16)
+    mix[:, nz : 2 * nz] = ((up - down) * 0.5).astype(BF16)
+    batch, tall = 4, 16
 
     def update(i):
-        @pl.loop(0, BLK)
+        @pl.loop(0, BLK // batch)
         def _(q):
-            x = i * BLK + q
-            for y0 in range(0, BLK, half):
-                at = pl.ds(TOP + y0, half)
-                mid = [fld[f, x + 1, at, :] for f in range(3)]
-                field = fld[3, x + 1, at, :]
-                fluid = s_v[x, pl.ds(y0, half), :] > 0
-                cn0 = cn_v[0, x, pl.ds(y0, half), :].astype(F32)
-                cn1 = cn_v[1, x, pl.ds(y0, half), :].astype(F32)
-                push = (cn0 - cn1) * k_adv
-                plus = [k_mid - k_adv * u for u in mid]
-                minus = [k_mid + k_adv * u for u in mid]
+            x = i * BLK + q * batch
+            here = pl.ds(x + 1, batch)
+            for y0 in range(0, BLK, tall):
+                at = pl.ds(TOP + y0, tall)
+                next_y, last_y = pl.ds(TOP + 1 + y0, tall), pl.ds(TOP - 1 + y0, tall)
+                own = pl.ds(y0, tall)
+                mid = [fld[f, here, at, :] for f in range(4)]
+                m = batch * tall
+                stack = jnp.concatenate([v.reshape(m, nz) for v in mid], axis=0).astype(BF16)
+                z = jnp.dot(stack, mix[...], preferred_element_type=F32)
+                z = [z[f * m : (f + 1) * m] for f in range(4)]
+                fluid = s_v[pl.ds(x, batch), own, :] > 0
+                push = cn_v[0, pl.ds(x, batch), own, :].astype(F32)
+                push = (push - cn_v[1, pl.ds(x, batch), own, :].astype(F32)) * 0.5
+                plus = [viscosity - 0.5 * u for u in mid[:2]]
+                minus = [viscosity + 0.5 * u for u in mid[:2]]
                 for a in range(3):
-                    total = mid[a] * (1.0 - 6.0 * k_mid)
-                    total = total + fld[a, x + 2, at, :] * plus[0] + fld[a, x, at, :] * minus[0]
-                    total = total + fld[a, x + 1, pl.ds(TOP + 1 + y0, half), :] * plus[1]
-                    total = total + fld[a, x + 1, pl.ds(TOP - 1 + y0, half), :] * minus[1]
-                    total = total + above(mid[a]) * plus[2] + below(mid[a]) * minus[2]
+                    total = fld[a, pl.ds(x + 2, batch), at, :] * plus[0]
+                    total = total + fld[a, pl.ds(x, batch), at, :] * minus[0]
+                    total = total + fld[a, here, next_y, :] * plus[1]
+                    total = total + fld[a, here, last_y, :] * minus[1]
+                    total = total + z[a][:, :nz].reshape(batch, tall, nz)
+                    total = total - mid[2] * z[a][:, nz:].reshape(batch, tall, nz)
                     if a == 0:
-                        rise = fld[3, x + 2, at, :] - fld[3, x, at, :]
+                        rise = fld[3, pl.ds(x + 2, batch), at, :] - fld[3, pl.ds(x, batch), at, :]
                     elif a == 1:
-                        rise = (
-                            fld[3, x + 1, pl.ds(TOP + 1 + y0, half), :]
-                            - fld[3, x + 1, pl.ds(TOP - 1 + y0, half), :]
-                        )
+                        rise = fld[3, here, next_y, :] - fld[3, here, last_y, :]
                     else:
-                        rise = above(field) - below(field)
-                    total = jnp.where(fluid, total - push * rise, 0.0)
-                    un_v[a, x, pl.ds(y0, half), :] = total.astype(BF16)
+                        rise = z[3][:, nz:].reshape(batch, tall, nz) * 2.0
+                    total = total - push * rise
+                    value = mid[a] * (1.0 - 6.0 * viscosity * flow_step) + flow_step * total
+                    value = jnp.where(fluid, value, 0.0)
+                    un_v[a, pl.ds(x, batch), own, :] = value.astype(BF16)
 
     def saves(i):
         part = pl.ds(i * BLK, BLK)
@@ -762,6 +767,7 @@
             vm((4, nx, nz), F32),
             vm((4, nx + 2, ROWS, nz), F32),
             vm(u.shape, BF16),
+            vm((nz, 2 * nz), BF16),
             dma((4, chunks)),
             dma((8,)),
             dma((chunks,)),
@@ -786,22 +792,28 @@
         part = lax.all_to_all(part, "tile", split_axis=0, concat_axis=0, tiled=True)
         return part.reshape((slots,) + part.shape[2:])
 
-    def pass_on(part, shift):
-        piece = part[shift * capacity : (shift + 1) * capacity]
+    def pass_on(piece, shift):
         if shift == 0:
             return piece
         return lax.ppermute(piece, "tile", [(i, (i + shift) % tiles) for i in range(tiles)])
 
-    halo = edges(concentration, potential, diffusivity, spacer, velocity)
-    given = (balance_plan[:, 0], me, concentration, potential, diffusivity, spacer)
-    conc, first = ion_call(*given, None, None, capacity, tiles)
+    given = (balance_plan[:, 0], me, concentration, potential, diffusivity, spacer, velocity)
+    conc, first, x_first, x_last = ion_call("inner", *given, None, None, capacity, tiles)
     first = exchange(first)
-    conc_next, second = ion_call(*given, halo, conc, capacity, tiles)
+    x_halo = swap_ends(x_first, x_last, "stream")
+    y_first, y_last = edge_call(*given[2:])
+    y_halo = swap_ends(y_first, y_last, "tile")
+    conc, second = ion_call("mid", *given, x_halo, conc, capacity, tiles)
+    second = exchange(second)
+    halo = x_halo + y_halo
+    conc_next, *third = ion_call("outer", *given, halo, conc, capacity, tiles)
     order = sorted(range(1, tiles), key=lambda d: -min(d, tiles - d)) + [0]
-    pieces = [pass_on(second, d) for d in order]
+    third = [pass_on(third[d], d) for d in order]
     flow_next = flow_call(velocity, potential, spacer, conc_next, halo)
-    owned = gather_call(jnp.zeros_like(me), [first], (0,), True, None, slots, capacity)
-    owned = gather_call(me, pieces, tuple(order), False, owned, slots, capacity)
+    none = jnp.zeros_like(me)
+    owned = gather_call("inner", none, [first], (0,), None, slots, capacity)
+    owned = gather_call("mid", none, [second], (0,), owned, slots, capacity)
+    owned = gather_call("outer", me, third, tuple(order), owned, slots, capacity)
     return conc_next, flow_next, owned
 
 

time: 123 us -> 133 us (1.081)
  the two profiles are of different devices: /device:TPU:1 before, /device:TPU:0 now
where the time goes in v2:
time: 133 us
  Pallas kernels  67.3 us (51%)
  waiting for transfers between devices  34.4 us (26%)
  starting transfers between devices  28.5 us (21%)
  local copies, waits for them, and re-layouts  1.55 us (1%)
    pallas_call x3, Pallas kernels, ion_call(): pl.pallas_call(functools.partial(ion_kernel, capacity, mode, spread), out...  40.1 us
    pallas_call x1, Pallas kernels, flow_call(): pl.pallas_call(flow_kernel, name='flow', out_shape=jax.ShapeDtypeStruct(u...  19.5 us
    ppermute x2, waiting for transfers between devices, swap_ends(): lax.ppermute(last, axis, forward)  18.7 us
    ppermute x7, waiting for transfers between devices, pass_on(): lax.ppermute(piece, 'tile', [(i, (i + shift) % tiles) for i in range(tile...  13.2 us
    ppermute x7, starting transfers between devices, pass_on(): lax.ppermute(piece, 'tile', [(i, (i + shift) % tiles) for i in range(tile...  12 us
    all_to_all x2, starting transfers between devices, exchange(): part = lax.all_to_all(part, 'tile', split_axis=0, concat_axis=0, tiled=True)  9.94 us
    pallas_call x1, Pallas kernels, edge_call(): pl.pallas_call(edge_kernel, name='edges', out_shape=(jax.ShapeDtypeStruct...  4.66 us
    ppermute x2, starting transfers between devices, swap_ends(): lax.ppermute(first, axis, backward)  4.55 us
  transfers between devices with their start and end apart: 13, of which 6 were waited for; matrix products, arithmetic and copies ran while one was open for 0% of the time, Pallas kernels for 42%

profile of v2, /device:TPU:0, one launch (start us, length us, event | category | flops | bytes accessed | tf_op | source)
XLA Modules:
  0.0 132.6 jit_solution(1236138518938264996)
XLA Ops:
  0.6 10.6 %shard_map.85 = (bf16[2,192,32,128]{3,2,1,0:T(8,128)(2,1)}, bf16[48,16,512]{2,1,0:T(8,128)(2,1)}, bf16[7,32,128]{2,1,0:T(8,128)(2,1)}, bf16[7,32,128]{2,1,0:T(8,128)(2,1)}) custom-call(s32[24]{0:T(128)} %bitcast.10, s32[1]{0:T(128)} %bitcast.1.refs_1_.refs_0_, bf16[2,192,32,128]{3,2,1,0:T(8,128)(2,1)} %refs_2_.7, bf16[192,32,128]{2,1,0:T(8,128)(2,1)} %p_hbm.1, ...), custom_call_target="tpu_custom_call" | custom-call | flops 19660800 | bytes 11796480 | tf_op jit(solution)/shard_map/pallas_call | solution.py:498
  11.3 6.4 %all-to-all-start.1 = ((bf16[8,6,16,512]{3,2,1,0:T(8,128)(2,1)}), bf16[8,6,16,512]{3,2,1,0:T(8,128)(2,1)S(1)}, u32[]{:S(2)}, u32[]{:S(2)}) async-start(bf16[8,6,16,512]{3,2,1,0:T(8,128)(2,1)} %bitcast.9), calls=%async_computation.1 | async-start | bytes 1572864 | tf_op jit(solution)/shard_map/all_to_all | solution.py:792
  17.7 1.5 %collective-permute-start = (bf16[7,32,128]{2,1,0:T(8,128)(2,1)}, bf16[7,32,128]{2,1,0:T(8,128)(2,1)S(1)}, u32[]{:S(2)}, u32[]{:S(2)}) collective-permute-start(bf16[7,32,128]{2,1,0:T(8,128)(2,1)} %get-tuple-element.20), channel_id=1, source_target_pairs={{0,8},{8,16},{16,24},{24,0},{1,9},{9,17},{17,25},{25,1},{2,10},{10... | collective-permute-start | bytes 172040 | tf_op jit(solution)/shard_map/ppermute | solution.py:114
  19.1 1.5 %collective-permute-start.1 = (bf16[7,32,128]{2,1,0:T(8,128)(2,1)}, bf16[7,32,128]{2,1,0:T(8,128)(2,1)S(1)}, u32[]{:S(2)}, u32[]{:S(2)}) collective-permute-start(bf16[7,32,128]{2,1,0:T(8,128)(2,1)} %get-tuple-element.21), channel_id=1, source_target_pairs={{8,0},{16,8},{24,16},{0,24},{9,1},{17,9},{25,17},{1,25},{10,2},{18... | collective-permute-start | bytes 172040 | tf_op jit(solution)/shard_map/ppermute | solution.py:114
  20.6 2.5 %collective-permute-done.refs_6_.xl_hbm = bf16[7,32,128]{2,1,0:T(8,128)(2,1)S(1)} collective-permute-done((bf16[7,32,128]{2,1,0:T(8,128)(2,1)}, bf16[7,32,128]{2,1,0:T(8,128)(2,1)S(1)}, u32[]{:S(2)}, u32[]{:S(2)}) %collective-permute-start) | collective-permute-done | bytes 57376 | tf_op jit(solution)/shard_map/ppermute | solution.py:114
  23.1 0.0 copy-start.3
  23.1 1.3 collective-permute-done.1.refs_7_.xh_hbm
  24.4 0.0 copy-start.4
  24.4 0.0 copy-done.3
  24.4 0.6 copy-done.4
  25.0 12.4 %shard_map.86 = (bf16[2,192,32,128]{3,2,1,0:T(8,128)(2,1)}, bf16[48,16,512]{2,1,0:T(8,128)(2,1)}) custom-call(s32[24]{0:T(128)} %bitcast.11, s32[1]{0:T(128)} %bitcast.1.refs_1_.refs_0_, bf16[2,192,32,128]{3,2,1,0:T(8,128)(2,1)} %refs_2_.7, bf16[192,32,128]{2,1,0:T(8,128)(2,1)} %p_hbm.1, ...), custom_call_target="tpu_custom_call", output_to_operand_aliasing={{0}: (8, {})} | custom-call | flops 19660800 | bytes 11796480 | tf_op jit(solution)/shard_map/pallas_call | solution.py:498
  37.4 1.2 all-to-all-done.1
  38.6 3.5 %all-to-all-start = ((bf16[8,6,16,512]{3,2,1,0:T(8,128)(2,1)}), bf16[8,6,16,512]{3,2,1,0:T(8,128)(2,1)S(1)}, u32[]{:S(2)}, u32[]{:S(2)}) async-start(bf16[8,6,16,512]{3,2,1,0:T(8,128)(2,1)} %bitcast.8), calls=%async_computation | async-start | bytes 1572864 | tf_op jit(solution)/shard_map/all_to_all | solution.py:792
  42.2 4.7 %edges.1 = (bf16[7,192,128]{2,1,0:T(8,128)(2,1)}, bf16[7,192,128]{2,1,0:T(8,128)(2,1)}) custom-call(bf16[2,192,32,128]{3,2,1,0:T(8,128)(2,1)} %refs_2_.7, bf16[192,32,128]{2,1,0:T(8,128)(2,1)} %p_hbm.1, bf16[192,32,128]{2,1,0:T(8,128)(2,1)} %refs_4_.7, s32[192,32,128]{2,1,0:T(8,128)} %s_hbm.1, bf16[3,192,32,128]{3,2,1,0:T(8,128)(2,1)} %u_hbm.1), custom_call_target="tpu_custom_call" | custom-call | flops 491520 | bytes 4915200 | tf_op jit(solution)/shard_map/edges/pallas_call | solution.py:93
  46.8 0.5 collective-permute-start.2
  47.3 3.1 %collective-permute-start.3 = (bf16[7,192,128]{2,1,0:T(8,128)(2,1)}, bf16[7,192,128]{2,1,0:T(8,128)(2,1)S(1)}, u32[]{:S(2)}, u32[]{:S(2)}) collective-permute-start(bf16[7,192,128]{2,1,0:T(8,128)(2,1)} %get-tuple-element.23), channel_id=1, source_target_pairs={{1,0},{2,1},{3,2},{4,3},{5,4},{6,5},{7,6},{0,7},{9,8},{10,9},{11,1... | collective-permute-start | bytes 1032200 | tf_op jit(solution)/shard_map/ppermute | solution.py:114
  50.4 16.2 %collective-permute-done.2.refs_8_.yl_hbm = bf16[7,192,128]{2,1,0:T(8,128)(2,1)S(1)} collective-permute-done((bf16[7,192,128]{2,1,0:T(8,128)(2,1)}, bf16[7,192,128]{2,1,0:T(8,128)(2,1)S(1)}, u32[]{:S(2)}, u32[]{:S(2)}) %collective-permute-start.2) | collective-permute-done | bytes 344096 | tf_op jit(solution)/shard_map/ppermute | solution.py:114
  66.6 0.0 copy-start.1
  66.6 0.0 collective-permute-done.3.refs_9_.yh_hbm
  66.6 0.0 copy-start.2
  66.6 0.7 copy-done.1
  67.4 0.1 copy-done.2
  67.5 17.1 %shard_map.87 = (bf16[2,192,32,128]{3,2,1,0:T(8,128)(2,1)}, bf16[6,32,512]{2,1,0:T(8,128)(2,1)}, bf16[6,32,512]{2,1,0:T(8,128)(2,1)}, bf16[6,32,512]{2,1,0:T(8,1...) custom-call(s32[24]{0:T(128)} %bitcast.12, ...), custom_call_target="tpu_custom_call", output_to_operand_aliasing={{0}: (10, {})} | custom-call | flops 39321600 | bytes 23592960 | tf_op jit(solution)/shard_map/pallas_call | solution.py:498
  84.6 4.2 %collective-permute-start.4 = (bf16[6,32,512]{2,1,0:T(8,128)(2,1)}, bf16[6,32,512]{2,1,0:T(8,128)(2,1)S(1)}, u32[]{:S(2)}, u32[]{:S(2)}) collective-permute-start(bf16[6,32,512]{2,1,0:T(8,128)(2,1)} %get-tuple-element.27), channel_id=1, source_target_pairs={{0,4},{1,5},{2,6},{3,7},{4,0},{5,1},{6,2},{7,3},{8,12},{9,13},{10,... | collective-permute-start | bytes 589832 | tf_op jit(solution)/shard_map/ppermute | solution.py:798
  88.8 0.0 collective-permute-start.5
  88.8 2.6 %collective-permute-start.6 = (bf16[6,32,512]{2,1,0:T(8,128)(2,1)}, bf16[6,32,512]{2,1,0:T(8,128)(2,1)S(1)}, u32[]{:S(2)}, u32[]{:S(2)}) collective-permute-start(bf16[6,32,512]{2,1,0:T(8,128)(2,1)} %get-tuple-element.29), channel_id=1, source_target_pairs={{0,5},{1,6},{2,7},{3,0},{4,1},{5,2},{6,3},{7,4},{8,13},{9,14},{10,... | collective-permute-start | bytes 589832 | tf_op jit(solution)/shard_map/ppermute | solution.py:798
  91.5 0.0 collective-permute-start.7
  91.5 3.8 %collective-permute-start.8 = (bf16[6,32,512]{2,1,0:T(8,128)(2,1)}, bf16[6,32,512]{2,1,0:T(8,128)(2,1)S(1)}, u32[]{:S(2)}, u32[]{:S(2)}) collective-permute-start(bf16[6,32,512]{2,1,0:T(8,128)(2,1)} %get-tuple-element.31), channel_id=1, source_target_pairs={{0,6},{1,7},{2,0},{3,1},{4,2},{5,3},{6,4},{7,5},{8,14},{9,15},{10,... | collective-permute-start | bytes 589832 | tf_op jit(solution)/shard_map/ppermute | solution.py:798
  95.3 10.9 %collective-permute-done.4.refs_1_ = bf16[6,32,512]{2,1,0:T(8,128)(2,1)S(1)} collective-permute-done((bf16[6,32,512]{2,1,0:T(8,128)(2,1)}, bf16[6,32,512]{2,1,0:T(8,128)(2,1)S(1)}, u32[]{:S(2)}, u32[]{:S(2)}) %collective-permute-start.4) | collective-permute-done | bytes 196640 | tf_op jit(solution)/shard_map/ppermute | solution.py:798
  106.2 0.0 collective-permute-start.9
  106.2 2.2 %collective-permute-done.5.refs_2_ = bf16[6,32,512]{2,1,0:T(8,128)(2,1)S(1)} collective-permute-done((bf16[6,32,512]{2,1,0:T(8,128)(2,1)}, bf16[6,32,512]{2,1,0:T(8,128)(2,1)S(1)}, u32[]{:S(2)}, u32[]{:S(2)}) %collective-permute-start.5) | collective-permute-done | bytes 196640 | tf_op jit(solution)/shard_map/ppermute | solution.py:798
  108.5 1.3 collective-permute-start.10
  109.8 19.5 %flow.1 = bf16[3,192,32,128]{3,2,1,0:T(8,128)(2,1)} custom-call(bf16[3,192,32,128]{3,2,1,0:T(8,128)(2,1)} %u_hbm.1, bf16[192,32,128]{2,1,0:T(8,128)(2,1)} %p_hbm.1, s32[192,32,128]{2,1,0:T(8,128)} %s_hbm.1, bf16[2,192,32,128]{3,2,1,0:T(8,128)(2,1)} %get-tuple-element.17.cn_hbm, bf16[7,32,128]{2,1,0:T(8,128)(2,1)} %copy-done.3, ...), custom_call_target="tpu_custom_call" | custom-call | flops 62914560 | bytes 15728640 | tf_op jit(solution)/shard_map/flow/pallas_call | solution.py:747
  129.3 0.9 shard_map.88.refs_2_
  130.2 0.0 all-to-all-done
  130.2 0.0 copy-start
  130.2 0.9 shard_map.89.refs_9_
  131.2 0.0 collective-permute-done.6.refs_3_
  131.2 0.0 collective-permute-done.7.refs_4_
  131.2 0.0 collective-permute-done.8.refs_5_
  131.2 0.0 collective-permute-done.9.refs_6_
  131.2 0.0 collective-permute-done.10.refs_7_
  131.2 0.1 copy-done
  131.3 1.3 shard_map.90
Async XLA Ops:
  11.3 27.3 %all-to-all-start.1 = ((bf16[8,6,16,512]{3,2,1,0:T(8,128)(2,1)}), bf16[8,6,16,512]{3,2,1,0:T(8,128)(2,1)S(1)}, u32[]{:S(2)}, u32[]{:S(2)}) async-start(bf16[8,6,16,512]{3,2,1,0:T(8,128)(2,1)} %bitcast.9), calls=%async_computation.1 | async-start | bytes 1572864 | tf_op jit(solution)/shard_map/all_to_all | solution.py:792
  17.7 5.4 %collective-permute-start = (bf16[7,32,128]{2,1,0:T(8,128)(2,1)}, bf16[7,32,128]{2,1,0:T(8,128)(2,1)S(1)}, u32[]{:S(2)}, u32[]{:S(2)}) collective-permute-start(bf16[7,32,128]{2,1,0:T(8,128)(2,1)} %get-tuple-element.20), channel_id=1, source_target_pairs={{0,8},{8,16},{16,24},{24,0},{1,9},{9,17},{17,25},{25,1},{2,10},{10... | collective-permute-start | bytes 172040 | tf_op jit(solution)/shard_map/ppermute | solution.py:114
  19.1 5.2 %collective-permute-start.1 = (bf16[7,32,128]{2,1,0:T(8,128)(2,1)}, bf16[7,32,128]{2,1,0:T(8,128)(2,1)S(1)}, u32[]{:S(2)}, u32[]{:S(2)}) collective-permute-start(bf16[7,32,128]{2,1,0:T(8,128)(2,1)} %get-tuple-element.21), channel_id=1, source_target_pairs={{8,0},{16,8},{24,16},{0,24},{9,1},{17,9},{25,17},{1,25},{10,2},{18... | collective-permute-start | bytes 172040 | tf_op jit(solution)/shard_map/ppermute | solution.py:114
  23.1 1.3 copy-start.3
  24.4 0.6 copy-start.4
  38.6 91.6 %all-to-all-start = ((bf16[8,6,16,512]{3,2,1,0:T(8,128)(2,1)}), bf16[8,6,16,512]{3,2,1,0:T(8,128)(2,1)S(1)}, u32[]{:S(2)}, u32[]{:S(2)}) async-start(bf16[8,6,16,512]{3,2,1,0:T(8,128)(2,1)} %bitcast.8), calls=%async_computation | async-start | bytes 1572864 | tf_op jit(solution)/shard_map/all_to_all | solution.py:792
  46.8 19.8 %collective-permute-start.2 = (bf16[7,192,128]{2,1,0:T(8,128)(2,1)}, bf16[7,192,128]{2,1,0:T(8,128)(2,1)S(1)}, u32[]{:S(2)}, u32[]{:S(2)}) collective-permute-start(bf16[7,192,128]{2,1,0:T(8,128)(2,1)} %get-tuple-element.22), channel_id=1, source_target_pairs={{0,1},{1,2},{2,3},{3,4},{4,5},{5,6},{6,7},{7,0},{8,9},{9,10},{10,1... | collective-permute-start | bytes 1032200 | tf_op jit(solution)/shard_map/ppermute | solution.py:114
  47.3 19.3 %collective-permute-start.3 = (bf16[7,192,128]{2,1,0:T(8,128)(2,1)}, bf16[7,192,128]{2,1,0:T(8,128)(2,1)S(1)}, u32[]{:S(2)}, u32[]{:S(2)}) collective-permute-start(bf16[7,192,128]{2,1,0:T(8,128)(2,1)} %get-tuple-element.23), channel_id=1, source_target_pairs={{1,0},{2,1},{3,2},{4,3},{5,4},{6,5},{7,6},{0,7},{9,8},{10,9},{11,1... | collective-permute-start | bytes 1032200 | tf_op jit(solution)/shard_map/ppermute | solution.py:114
  66.6 0.8 copy-start.1
  66.6 0.8 copy-start.2
  84.6 21.7 %collective-permute-start.4 = (bf16[6,32,512]{2,1,0:T(8,128)(2,1)}, bf16[6,32,512]{2,1,0:T(8,128)(2,1)S(1)}, u32[]{:S(2)}, u32[]{:S(2)}) collective-permute-start(bf16[6,32,512]{2,1,0:T(8,128)(2,1)} %get-tuple-element.27), channel_id=1, source_target_pairs={{0,4},{1,5},{2,6},{3,7},{4,0},{5,1},{6,2},{7,3},{8,12},{9,13},{10,... | collective-permute-start | bytes 589832 | tf_op jit(solution)/shard_map/ppermute | solution.py:798
  88.8 19.7 %collective-permute-start.5 = (bf16[6,32,512]{2,1,0:T(8,128)(2,1)}, bf16[6,32,512]{2,1,0:T(8,128)(2,1)S(1)}, u32[]{:S(2)}, u32[]{:S(2)}) collective-permute-start(bf16[6,32,512]{2,1,0:T(8,128)(2,1)} %get-tuple-element.28), channel_id=1, source_target_pairs={{0,3},{1,4},{2,5},{3,6},{4,7},{5,0},{6,1},{7,2},{8,11},{9,12},{10,... | collective-permute-start | bytes 589832 | tf_op jit(solution)/shard_map/ppermute | solution.py:798
  88.8 42.3 %collective-permute-start.6 = (bf16[6,32,512]{2,1,0:T(8,128)(2,1)}, bf16[6,32,512]{2,1,0:T(8,128)(2,1)S(1)}, u32[]{:S(2)}, u32[]{:S(2)}) collective-permute-start(bf16[6,32,512]{2,1,0:T(8,128)(2,1)} %get-tuple-element.29), channel_id=1, source_target_pairs={{0,5},{1,6},{2,7},{3,0},{4,1},{5,2},{6,3},{7,4},{8,13},{9,14},{10,... | collective-permute-start | bytes 589832 | tf_op jit(solution)/shard_map/ppermute | solution.py:798
  91.5 39.7 %collective-permute-start.7 = (bf16[6,32,512]{2,1,0:T(8,128)(2,1)}, bf16[6,32,512]{2,1,0:T(8,128)(2,1)S(1)}, u32[]{:S(2)}, u32[]{:S(2)}) collective-permute-start(bf16[6,32,512]{2,1,0:T(8,128)(2,1)} %get-tuple-element.30), channel_id=1, source_target_pairs={{0,2},{1,3},{2,4},{3,5},{4,6},{5,7},{6,0},{7,1},{8,10},{9,11},{10,... | collective-permute-start | bytes 589832 | tf_op jit(solution)/shard_map/ppermute | solution.py:798
  91.5 39.7 %collective-permute-start.8 = (bf16[6,32,512]{2,1,0:T(8,128)(2,1)}, bf16[6,32,512]{2,1,0:T(8,128)(2,1)S(1)}, u32[]{:S(2)}, u32[]{:S(2)}) collective-permute-start(bf16[6,32,512]{2,1,0:T(8,128)(2,1)} %get-tuple-element.31), channel_id=1, source_target_pairs={{0,6},{1,7},{2,0},{3,1},{4,2},{5,3},{6,4},{7,5},{8,14},{9,15},{10,... | collective-permute-start | bytes 589832 | tf_op jit(solution)/shard_map/ppermute | solution.py:798
  106.2 25.0 %collective-permute-start.9 = (bf16[6,32,512]{2,1,0:T(8,128)(2,1)}, bf16[6,32,512]{2,1,0:T(8,128)(2,1)S(1)}, u32[]{:S(2)}, u32[]{:S(2)}) collective-permute-start(bf16[6,32,512]{2,1,0:T(8,128)(2,1)} %get-tuple-element.32), channel_id=1, source_target_pairs={{0,1},{1,2},{2,3},{3,4},{4,5},{5,6},{6,7},{7,0},{8,9},{9,10},{10,1... | collective-permute-start | bytes 589832 | tf_op jit(solution)/shard_map/ppermute | solution.py:798
  108.5 22.7 %collective-permute-start.10 = (bf16[6,32,512]{2,1,0:T(8,128)(2,1)}, bf16[6,32,512]{2,1,0:T(8,128)(2,1)S(1)}, u32[]{:S(2)}, u32[]{:S(2)}) collective-permute-start(bf16[6,32,512]{2,1,0:T(8,128)(2,1)} %get-tuple-element.33), channel_id=1, source_target_pairs={{0,7},{1,0},{2,1},{3,2},{4,3},{5,4},{6,5},{7,6},{8,15},{9,8},{10,9... | collective-permute-start | bytes 589832 | tf_op jit(solution)/shard_map/ppermute | solution.py:798
  130.2 1.1 copy-start

commit v3 on v2

--- a/solution.py
+++ b/solution.py
@@ -11,6 +11,7 @@
 BLK = 32
 TOP = 8
 ROWS = 48
+AHEAD = 2
 
 ion_step = 0.04
 flow_step = 0.1
@@ -33,80 +34,10 @@
     return forward, backward
 
 
-def edge_kernel(*refs):
-    c_hbm, p_hbm, d_hbm, s_hbm, u_hbm, first, last = refs[:7]
-    c_y, p_y, d_y, s_y, u_y, tmp, tmp_s, y_sem = refs[7:]
-    nx, ny, nz = p_hbm.shape
-    cuts = y_sem.shape[2]
-    step = nx // cuts
-
-    def rows(n, i):
-        part = pl.ds(i * step, step)
-        row = pl.ds(0 if n == 0 else ny - TOP, TOP)
-        copies = []
-        pairs = zip((c_hbm, p_hbm, d_hbm, s_hbm, u_hbm), (c_y, p_y, d_y, s_y, u_y))
-        for j, (src, dst) in enumerate(pairs):
-            if len(src.shape) == 4:
-                pair = src.at[:, part, row], dst.at[n, :, part]
-            else:
-                pair = src.at[part, row], dst.at[n, part]
-            copies.append(pltpu.make_async_copy(*pair, y_sem.at[n, j, i]))
-        return copies
-
-    for i in range(cuts):
-        for n in range(2):
-            for copy in rows(n, i):
-                copy.start()
-    size = 16
-    for i in range(cuts):
-        for n, out in enumerate((first, last)):
-            for copy in rows(n, i):
-                copy.wait()
-            row = 0 if n == 0 else TOP - 1
-
-            @pl.loop(0, step // size)
-            def _(q, i=i, n=n, out=out, row=row):
-                at = pl.ds(pl.multiple_of(i * step + q * size, size), size)
-                picked = pl.ds(row, size, stride=TOP)
-                tmp_s[...] = s_y[n, at].reshape(size * TOP, nz)
-                solid = tmp_s[picked, :] > 0
-                loaded = [c_y[n, 0, at], c_y[n, 1, at], p_y[n, at], d_y[n, at]]
-                loaded += [u_y[n, f, at] for f in range(3)]
-                for f, v in enumerate(loaded):
-                    tmp[f] = v.astype(F32).reshape(size * TOP, nz)
-                for f in range(7):
-                    v = tmp[f, picked, :]
-                    if f > 2:
-                        v = jnp.where(solid, v, 0.0)
-                    out[f, at, :] = v.astype(BF16)
-
-
 def field_scratch(shape):
     leads = ((2, 2), (2,), (2,), (2,), (2, 3))
     kinds = (BF16, BF16, BF16, jnp.int32, BF16)
     return [pltpu.VMEM(lead + shape, kind) for lead, kind in zip(leads, kinds)]
-
-
-def edge_call(c, p, d, s, u):
-    nx, _, nz = p.shape
-    cuts = 4
-    return pl.pallas_call(
-        edge_kernel,
-        name="edges",
-        out_shape=(jax.ShapeDtypeStruct((7, nx, nz), BF16),) * 2,
-        in_specs=[HBM] * 5,
-        out_specs=(VMEM,) * 2,
-        scratch_shapes=field_scratch((nx, TOP, nz))
-        + [
-            pltpu.VMEM((7, 16 * TOP, nz), F32),
-            pltpu.VMEM((16 * TOP, nz), jnp.int32),
-            pltpu.SemaphoreType.DMA((2, 5, cuts)),
-        ],
-        compiler_params=PARAMS,
-        cost_estimate=pl.CostEstimate(
-            flops=20 * nx * nz, bytes_accessed=200 * nx * nz, transcendentals=0
-        ),
-    )(c, p, d, s, u)
 
 
 def swap_ends(first, last, axis):
@@ -138,7 +69,7 @@
         return taken
 
     plan, me, c_hbm, p_hbm, d_hbm, s_hbm = take(6)
-    nx, _, nz = p_hbm.shape
+    nx, ny, nz = p_hbm.shape
     chunks = nx // BLK
     bz = nz // BLK
     count = chunks * bz
@@ -148,8 +79,11 @@
     cn_hbm = take(1)[0]
     outs = take(spread)
     ends = take(2 if inner else 0)
+    rims = take(2 if inner else 0)
     c_v, p_v, d_v, s_v = take(4)
     raw = take(5 if inner else 0)
+    rim_v = take(5 if inner else 0)
+    tmp, tmp_s, rim_sem = take(3) if inner else (None, None, None)
     edges_v = take(len(edges_hbm))
     edges_f = take(2 if outer else 0)
     fld, cn_v, chs, blk, zero, perm, lanes, shift, shift2, dpot = take(10)
@@ -181,9 +115,49 @@
     else:
         for copy in halos:
             copy.start()
-    for i in range(chunks):
+    sources = (c_hbm, p_hbm, d_hbm, s_hbm, u_hbm)
+
+    def rim_loads(i):
+        part = pl.ds(i * BLK, BLK)
+        copies = []
+        for n in range(2):
+            row = pl.ds(n * (ny - TOP), TOP)
+            for j, (src, dst) in enumerate(zip(sources, rim_v)):
+                if len(src.shape) == 4:
+                    pair = src.at[:, part, row], dst.at[n, :, part]
+                else:
+                    pair = src.at[part, row], dst.at[n, part]
+                copies.append(pltpu.make_async_copy(*pair, rim_sem.at[n, j, i]))
+        return copies
+
+    def rim(i, n, half_block):
+        number = BLK // 2
+        at = pl.ds(pl.multiple_of(i * BLK + half_block * number, number), number)
+        picked = pl.ds(n * (TOP - 1), number, stride=TOP)
+        spot = 2 * n + half_block
+        c_y, p_y, d_y, s_y, u_y = rim_v
+        tmp_s[spot] = s_y[n, at].reshape(number * TOP, nz)
+        solid = tmp_s[spot, picked, :] > 0
+        loaded = [c_y[n, 0, at], c_y[n, 1, at], p_y[n, at], d_y[n, at]]
+        loaded += [u_y[n, f, at] for f in range(3)]
+        for f, v in enumerate(loaded):
+            tmp[spot, f] = v.astype(F32).reshape(number * TOP, nz)
+        for f in range(7):
+            v = tmp[spot, f, picked, :]
+            if f > 2:
+                v = jnp.where(solid, v, 0.0)
+            rims[n][f, at, :] = v.astype(BF16)
+
+    def fetch(i):
         for copy in loads(i):
             copy.start()
+        if inner:
+            for copy in rim_loads(i):
+                copy.start()
+
+    ahead = chunks if inner else min(AHEAD, chunks)
+    for i in range(ahead):
+        fetch(i)
     if inner:
         for copy in halos:
             copy.start()
@@ -310,61 +284,78 @@
 
     batch = TOP
 
-    def planes(x, number, row, tall):
-        return [fld[f, pl.ds(x + 1, number), pl.ds(TOP + row, tall), :] for f in range(4)]
-
-    def update(x, row, tall):
-        mid = planes(x, batch, row, tall)
-        c0, c1, pot, s = mid
+    strips = ((0, TOP), (m1, TOP)) if outer else ((m0, m1 - m0),)
+    tall = sum(number for _, number in strips)
+
+    def planes(x, number, off=0):
+        return [
+            jnp.concatenate(
+                [
+                    fld[f, pl.ds(x + 1, number), pl.ds(TOP + row + off, rows), :]
+                    for row, rows in strips
+                ],
+                axis=1,
+            )
+            for f in range(4)
+        ]
+
+    def update(x):
         m = batch * tall
-
-        def flat(v):
-            return v.reshape(m, nz)
-
+        c0, c1, pot, s = [v.reshape(m, nz) for v in planes(x, batch)]
         high = s.astype(BF16)
         low = (s - high.astype(F32)).astype(BF16)
-        both = jnp.concatenate([flat(c0), flat(c1)], axis=0).astype(BF16)
-        zc = jnp.dot(both, shift[...], preferred_element_type=F32)
-        zs = jnp.dot(
-            jnp.concatenate([flat(high), flat(low)], axis=1),
-            shift2[...],
+        zc = jnp.dot(
+            jnp.concatenate([c0, c1], axis=0).astype(BF16),
+            shift[...],
             preferred_element_type=F32,
         )
-        zp = jnp.dot(flat(pot).astype(BF16), dpot[...], preferred_element_type=F32)
-        lows = planes(x - 1, batch + 1, row, tall)
-        highs = planes(x, batch + 1, row, tall)
-        fx = face(lows, highs)
-        total = [fx[sp][1:] - fx[sp][:batch] for sp in range(2)]
-        sides = []
-        for off in (-1, 1):
-            n0, n1, npot, ns = planes(x, batch, row + off, tall)
-            sides.append((n0, n1, npot - pot, ns))
-        for part in (slice(0, nz), slice(nz, 2 * nz)):
-            parts = (zc[:m, part], zc[m:, part], zp[:, part], zs[:, part])
-            sides.append(tuple(v.reshape(batch, tall, nz) for v in parts))
-        sum_a = sum_b = None
-        for n0, n1, dp, ns in sides:
-            f = s * ns
-            h = f * dp
-            a = f + h
-            b = f - h
-            total[0] = total[0] + n0 * a
-            total[1] = total[1] + n1 * b
-            sum_a = a if sum_a is None else sum_a + a
-            sum_b = b if sum_b is None else sum_b + b
-        total[0] = total[0] - c0 * sum_b
-        total[1] = total[1] - c1 * sum_a
-        new = []
-        for sp in range(2):
-            value = mid[sp] + (ion_step * species_diff[sp]) * total[sp]
-            new.append(value.astype(BF16))
-            cn_v[sp, pl.ds(x, batch), pl.ds(row, tall), :] = new[sp]
-        return (new[0].astype(F32) - new[1].astype(F32)).astype(BF16)
-
-    def keep(group, offset, charge):
-        m = charge.shape[0] * charge.shape[1]
-        at = pl.multiple_of(offset, m) if not isinstance(offset, int) else offset
-        chs[group, pl.ds(at, m), :] = charge.reshape(m, nz)
+        zs = jnp.dot(
+            jnp.concatenate([high, low], axis=1), shift2[...], preferred_element_type=F32
+        )
+        zp = jnp.dot(pot.astype(BF16), dpot[...], preferred_element_type=F32)
+
+        def plane(j, off=0):
+            return [v[0] for v in planes(x + j, 1, off)]
+
+        mid = plane(0)
+        below = face(plane(-1), mid)
+        charges = []
+        for j in range(batch):
+            after = plane(j + 1)
+            above = face(mid, after)
+            total = [above[sp] - below[sp] for sp in range(2)]
+            c0, c1, pot, s = mid
+            sides = []
+            for off in (-1, 1):
+                n0, n1, npot, ns = plane(j, off)
+                sides.append((n0, n1, npot - pot, ns))
+            own = slice(j * tall, (j + 1) * tall)
+            again = slice(m + j * tall, m + (j + 1) * tall)
+            for part in (slice(0, nz), slice(nz, 2 * nz)):
+                sides.append((zc[own, part], zc[again, part], zp[own, part], zs[own, part]))
+            sum_a = sum_b = None
+            for n0, n1, dp, ns in sides:
+                f = s * ns
+                h = f * dp
+                a = f + h
+                b = f - h
+                total[0] = total[0] + n0 * a
+                total[1] = total[1] + n1 * b
+                sum_a = a if sum_a is None else sum_a + a
+                sum_b = b if sum_b is None else sum_b + b
+            total[0] = total[0] - c0 * sum_b
+            total[1] = total[1] - c1 * sum_a
+            new = []
+            for sp in range(2):
+                value = mid[sp] + (ion_step * species_diff[sp]) * total[sp]
+                new.append(value.astype(BF16))
+                at = 0
+                for row, rows in strips:
+                    cn_v[sp, x + j, pl.ds(row, rows), :] = new[sp][at : at + rows]
+                    at += rows
+            charges.append((new[0].astype(F32) - new[1].astype(F32)).astype(BF16)[None])
+            mid, below = after, above
+        return jnp.concatenate(charges, axis=0)
 
     def saves(i):
         x = i * BLK
@@ -380,7 +371,7 @@
         return copies
 
     def put(b, n=0):
-        return pltpu.make_async_copy(blk.at[b], outs[n].at[tally[b]], blk_sem.at[b])
+        return pltpu.make_async_copy(blk.at[b + bz], outs[n].at[tally[b]], blk_sem.at[b])
 
     def send(b):
         if spread == 1:
@@ -402,42 +393,10 @@
             for j in range(groups)
         ]
 
-    prepare(0)
-
-    @pl.loop(0, chunks)
-    def _(i):
-        @pl.when(i + 1 < chunks)
-        def _():
-            prepare(i + 1)
-
-        x = i * BLK
-        middle = half * TOP
-        if inner:
-
-            @pl.loop(0, (m1 - m0) // batch)
-            def _(q):
-                charge = update(x + m0 + q * batch, m0, m1 - m0)
-                for t in range(2):
-                    keep(0, t * middle + q * batch * TOP, charge[:, t * TOP : (t + 1) * TOP])
-
-        if mid:
-
-            @pl.loop(0, 2)
-            def _(q):
-                charge = update(x + q * m1, m0, m1 - m0)
-                for t in range(2):
-                    keep(0, t * middle + q * batch * TOP, charge[:, t * TOP : (t + 1) * TOP])
-
-        if outer:
-
-            @pl.loop(0, BLK // batch)
-            def _(q):
-                for t, row in enumerate((0, m1)):
-                    keep(t, q * batch * TOP, update(x + q * batch, row, TOP))
-
-        for copy in saves(i):
-            copy.start()
-        size = BLK if outer else half
+    offsets = {"inner": (m0, m0 + batch), "mid": (0, m1), "outer": range(0, BLK, batch)}[mode]
+    size = BLK if outer else half
+
+    def relayout(i):
         rowsets = []
         for t in range(2 if outer else 1):
             v = jnp.dot(perm[0], chs[t], preferred_element_type=F32).astype(BF16)
@@ -447,10 +406,51 @@
         ).astype(BF16)
         for k in range(bz):
             for j in range(len(rowsets)):
-                blk[i * bz + k, :, j * nz : (j + 1) * nz] = res[
+                blk[(i + 1) * bz + k, :, j * nz : (j + 1) * nz] = res[
                     j * size : (j + 1) * size, k * nz : (k + 1) * nz
                 ]
-            send(i * bz + k)
+
+    prepare(0)
+
+    @pl.loop(0, chunks)
+    def _(i):
+        @pl.when(i + ahead < chunks)
+        def _():
+            fetch(i + ahead)
+
+        @pl.when(i + 1 < chunks)
+        def _():
+            prepare(i + 1)
+
+        if inner:
+            for copy in rim_loads(i):
+                copy.wait()
+        relayout(i - 1)
+        if inner:
+            for n in range(2):
+                for half_block in range(2):
+                    rim(i, n, half_block)
+        for q, offset in enumerate(offsets):
+            charge = update(i * BLK + offset)
+            m = batch * TOP
+            for t in range(2):
+                strip = charge[:, t * TOP : (t + 1) * TOP].reshape(m, nz)
+                if outer:
+                    chs[t, q * m : (q + 1) * m, :] = strip
+                else:
+                    at = t * half * TOP + q * m
+                    chs[0, at : at + m, :] = strip
+        for copy in saves(i):
+            copy.start()
+
+        @pl.when(i > 0)
+        def _():
+            for k in range(bz):
+                send((i - 1) * bz + k)
+
+    relayout(chunks - 1)
+    for k in range(bz):
+        send((chunks - 1) * bz + k)
 
     if inner:
         for copy in halos:
@@ -489,17 +489,22 @@
     spread = tiles if outer else 1
     vm = pltpu.VMEM
     dma = pltpu.SemaphoreType.DMA
-    extra = field_scratch((ny, nz)) if inner else [vm((4, ny, nz), BF16)] * 2
+    extra = [vm((4, ny, nz), BF16)] * 2
+    if inner:
+        extra = field_scratch((ny, nz)) + field_scratch((nx, TOP, nz))
+        extra += [vm((4, 7, BLK // 2 * TOP, nz), F32), vm((4, BLK // 2 * TOP, nz), jnp.int32)]
+        extra.append(dma((2, 5, chunks)))
     if outer:
         extra += [vm((4, nx, nz), BF16)] * 2 + [vm((4, nx, nz), F32)] * 2
     share = 0.5 if outer else 0.25
     part = jax.ShapeDtypeStruct((tiles * capacity // spread, deep, wide), BF16)
-    end = jax.ShapeDtypeStruct((7, ny, nz), BF16)
+    ends = [jax.ShapeDtypeStruct((7, number, nz), BF16) for number in (ny, ny, nx, nx)]
+    ends = ends if inner else []
     return pl.pallas_call(
         functools.partial(ion_kernel, capacity, mode, spread),
-        out_shape=[jax.ShapeDtypeStruct(c.shape, BF16)] + [part] * spread + [end] * (2 * inner),
+        out_shape=[jax.ShapeDtypeStruct(c.shape, BF16)] + [part] * spread + ends,
         in_specs=[SMEM] * 2 + [HBM] * (len(args) - 2),
-        out_specs=[HBM] * (1 + spread) + [VMEM] * (2 * inner),
+        out_specs=[HBM] * (1 + spread) + [VMEM] * len(ends),
         scratch_shapes=[
             vm(c.shape, BF16),
             vm(p.shape, BF16),
@@ -511,7 +516,7 @@
             vm((4, nx + 2, ROWS, nz), F32),
             vm(c.shape, BF16),
             vm((2 if outer else 1, BLK * TOP, nz), BF16),
-            vm((count, deep, wide), BF16),
+            vm((count + bz, deep, wide), BF16),
             vm((deep, wide), BF16),
             vm((1, BLK * TOP, BLK * TOP), BF16),
             vm((bz * nz, bz * nz), BF16),
@@ -526,7 +531,7 @@
             dma((tiles * capacity,)),
         ],
         input_output_aliases={} if inner else {len(args) - 1: 0},
-        compiler_params=PARAMS,
+        compiler_params=pltpu.CompilerParams(vmem_limit_bytes=60 * 2**20),
         cost_estimate=pl.CostEstimate(
             flops=int(100 * p.size * share),
             bytes_accessed=int(60 * p.size * share),
@@ -646,7 +651,7 @@
     ]
     for copy in halos:
         copy.start()
-    for i in range(chunks):
+    for i in range(min(AHEAD, chunks)):
         for copy in loads(i):
             copy.start()
     for copy in halos:
@@ -727,6 +732,11 @@
 
     @pl.loop(0, chunks)
     def _(i):
+        @pl.when(i + AHEAD < chunks)
+        def _():
+            for copy in loads(i + AHEAD):
+                copy.start()
+
         @pl.when(i + 1 < chunks)
         def _():
             prepare(i + 1)
@@ -798,11 +808,10 @@
         return lax.ppermute(piece, "tile", [(i, (i + shift) % tiles) for i in range(tiles)])
 
     given = (balance_plan[:, 0], me, concentration, potential, diffusivity, spacer, velocity)
-    conc, first, x_first, x_last = ion_call("inner", *given, None, None, capacity, tiles)
+    conc, first, *ends = ion_call("inner", *given, None, None, capacity, tiles)
     first = exchange(first)
-    x_halo = swap_ends(x_first, x_last, "stream")
-    y_first, y_last = edge_call(*given[2:])
-    y_halo = swap_ends(y_first, y_last, "tile")
+    x_halo = swap_ends(*ends[:2], "stream")
+    y_halo = swap_ends(*ends[2:], "tile")
     conc, second = ion_call("mid", *given, x_halo, conc, capacity, tiles)
     second = exchange(second)
     halo = x_halo + y_halo

time: 133 us -> 128 us (0.962)
  Pallas kernels: 67.3 us -> 56.4 us
  waiting for transfers between devices: 34.4 us -> 40.5 us
    pallas_call x1 -> x0, Pallas kernels: 4.66 us -> none  [edge_call(): pl.pallas_call(edge_kernel, name='edges', out_shape=(jax.ShapeDtypeStruct...]
    ppermute x2, waiting for transfers between devices: 18.7 us -> 23.4 us  [swap_ends(): lax.ppermute(last, axis, forward)]
    pallas_call x3, Pallas kernels: 40.1 us -> 36.4 us  [ion_call(): pl.pallas_call(functools.partial(ion_kernel, capacity, mode, spread), out...]
    pallas_call x1, Pallas kernels: 19.5 us -> 17 us  [flow_call(): pl.pallas_call(flow_kernel, name='flow', out_shape=jax.ShapeDtypeStruct(u...]
  transfers between devices with their start and end apart: 13 -> 13, of which waited for: 6 -> 6; matrix products, arithmetic and copies ran while one was open for 0% -> 0% of each run, Pallas kernels for 42% -> 34%
where the time goes in v3:
time: 128 us
  Pallas kernels  56.4 us (44%)
  waiting for transfers between devices  40.5 us (32%)
  starting transfers between devices  28.3 us (22%)
  local copies, waits for them, and re-layouts  1.59 us (1%)
    pallas_call x3, Pallas kernels, ion_call(): pl.pallas_call(functools.partial(ion_kernel, capacity, mode, spread), out...  36.4 us
    ppermute x2, waiting for transfers between devices, swap_ends(): lax.ppermute(last, axis, forward)  23.4 us
    pallas_call x1, Pallas kernels, flow_call(): pl.pallas_call(flow_kernel, name='flow', out_shape=jax.ShapeDtypeStruct(u...  17 us
    ppermute x7, waiting for transfers between devices, pass_on(): lax.ppermute(piece, 'tile', [(i, (i + shift) % tiles) for i in range(tile...  13.3 us
    ppermute x7, starting transfers between devices, pass_on(): lax.ppermute(piece, 'tile', [(i, (i + shift) % tiles) for i in range(tile...  11.8 us
    all_to_all x2, starting transfers between devices, exchange(): part = lax.all_to_all(part, 'tile', split_axis=0, concat_axis=0, tiled=True)  9.93 us
    ppermute x2, starting transfers between devices, swap_ends(): lax.ppermute(first, axis, backward)  4.65 us
    pallas_call x3, Pallas kernels, gather_call(): pl.pallas_call(functools.partial(gather_kernel, boxes, capacity, shifts,...  3.06 us
  transfers between devices with their start and end apart: 13, of which 6 were waited for; matrix products, arithmetic and copies ran while one was open for 0% of the time, Pallas kernels for 34%

profile of v3, /device:TPU:0, one launch (start us, length us, event | category | flops | bytes accessed | tf_op | source)
XLA Modules:
  0.0 127.5 jit_solution(2604040688551131892)
XLA Ops:
  0.6 11.8 %shard_map.85 = (bf16[2,192,32,128]{3,2,1,0:T(8,128)(2,1)}, bf16[48,16,512]{2,1,0:T(8,128)(2,1)}, bf16[7,32,128]{2,1,0:T(8,128)(2,1)}, bf16[7,32,128]{2,1,0:T(8,...) custom-call(s32[24]{0:T(128)} %bitcast.10, s32[1]{0:T(128)} %bitcast.1.refs_1_.refs_0_, ...), custom_call_target="tpu_custom_call" | custom-call | flops 19660800 | bytes 11796480 | tf_op jit(solution)/shard_map/pallas_call | solution.py:503
  12.5 6.4 %all-to-all-start.1 = ((bf16[8,6,16,512]{3,2,1,0:T(8,128)(2,1)}), bf16[8,6,16,512]{3,2,1,0:T(8,128)(2,1)S(1)}, u32[]{:S(2)}, u32[]{:S(2)}) async-start(bf16[8,6,16,512]{3,2,1,0:T(8,128)(2,1)} %bitcast.9), calls=%async_computation.1 | async-start | bytes 1572864 | tf_op jit(solution)/shard_map/all_to_all | solution.py:802
  18.9 1.5 %collective-permute-start = (bf16[7,32,128]{2,1,0:T(8,128)(2,1)}, bf16[7,32,128]{2,1,0:T(8,128)(2,1)S(1)}, u32[]{:S(2)}, u32[]{:S(2)}) collective-permute-start(bf16[7,32,128]{2,1,0:T(8,128)(2,1)} %get-tuple-element.20), channel_id=1, source_target_pairs={{0,8},{8,16},{16,24},{24,0},{1,9},{9,17},{17,25},{25,1},{2,10},{10... | collective-permute-start | bytes 172040 | tf_op jit(solution)/shard_map/ppermute | solution.py:45
  20.3 1.4 %collective-permute-start.1 = (bf16[7,32,128]{2,1,0:T(8,128)(2,1)}, bf16[7,32,128]{2,1,0:T(8,128)(2,1)S(1)}, u32[]{:S(2)}, u32[]{:S(2)}) collective-permute-start(bf16[7,32,128]{2,1,0:T(8,128)(2,1)} %get-tuple-element.21), channel_id=1, source_target_pairs={{8,0},{16,8},{24,16},{0,24},{9,1},{17,9},{25,17},{1,25},{10,2},{18... | collective-permute-start | bytes 172040 | tf_op jit(solution)/shard_map/ppermute | solution.py:45
  21.8 2.5 %collective-permute-done.refs_6_.xl_hbm = bf16[7,32,128]{2,1,0:T(8,128)(2,1)S(1)} collective-permute-done((bf16[7,32,128]{2,1,0:T(8,128)(2,1)}, bf16[7,32,128]{2,1,0:T(8,128)(2,1)S(1)}, u32[]{:S(2)}, u32[]{:S(2)}) %collective-permute-start) | collective-permute-done | bytes 57376 | tf_op jit(solution)/shard_map/ppermute | solution.py:45
  24.3 0.0 copy-start.3
  24.3 1.3 collective-permute-done.1.refs_7_.xh_hbm
  25.6 0.0 copy-start.4
  25.6 0.0 copy-done.3
  25.6 0.6 copy-done.4
  26.2 0.0 copy-start.6
  26.2 0.0 copy-start.5
  26.2 11.1 %shard_map.86 = (bf16[2,192,32,128]{3,2,1,0:T(8,128)(2,1)}, bf16[48,16,512]{2,1,0:T(8,128)(2,1)}) custom-call(s32[24]{0:T(128)} %bitcast.11, s32[1]{0:T(128)} %bitcast.1.refs_1_.refs_0_, bf16[2,192,32,128]{3,2,1,0:T(8,128)(2,1)} %refs_2_.5, bf16[192,32,128]{2,1,0:T(8,128)(2,1)} %p_hbm.1, ...), custom_call_target="tpu_custom_call", output_to_operand_aliasing={{0}: (8, {})} | custom-call | flops 19660800 | bytes 11796480 | tf_op jit(solution)/shard_map/pallas_call | solution.py:503
  37.3 2.5 %all-to-all-done.1 = bf16[8,6,16,512]{3,2,1,0:T(8,128)(2,1)S(1)} async-done(((bf16[8,6,16,512]{3,2,1,0:T(8,128)(2,1)}), bf16[8,6,16,512]{3,2,1,0:T(8,128)(2,1)S(1)}, u32[]{:S(2)}, u32[]{:S(2)}) %all-to-all-start.1) | async-done | bytes 786464 | tf_op jit(solution)/shard_map/all_to_all | solution.py:802
  39.8 3.5 %all-to-all-start = ((bf16[8,6,16,512]{3,2,1,0:T(8,128)(2,1)}), bf16[8,6,16,512]{3,2,1,0:T(8,128)(2,1)S(1)}, u32[]{:S(2)}, u32[]{:S(2)}) async-start(bf16[8,6,16,512]{3,2,1,0:T(8,128)(2,1)} %bitcast.8), calls=%async_computation | async-start | bytes 1572864 | tf_op jit(solution)/shard_map/all_to_all | solution.py:802
  43.4 0.0 copy-done.6
  43.4 0.4 collective-permute-start.2
  43.8 0.0 copy-done.5
  43.8 3.2 %collective-permute-start.3 = (bf16[7,192,128]{2,1,0:T(8,128)(2,1)S(1)}, bf16[7,192,128]{2,1,0:T(8,128)(2,1)S(1)}, u32[]{:S(2)}, u32[]{:S(2)}) collective-permute-start(bf16[7,192,128]{2,1,0:T(8,128)(2,1)S(1)} %copy-done.5), channel_id=1, source_target_pairs={{1,0},{2,1},{3,2},{4,3},{5,4},{6,5},{7,6},{0,7},{9,8},{10,9},{11,1... | collective-permute-start | bytes 1032200 | tf_op jit(solution)/shard_map/ppermute | solution.py:45
  47.0 20.9 %collective-permute-done.2.refs_8_.yl_hbm = bf16[7,192,128]{2,1,0:T(8,128)(2,1)S(1)} collective-permute-done((bf16[7,192,128]{2,1,0:T(8,128)(2,1)S(1)}, bf16[7,192,128]{2,1,0:T(8,128)(2,1)S(1)}, u32[]{:S(2)}, u32[]{:S(2)}) %collective-permute-start.2) | collective-permute-done | bytes 344096 | tf_op jit(solution)/shard_map/ppermute | solution.py:45
  67.8 0.0 copy-start.1
  67.8 0.0 collective-permute-done.3.refs_9_.yh_hbm
  67.8 0.0 copy-start.2
  67.8 0.7 copy-done.1
  68.6 0.1 copy-done.2
  68.7 13.4 %shard_map.87 = (bf16[2,192,32,128]{3,2,1,0:T(8,128)(2,1)}, bf16[6,32,512]{2,1,0:T(8,128)(2,1)}, bf16[6,32,512]{2,1,0:T(8,128)(2,1)}, bf16[6,32,512]{2,1,0:T(8,1...) custom-call(s32[24]{0:T(128)} %bitcast.12, ...), custom_call_target="tpu_custom_call", output_to_operand_aliasing={{0}: (10, {})} | custom-call | flops 39321600 | bytes 23592960 | tf_op jit(solution)/shard_map/pallas_call | solution.py:503
  82.2 4.2 %collective-permute-start.4 = (bf16[6,32,512]{2,1,0:T(8,128)(2,1)}, bf16[6,32,512]{2,1,0:T(8,128)(2,1)S(1)}, u32[]{:S(2)}, u32[]{:S(2)}) collective-permute-start(bf16[6,32,512]{2,1,0:T(8,128)(2,1)} %get-tuple-element.27), channel_id=1, source_target_pairs={{0,4},{1,5},{2,6},{3,7},{4,0},{5,1},{6,2},{7,3},{8,12},{9,13},{10,... | collective-permute-start | bytes 589832 | tf_op jit(solution)/shard_map/ppermute | solution.py:808
  86.4 0.0 collective-permute-start.5
  86.4 2.6 %collective-permute-start.6 = (bf16[6,32,512]{2,1,0:T(8,128)(2,1)}, bf16[6,32,512]{2,1,0:T(8,128)(2,1)S(1)}, u32[]{:S(2)}, u32[]{:S(2)}) collective-permute-start(bf16[6,32,512]{2,1,0:T(8,128)(2,1)} %get-tuple-element.29), channel_id=1, source_target_pairs={{0,5},{1,6},{2,7},{3,0},{4,1},{5,2},{6,3},{7,4},{8,13},{9,14},{10,... | collective-permute-start | bytes 589832 | tf_op jit(solution)/shard_map/ppermute | solution.py:808
  89.0 0.0 collective-permute-start.7
  89.0 3.8 %collective-permute-start.8 = (bf16[6,32,512]{2,1,0:T(8,128)(2,1)}, bf16[6,32,512]{2,1,0:T(8,128)(2,1)S(1)}, u32[]{:S(2)}, u32[]{:S(2)}) collective-permute-start(bf16[6,32,512]{2,1,0:T(8,128)(2,1)} %get-tuple-element.31), channel_id=1, source_target_pairs={{0,6},{1,7},{2,0},{3,1},{4,2},{5,3},{6,4},{7,5},{8,14},{9,15},{10,... | collective-permute-start | bytes 589832 | tf_op jit(solution)/shard_map/ppermute | solution.py:808
  92.8 10.9 %collective-permute-done.4.refs_1_ = bf16[6,32,512]{2,1,0:T(8,128)(2,1)S(1)} collective-permute-done((bf16[6,32,512]{2,1,0:T(8,128)(2,1)}, bf16[6,32,512]{2,1,0:T(8,128)(2,1)S(1)}, u32[]{:S(2)}, u32[]{:S(2)}) %collective-permute-start.4) | collective-permute-done | bytes 196640 | tf_op jit(solution)/shard_map/ppermute | solution.py:808
  103.7 0.0 collective-permute-start.9
  103.7 2.4 %collective-permute-done.5.refs_2_ = bf16[6,32,512]{2,1,0:T(8,128)(2,1)S(1)} collective-permute-done((bf16[6,32,512]{2,1,0:T(8,128)(2,1)}, bf16[6,32,512]{2,1,0:T(8,128)(2,1)S(1)}, u32[]{:S(2)}, u32[]{:S(2)}) %collective-permute-start.5) | collective-permute-done | bytes 196640 | tf_op jit(solution)/shard_map/ppermute | solution.py:808
  106.1 1.2 collective-permute-start.10
  107.3 17.0 %flow.1 = bf16[3,192,32,128]{3,2,1,0:T(8,128)(2,1)} custom-call(bf16[3,192,32,128]{3,2,1,0:T(8,128)(2,1)} %u_hbm.1, bf16[192,32,128]{2,1,0:T(8,128)(2,1)} %p_hbm.1, s32[192,32,128]{2,1,0:T(8,128)} %s_hbm.1, bf16[2,192,32,128]{3,2,1,0:T(8,128)(2,1)} %get-tuple-element.17.cn_hbm, bf16[7,32,128]{2,1,0:T(8,128)(2,1)} %copy-done.3, ...), custom_call_target="tpu_custom_call" | custom-call | flops 62914560 | bytes 15728640 | tf_op jit(solution)/shard_map/flow/pallas_call | solution.py:757
  124.3 0.9 shard_map.88.refs_2_
  125.2 0.0 all-to-all-done
  125.2 0.0 copy-start
  125.2 0.9 shard_map.89.refs_9_
  126.1 0.0 collective-permute-done.6.refs_3_
  126.1 0.0 collective-permute-done.7.refs_4_
  126.1 0.0 collective-permute-done.8.refs_5_
  126.2 0.0 collective-permute-done.9.refs_6_
  126.2 0.0 collective-permute-done.10.refs_7_
  126.2 0.1 copy-done
  126.3 1.3 shard_map.90
Async XLA Ops:
  12.5 27.3 %all-to-all-start.1 = ((bf16[8,6,16,512]{3,2,1,0:T(8,128)(2,1)}), bf16[8,6,16,512]{3,2,1,0:T(8,128)(2,1)S(1)}, u32[]{:S(2)}, u32[]{:S(2)}) async-start(bf16[8,6,16,512]{3,2,1,0:T(8,128)(2,1)} %bitcast.9), calls=%async_computation.1 | async-start | bytes 1572864 | tf_op jit(solution)/shard_map/all_to_all | solution.py:802
  18.9 5.4 %collective-permute-start = (bf16[7,32,128]{2,1,0:T(8,128)(2,1)}, bf16[7,32,128]{2,1,0:T(8,128)(2,1)S(1)}, u32[]{:S(2)}, u32[]{:S(2)}) collective-permute-start(bf16[7,32,128]{2,1,0:T(8,128)(2,1)} %get-tuple-element.20), channel_id=1, source_target_pairs={{0,8},{8,16},{16,24},{24,0},{1,9},{9,17},{17,25},{25,1},{2,10},{10... | collective-permute-start | bytes 172040 | tf_op jit(solution)/shard_map/ppermute | solution.py:45
  20.3 5.2 %collective-permute-start.1 = (bf16[7,32,128]{2,1,0:T(8,128)(2,1)}, bf16[7,32,128]{2,1,0:T(8,128)(2,1)S(1)}, u32[]{:S(2)}, u32[]{:S(2)}) collective-permute-start(bf16[7,32,128]{2,1,0:T(8,128)(2,1)} %get-tuple-element.21), channel_id=1, source_target_pairs={{8,0},{16,8},{24,16},{0,24},{9,1},{17,9},{25,17},{1,25},{10,2},{18... | collective-permute-start | bytes 172040 | tf_op jit(solution)/shard_map/ppermute | solution.py:45
  24.3 1.3 %copy-start.3 = (bf16[7,32,128]{2,1,0:T(8,128)(2,1)}, bf16[7,32,128]{2,1,0:T(8,128)(2,1)S(1)}, u32[]{:S(2)}) copy-start(bf16[7,32,128]{2,1,0:T(8,128)(2,1)S(1)} %collective-permute-done.refs_6_.xl_hbm) | copy-start | bytes 172036
  25.6 0.6 copy-start.4
  26.2 17.2 %copy-start.6 = (bf16[7,192,128]{2,1,0:T(8,128)(2,1)S(1)}, bf16[7,192,128]{2,1,0:T(8,128)(2,1)}, u32[]{:S(2)}) copy-start(bf16[7,192,128]{2,1,0:T(8,128)(2,1)} %get-tuple-element.22) | copy-start | bytes 1032196
  26.2 17.6 %copy-start.5 = (bf16[7,192,128]{2,1,0:T(8,128)(2,1)S(1)}, bf16[7,192,128]{2,1,0:T(8,128)(2,1)}, u32[]{:S(2)}) copy-start(bf16[7,192,128]{2,1,0:T(8,128)(2,1)} %get-tuple-element.23) | copy-start | bytes 1032196
  39.8 85.4 %all-to-all-start = ((bf16[8,6,16,512]{3,2,1,0:T(8,128)(2,1)}), bf16[8,6,16,512]{3,2,1,0:T(8,128)(2,1)S(1)}, u32[]{:S(2)}, u32[]{:S(2)}) async-start(bf16[8,6,16,512]{3,2,1,0:T(8,128)(2,1)} %bitcast.8), calls=%async_computation | async-start | bytes 1572864 | tf_op jit(solution)/shard_map/all_to_all | solution.py:802
  43.4 24.5 %collective-permute-start.2 = (bf16[7,192,128]{2,1,0:T(8,128)(2,1)S(1)}, bf16[7,192,128]{2,1,0:T(8,128)(2,1)S(1)}, u32[]{:S(2)}, u32[]{:S(2)}) collective-permute-start(bf16[7,192,128]{2,1,0:T(8,128)(2,1)S(1)} %copy-done.6), channel_id=1, source_target_pairs={{0,1},{1,2},{2,3},{3,4},{4,5},{5,6},{6,7},{7,0},{8,9},{9,10},{10,1... | collective-permute-start | bytes 1032200 | tf_op jit(solution)/shard_map/ppermute | solution.py:45
  43.8 24.1 %collective-permute-start.3 = (bf16[7,192,128]{2,1,0:T(8,128)(2,1)S(1)}, bf16[7,192,128]{2,1,0:T(8,128)(2,1)S(1)}, u32[]{:S(2)}, u32[]{:S(2)}) collective-permute-start(bf16[7,192,128]{2,1,0:T(8,128)(2,1)S(1)} %copy-done.5), channel_id=1, source_target_pairs={{1,0},{2,1},{3,2},{4,3},{5,4},{6,5},{7,6},{0,7},{9,8},{10,9},{11,1... | collective-permute-start | bytes 1032200 | tf_op jit(solution)/shard_map/ppermute | solution.py:45
  67.8 0.7 copy-start.1
  67.8 0.9 copy-start.2
  82.2 21.6 %collective-permute-start.4 = (bf16[6,32,512]{2,1,0:T(8,128)(2,1)}, bf16[6,32,512]{2,1,0:T(8,128)(2,1)S(1)}, u32[]{:S(2)}, u32[]{:S(2)}) collective-permute-start(bf16[6,32,512]{2,1,0:T(8,128)(2,1)} %get-tuple-element.27), channel_id=1, source_target_pairs={{0,4},{1,5},{2,6},{3,7},{4,0},{5,1},{6,2},{7,3},{8,12},{9,13},{10,... | collective-permute-start | bytes 589832 | tf_op jit(solution)/shard_map/ppermute | solution.py:808
  86.4 19.7 %collective-permute-start.5 = (bf16[6,32,512]{2,1,0:T(8,128)(2,1)}, bf16[6,32,512]{2,1,0:T(8,128)(2,1)S(1)}, u32[]{:S(2)}, u32[]{:S(2)}) collective-permute-start(bf16[6,32,512]{2,1,0:T(8,128)(2,1)} %get-tuple-element.28), channel_id=1, source_target_pairs={{0,3},{1,4},{2,5},{3,6},{4,7},{5,0},{6,1},{7,2},{8,11},{9,12},{10,... | collective-permute-start | bytes 589832 | tf_op jit(solution)/shard_map/ppermute | solution.py:808
  86.4 39.8 %collective-permute-start.6 = (bf16[6,32,512]{2,1,0:T(8,128)(2,1)}, bf16[6,32,512]{2,1,0:T(8,128)(2,1)S(1)}, u32[]{:S(2)}, u32[]{:S(2)}) collective-permute-start(bf16[6,32,512]{2,1,0:T(8,128)(2,1)} %get-tuple-element.29), channel_id=1, source_target_pairs={{0,5},{1,6},{2,7},{3,0},{4,1},{5,2},{6,3},{7,4},{8,13},{9,14},{10,... | collective-permute-start | bytes 589832 | tf_op jit(solution)/shard_map/ppermute | solution.py:808
  89.0 37.1 %collective-permute-start.7 = (bf16[6,32,512]{2,1,0:T(8,128)(2,1)}, bf16[6,32,512]{2,1,0:T(8,128)(2,1)S(1)}, u32[]{:S(2)}, u32[]{:S(2)}) collective-permute-start(bf16[6,32,512]{2,1,0:T(8,128)(2,1)} %get-tuple-element.30), channel_id=1, source_target_pairs={{0,2},{1,3},{2,4},{3,5},{4,6},{5,7},{6,0},{7,1},{8,10},{9,11},{10,... | collective-permute-start | bytes 589832 | tf_op jit(solution)/shard_map/ppermute | solution.py:808
  89.0 37.1 %collective-permute-start.8 = (bf16[6,32,512]{2,1,0:T(8,128)(2,1)}, bf16[6,32,512]{2,1,0:T(8,128)(2,1)S(1)}, u32[]{:S(2)}, u32[]{:S(2)}) collective-permute-start(bf16[6,32,512]{2,1,0:T(8,128)(2,1)} %get-tuple-element.31), channel_id=1, source_target_pairs={{0,6},{1,7},{2,0},{3,1},{4,2},{5,3},{6,4},{7,5},{8,14},{9,15},{10,... | collective-permute-start | bytes 589832 | tf_op jit(solution)/shard_map/ppermute | solution.py:808
  103.7 22.4 %collective-permute-start.9 = (bf16[6,32,512]{2,1,0:T(8,128)(2,1)}, bf16[6,32,512]{2,1,0:T(8,128)(2,1)S(1)}, u32[]{:S(2)}, u32[]{:S(2)}) collective-permute-start(bf16[6,32,512]{2,1,0:T(8,128)(2,1)} %get-tuple-element.32), channel_id=1, source_target_pairs={{0,1},{1,2},{2,3},{3,4},{4,5},{5,6},{6,7},{7,0},{8,9},{9,10},{10,1... | collective-permute-start | bytes 589832 | tf_op jit(solution)/shard_map/ppermute | solution.py:808
  106.1 20.1 %collective-permute-start.10 = (bf16[6,32,512]{2,1,0:T(8,128)(2,1)}, bf16[6,32,512]{2,1,0:T(8,128)(2,1)S(1)}, u32[]{:S(2)}, u32[]{:S(2)}) collective-permute-start(bf16[6,32,512]{2,1,0:T(8,128)(2,1)} %get-tuple-element.33), channel_id=1, source_target_pairs={{0,7},{1,0},{2,1},{3,2},{4,3},{5,4},{6,5},{7,6},{8,15},{9,8},{10,9... | collective-permute-start | bytes 589832 | tf_op jit(solution)/shard_map/ppermute | solution.py:808
  125.2 1.1 copy-start

commit v4 on v3

--- a/solution.py
+++ b/solution.py
@@ -11,7 +11,7 @@
 BLK = 32
 TOP = 8
 ROWS = 48
-AHEAD = 2
+AHEAD = 3
 
 ion_step = 0.04
 flow_step = 0.1
@@ -79,7 +79,7 @@
     cn_hbm = take(1)[0]
     outs = take(spread)
     ends = take(2 if inner else 0)
-    rims = take(2 if inner else 0)
+    rims = take(4 if inner else 0)
     c_v, p_v, d_v, s_v = take(4)
     raw = take(5 if inner else 0)
     rim_v = take(5 if inner else 0)
@@ -146,7 +146,8 @@
             v = tmp[spot, f, picked, :]
             if f > 2:
                 v = jnp.where(solid, v, 0.0)
-            rims[n][f, at, :] = v.astype(BF16)
+            out, field = (rims[n], f) if f < 4 else (rims[2 + n], f - 4)
+            out[field, at, :] = v.astype(BF16)
 
     def fetch(i):
         for copy in loads(i):
@@ -498,8 +499,8 @@
         extra += [vm((4, nx, nz), BF16)] * 2 + [vm((4, nx, nz), F32)] * 2
     share = 0.5 if outer else 0.25
     part = jax.ShapeDtypeStruct((tiles * capacity // spread, deep, wide), BF16)
-    ends = [jax.ShapeDtypeStruct((7, number, nz), BF16) for number in (ny, ny, nx, nx)]
-    ends = ends if inner else []
+    sizes = ((7, ny), (7, ny), (4, nx), (4, nx), (3, nx), (3, nx)) if inner else ()
+    ends = [jax.ShapeDtypeStruct((fields, number, nz), BF16) for fields, number in sizes]
     return pl.pallas_call(
         functools.partial(ion_kernel, capacity, mode, spread),
         out_shape=[jax.ShapeDtypeStruct(c.shape, BF16)] + [part] * spread + ends,
@@ -601,6 +602,8 @@
     xh_hbm,
     yl_hbm,
     yh_hbm,
+    ul_hbm,
+    uh_hbm,
     un_hbm,
     u_v,
     p_v,
@@ -638,15 +641,17 @@
     pairs = (
         (xl_hbm, uxl_v),
         (xh_hbm, uxh_v),
-        (yl_hbm, uyl_v),
-        (yh_hbm, uyh_v),
+        (ul_hbm, uyl_v),
+        (uh_hbm, uyh_v),
         (xl_hbm, pxl_v),
         (xh_hbm, pxh_v),
         (yl_hbm, pyl_v),
         (yh_hbm, pyh_v),
     )
     halos = [
-        pltpu.make_async_copy(src.at[2] if n > 3 else src.at[pl.ds(4, 3)], dst, halo_sem.at[n])
+        pltpu.make_async_copy(
+            src.at[2] if n > 3 else (src.at[pl.ds(4, 3)] if n < 2 else src), dst, halo_sem.at[n]
+        )
         for n, (src, dst) in enumerate(pairs)
     ]
     for copy in halos:
@@ -758,7 +763,7 @@
         flow_kernel,
         name="flow",
         out_shape=jax.ShapeDtypeStruct(u.shape, BF16),
-        in_specs=[HBM] * 8,
+        in_specs=[HBM] * 10,
         out_specs=HBM,
         scratch_shapes=[
             vm(u.shape, BF16),
@@ -811,14 +816,15 @@
     conc, first, *ends = ion_call("inner", *given, None, None, capacity, tiles)
     first = exchange(first)
     x_halo = swap_ends(*ends[:2], "stream")
-    y_halo = swap_ends(*ends[2:], "tile")
+    y_halo = swap_ends(*ends[2:4], "tile")
     conc, second = ion_call("mid", *given, x_halo, conc, capacity, tiles)
+    u_halo = swap_ends(*ends[4:], "tile")
     second = exchange(second)
     halo = x_halo + y_halo
     conc_next, *third = ion_call("outer", *given, halo, conc, capacity, tiles)
     order = sorted(range(1, tiles), key=lambda d: -min(d, tiles - d)) + [0]
     third = [pass_on(third[d], d) for d in order]
-    flow_next = flow_call(velocity, potential, spacer, conc_next, halo)
+    flow_next = flow_call(velocity, potential, spacer, conc_next, halo + u_halo)
     none = jnp.zeros_like(me)
     owned = gather_call("inner", none, [first], (0,), None, slots, capacity)
     owned = gather_call("mid", none, [second], (0,), owned, slots, capacity)

time: 128 us -> 131 us (1.023)
  the two profiles are of different devices: /device:TPU:0 before, /device:TPU:11 now
where the time goes in v4:
time: 131 us; the launch traced here: 130 us
  Pallas kernels  56.7 us (43%)
  waiting for transfers between devices  47.7 us (36%)
  starting transfers between devices  23.9 us (18%)
  local copies, waits for them, and re-layouts  1.43 us (1%)
    ppermute x3, waiting for transfers between devices, swap_ends(): lax.ppermute(last, axis, forward)  40.7 us
    pallas_call x3, Pallas kernels, ion_call(): pl.pallas_call(functools.partial(ion_kernel, capacity, mode, spread), out...  35.9 us
    pallas_call x1, Pallas kernels, flow_call(): pl.pallas_call(flow_kernel, name='flow', out_shape=jax.ShapeDtypeStruct(u...  17.7 us
    all_to_all x2, starting transfers between devices, exchange(): part = lax.all_to_all(part, 'tile', split_axis=0, concat_axis=0, tiled=True)  12.6 us
    ppermute x3, waiting for transfers between devices, swap_ends(): lax.ppermute(first, axis, backward)  5.85 us
    ppermute x7, starting transfers between devices, pass_on(): lax.ppermute(piece, 'tile', [(i, (i + shift) % tiles) for i in range(tile...  5.54 us
    ppermute x3, starting transfers between devices, swap_ends(): lax.ppermute(last, axis, forward)  5.52 us
    pallas_call x3, Pallas kernels, gather_call(): pl.pallas_call(functools.partial(gather_kernel, boxes, capacity, shifts,...  3.06 us
  transfers between devices with their start and end apart: 15, of which 7 were waited for; matrix products, arithmetic and copies ran while one was open for 0% of the time, Pallas kernels for 33%

profile of v4, /device:TPU:11, one launch (start us, length us, event | category | flops | bytes accessed | tf_op | source)
XLA Modules:
  0.0 130.4 jit_solution(16335993010865574002)
XLA Ops:
  0.6 11.8 %shard_map.85 = (bf16[2,192,32,128]{3,2,1,0:T(8,128)(2,1)}, bf16[48,16,512]{2,1,0:T(8,128)(2,1)}, bf16[7,32,128]{2,1,0:T(8,128)(2,1)}, bf16[7,32,128]{2,1,0:T(8,...) custom-call(s32[24]{0:T(128)} %bitcast.10, ...), custom_call_target="tpu_custom_call" | custom-call | flops 19660800 | bytes 11796480 | tf_op jit(solution)/shard_map/pallas_call | solution.py:504
  12.5 5.6 %all-to-all-start.1 = ((bf16[8,6,16,512]{3,2,1,0:T(8,128)(2,1)}), bf16[8,6,16,512]{3,2,1,0:T(8,128)(2,1)S(1)}, u32[]{:S(2)}, u32[]{:S(2)}) async-start(bf16[8,6,16,512]{3,2,1,0:T(8,128)(2,1)} %bitcast.9), calls=%async_computation.1 | async-start | bytes 1572864 | tf_op jit(solution)/shard_map/all_to_all | solution.py:807
  18.1 1.2 collective-permute-start
  19.3 0.3 collective-permute-start.1
  19.6 2.1 %collective-permute-done.refs_6_.xl_hbm = bf16[7,32,128]{2,1,0:T(8,128)(2,1)S(1)} collective-permute-done((bf16[7,32,128]{2,1,0:T(8,128)(2,1)}, bf16[7,32,128]{2,1,0:T(8,128)(2,1)S(1)}, u32[]{:S(2)}, u32[]{:S(2)}) %collective-permute-start) | collective-permute-done | bytes 57376 | tf_op jit(solution)/shard_map/ppermute | solution.py:45
  21.6 2.1 %collective-permute-done.1.refs_7_.xh_hbm = bf16[7,32,128]{2,1,0:T(8,128)(2,1)S(1)} collective-permute-done((bf16[7,32,128]{2,1,0:T(8,128)(2,1)}, bf16[7,32,128]{2,1,0:T(8,128)(2,1)S(1)}, u32[]{:S(2)}, u32[]{:S(2)}) %collective-permute-start.1) | collective-permute-done | bytes 57376 | tf_op jit(solution)/shard_map/ppermute | solution.py:45
  23.8 0.0 copy-done.3
  23.8 0.6 copy-done.4
  24.4 10.1 %shard_map.86 = (bf16[2,192,32,128]{3,2,1,0:T(8,128)(2,1)}, bf16[48,16,512]{2,1,0:T(8,128)(2,1)}) custom-call(s32[24]{0:T(128)} %bitcast.11, s32[1]{0:T(128)} %bitcast.1.refs_1_.refs_0_, bf16[2,192,32,128]{3,2,1,0:T(8,128)(2,1)} %refs_2_.5, bf16[192,32,128]{2,1,0:T(8,128)(2,1)} %p_hbm.1, ...), custom_call_target="tpu_custom_call", output_to_operand_aliasing={{0}: (8, {})} | custom-call | flops 19660800 | bytes 11796480 | tf_op jit(solution)/shard_map/pallas_call | solution.py:504
  34.5 1.1 all-to-all-done.1
  35.5 7.0 %all-to-all-start = ((bf16[8,6,16,512]{3,2,1,0:T(8,128)(2,1)}), bf16[8,6,16,512]{3,2,1,0:T(8,128)(2,1)S(1)}, u32[]{:S(2)}, u32[]{:S(2)}) async-start(bf16[8,6,16,512]{3,2,1,0:T(8,128)(2,1)} %bitcast.8), calls=%async_computation | async-start | bytes 1572864 | tf_op jit(solution)/shard_map/all_to_all | solution.py:807
  42.5 0.0 copy-done.8
  42.5 1.5 %collective-permute-start.2 = (bf16[4,192,128]{2,1,0:T(8,128)(2,1)S(1)}, bf16[4,192,128]{2,1,0:T(8,128)(2,1)S(1)}, u32[]{:S(2)}, u32[]{:S(2)}) collective-permute-start(bf16[4,192,128]{2,1,0:T(8,128)(2,1)S(1)} %copy-done.8), channel_id=1, source_target_pairs={{0,1},{1,2},{2,3},{3,4},{4,5},{5,6},{6,7},{7,0},{8,9},{9,10},{10,1... | collective-permute-start | bytes 589832 | tf_op jit(solution)/shard_map/ppermute | solution.py:45
  44.0 0.0 copy-done.7
  44.0 0.0 collective-permute-start.3
  44.0 20.1 %collective-permute-done.2.refs_8_.yl_hbm = bf16[4,192,128]{2,1,0:T(8,128)(2,1)S(1)} collective-permute-done((bf16[4,192,128]{2,1,0:T(8,128)(2,1)S(1)}, bf16[4,192,128]{2,1,0:T(8,128)(2,1)S(1)}, u32[]{:S(2)}, u32[]{:S(2)}) %collective-permute-start.2) | collective-permute-done | bytes 196640 | tf_op jit(solution)/shard_map/ppermute | solution.py:45
  64.1 1.8 %collective-permute-done.3.refs_9_.yh_hbm = bf16[4,192,128]{2,1,0:T(8,128)(2,1)S(1)} collective-permute-done((bf16[4,192,128]{2,1,0:T(8,128)(2,1)S(1)}, bf16[4,192,128]{2,1,0:T(8,128)(2,1)S(1)}, u32[]{:S(2)}, u32[]{:S(2)}) %collective-permute-start.3) | collective-permute-done | bytes 196640 | tf_op jit(solution)/shard_map/ppermute | solution.py:45
  65.9 0.0 copy-done.1
  65.9 0.7 copy-done.2
  66.6 14.0 %shard_map.87 = (bf16[2,192,32,128]{3,2,1,0:T(8,128)(2,1)}, bf16[6,32,512]{2,1,0:T(8,128)(2,1)}, bf16[6,32,512]{2,1,0:T(8,128)(2,1)}, bf16[6,32,512]{2,1,0:T(8,1...) custom-call(s32[24]{0:T(128)} %bitcast.12, ...), custom_call_target="tpu_custom_call", output_to_operand_aliasing={{0}: (10, {})} | custom-call | flops 39321600 | bytes 23592960 | tf_op jit(solution)/shard_map/pallas_call | solution.py:504
  80.6 0.1 collective-permute-start.6
  80.7 0.1 collective-permute-start.7
  80.8 0.0 copy-done.10
  80.8 2.8 %collective-permute-start.4 = (bf16[3,192,128]{2,1,0:T(8,128)(2,1)S(1)}, bf16[3,192,128]{2,1,0:T(8,128)(2,1)S(1)}, u32[]{:S(2)}, u32[]{:S(2)}) collective-permute-start(bf16[3,192,128]{2,1,0:T(8,128)(2,1)S(1)} %copy-done.10), channel_id=1, source_target_pairs={{0,1},{1,2},{2,3},{3,4},{4,5},{5,6},{6,7},{7,0},{8,9},{9,10},{10,1... | collective-permute-start | bytes 442376 | tf_op jit(solution)/shard_map/ppermute | solution.py:45
  83.6 0.0 copy-done.9
  83.6 0.0 collective-permute-start.5
  83.6 2.8 %collective-permute-start.8 = (bf16[6,32,512]{2,1,0:T(8,128)(2,1)}, bf16[6,32,512]{2,1,0:T(8,128)(2,1)S(1)}, u32[]{:S(2)}, u32[]{:S(2)}) collective-permute-start(bf16[6,32,512]{2,1,0:T(8,128)(2,1)} %get-tuple-element.33), channel_id=1, source_target_pairs={{0,5},{1,6},{2,7},{3,0},{4,1},{5,2},{6,3},{7,4},{8,13},{9,14},{10,... | collective-permute-start | bytes 589832 | tf_op jit(solution)/shard_map/ppermute | solution.py:813
  86.4 18.5 %collective-permute-done.4.ul_hbm = bf16[3,192,128]{2,1,0:T(8,128)(2,1)S(1)} collective-permute-done((bf16[3,192,128]{2,1,0:T(8,128)(2,1)S(1)}, bf16[3,192,128]{2,1,0:T(8,128)(2,1)S(1)}, u32[]{:S(2)}, u32[]{:S(2)}) %collective-permute-start.4) | collective-permute-done | bytes 147488 | tf_op jit(solution)/shard_map/ppermute | solution.py:45
  104.9 0.0 collective-permute-start.9
  104.9 1.9 %collective-permute-done.5.uh_hbm = bf16[3,192,128]{2,1,0:T(8,128)(2,1)S(1)} collective-permute-done((bf16[3,192,128]{2,1,0:T(8,128)(2,1)S(1)}, bf16[3,192,128]{2,1,0:T(8,128)(2,1)S(1)}, u32[]{:S(2)}, u32[]{:S(2)}) %collective-permute-start.5) | collective-permute-done | bytes 147488 | tf_op jit(solution)/shard_map/ppermute | solution.py:45
  106.9 0.0 collective-permute-start.10
  106.9 0.0 collective-permute-done.6.refs_1_
  106.9 2.6 %collective-permute-start.11 = (bf16[6,32,512]{2,1,0:T(8,128)(2,1)}, bf16[6,32,512]{2,1,0:T(8,128)(2,1)S(1)}, u32[]{:S(2)}, u32[]{:S(2)}) collective-permute-start(bf16[6,32,512]{2,1,0:T(8,128)(2,1)} %get-tuple-element.36), channel_id=1, source_target_pairs={{0,1},{1,2},{2,3},{3,4},{4,5},{5,6},{6,7},{7,0},{8,9},{9,10},{10,1... | collective-permute-start | bytes 589832 | tf_op jit(solution)/shard_map/ppermute | solution.py:813
  109.5 0.0 collective-permute-done.7.refs_2_
  109.5 0.0 collective-permute-start.12
  109.5 0.0 copy-done.5
  109.5 0.0 copy-done.6
  109.5 17.7 %flow.1 = bf16[3,192,32,128]{3,2,1,0:T(8,128)(2,1)} custom-call(bf16[3,192,32,128]{3,2,1,0:T(8,128)(2,1)} %u_hbm.1, bf16[192,32,128]{2,1,0:T(8,128)(2,1)} %p_hbm.1, s32[192,32,128]{2,1,0:T(8,128)} %s_hbm.1, bf16[2,192,32,128]{3,2,1,0:T(8,128)(2,1)} %get-tuple-element.19.cn_hbm, bf16[7,32,128]{2,1,0:T(8,128)(2,1)} %copy-done.3, ...), custom_call_target="tpu_custom_call" | custom-call | flops 62914560 | bytes 15728640 | tf_op jit(solution)/shard_map/flow/pallas_call | solution.py:762
  127.2 0.9 shard_map.88.refs_2_
  128.1 0.0 all-to-all-done
  128.1 0.9 shard_map.89.refs_9_
  129.0 0.0 collective-permute-done.8.refs_3_
  129.0 0.0 collective-permute-done.9.refs_4_
  129.0 0.0 collective-permute-done.10.refs_5_
  129.1 0.0 collective-permute-done.11.refs_6_
  129.1 0.0 collective-permute-done.12.refs_7_
  129.1 0.1 copy-done
  129.2 1.3 shard_map.90
  (11 shorter events, 0.0 us)
Async XLA Ops:
  12.5 23.1 %all-to-all-start.1 = ((bf16[8,6,16,512]{3,2,1,0:T(8,128)(2,1)}), bf16[8,6,16,512]{3,2,1,0:T(8,128)(2,1)S(1)}, u32[]{:S(2)}, u32[]{:S(2)}) async-start(bf16[8,6,16,512]{3,2,1,0:T(8,128)(2,1)} %bitcast.9), calls=%async_computation.1 | async-start | bytes 1572864 | tf_op jit(solution)/shard_map/all_to_all | solution.py:807
  18.1 3.5 %collective-permute-start = (bf16[7,32,128]{2,1,0:T(8,128)(2,1)}, bf16[7,32,128]{2,1,0:T(8,128)(2,1)S(1)}, u32[]{:S(2)}, u32[]{:S(2)}) collective-permute-start(bf16[7,32,128]{2,1,0:T(8,128)(2,1)} %get-tuple-element.22), channel_id=1, source_target_pairs={{0,8},{8,16},{16,24},{24,0},{1,9},{9,17},{17,25},{25,1},{2,10},{10... | collective-permute-start | bytes 172040 | tf_op jit(solution)/shard_map/ppermute | solution.py:45
  19.3 4.5 %collective-permute-start.1 = (bf16[7,32,128]{2,1,0:T(8,128)(2,1)}, bf16[7,32,128]{2,1,0:T(8,128)(2,1)S(1)}, u32[]{:S(2)}, u32[]{:S(2)}) collective-permute-start(bf16[7,32,128]{2,1,0:T(8,128)(2,1)} %get-tuple-element.23), channel_id=1, source_target_pairs={{8,0},{16,8},{24,16},{0,24},{9,1},{17,9},{25,17},{1,25},{10,2},{18... | collective-permute-start | bytes 172040 | tf_op jit(solution)/shard_map/ppermute | solution.py:45
  21.6 2.1 %copy-start.3 = (bf16[7,32,128]{2,1,0:T(8,128)(2,1)}, bf16[7,32,128]{2,1,0:T(8,128)(2,1)S(1)}, u32[]{:S(2)}) copy-start(bf16[7,32,128]{2,1,0:T(8,128)(2,1)S(1)} %collective-permute-done.refs_6_.xl_hbm) | copy-start | bytes 172036
  23.8 0.6 copy-start.4
  24.4 18.1 %copy-start.8 = (bf16[4,192,128]{2,1,0:T(8,128)(2,1)S(1)}, bf16[4,192,128]{2,1,0:T(8,128)(2,1)}, u32[]{:S(2)}) copy-start(bf16[4,192,128]{2,1,0:T(8,128)(2,1)} %get-tuple-element.24) | copy-start | bytes 589828
  24.4 19.6 %copy-start.7 = (bf16[4,192,128]{2,1,0:T(8,128)(2,1)S(1)}, bf16[4,192,128]{2,1,0:T(8,128)(2,1)}, u32[]{:S(2)}) copy-start(bf16[4,192,128]{2,1,0:T(8,128)(2,1)} %get-tuple-element.25) | copy-start | bytes 589828
  35.5 92.6 %all-to-all-start = ((bf16[8,6,16,512]{3,2,1,0:T(8,128)(2,1)}), bf16[8,6,16,512]{3,2,1,0:T(8,128)(2,1)S(1)}, u32[]{:S(2)}, u32[]{:S(2)}) async-start(bf16[8,6,16,512]{3,2,1,0:T(8,128)(2,1)} %bitcast.8), calls=%async_computation | async-start | bytes 1572864 | tf_op jit(solution)/shard_map/all_to_all | solution.py:807
  42.5 21.6 %collective-permute-start.2 = (bf16[4,192,128]{2,1,0:T(8,128)(2,1)S(1)}, bf16[4,192,128]{2,1,0:T(8,128)(2,1)S(1)}, u32[]{:S(2)}, u32[]{:S(2)}) collective-permute-start(bf16[4,192,128]{2,1,0:T(8,128)(2,1)S(1)} %copy-done.8), channel_id=1, source_target_pairs={{0,1},{1,2},{2,3},{3,4},{4,5},{5,6},{6,7},{7,0},{8,9},{9,10},{10,1... | collective-permute-start | bytes 589832 | tf_op jit(solution)/shard_map/ppermute | solution.py:45
  44.0 21.9 %collective-permute-start.3 = (bf16[4,192,128]{2,1,0:T(8,128)(2,1)S(1)}, bf16[4,192,128]{2,1,0:T(8,128)(2,1)S(1)}, u32[]{:S(2)}, u32[]{:S(2)}) collective-permute-start(bf16[4,192,128]{2,1,0:T(8,128)(2,1)S(1)} %copy-done.7), channel_id=1, source_target_pairs={{1,0},{2,1},{3,2},{4,3},{5,4},{6,5},{7,6},{0,7},{9,8},{10,9},{11,1... | collective-permute-start | bytes 589832 | tf_op jit(solution)/shard_map/ppermute | solution.py:45
  64.1 1.8 %copy-start.1 = (bf16[4,192,128]{2,1,0:T(8,128)(2,1)}, bf16[4,192,128]{2,1,0:T(8,128)(2,1)S(1)}, u32[]{:S(2)}) copy-start(bf16[4,192,128]{2,1,0:T(8,128)(2,1)S(1)} %collective-permute-done.2.refs_8_.yl_hbm) | copy-start | bytes 589828
  65.9 0.7 copy-start.2
  66.6 14.2 %copy-start.10 = (bf16[3,192,128]{2,1,0:T(8,128)(2,1)S(1)}, bf16[3,192,128]{2,1,0:T(8,128)(2,1)}, u32[]{:S(2)}) copy-start(bf16[3,192,128]{2,1,0:T(8,128)(2,1)} %get-tuple-element.29) | copy-start | bytes 442372
  66.6 17.0 %copy-start.9 = (bf16[3,192,128]{2,1,0:T(8,128)(2,1)S(1)}, bf16[3,192,128]{2,1,0:T(8,128)(2,1)}, u32[]{:S(2)}) copy-start(bf16[3,192,128]{2,1,0:T(8,128)(2,1)} %get-tuple-element.30) | copy-start | bytes 442372
  80.6 26.2 %collective-permute-start.6 = (bf16[6,32,512]{2,1,0:T(8,128)(2,1)}, bf16[6,32,512]{2,1,0:T(8,128)(2,1)S(1)}, u32[]{:S(2)}, u32[]{:S(2)}) collective-permute-start(bf16[6,32,512]{2,1,0:T(8,128)(2,1)} %get-tuple-element.31), channel_id=1, source_target_pairs={{0,4},{1,5},{2,6},{3,7},{4,0},{5,1},{6,2},{7,3},{8,12},{9,13},{10,... | collective-permute-start | bytes 589832 | tf_op jit(solution)/shard_map/ppermute | solution.py:813
  80.7 28.8 %collective-permute-start.7 = (bf16[6,32,512]{2,1,0:T(8,128)(2,1)}, bf16[6,32,512]{2,1,0:T(8,128)(2,1)S(1)}, u32[]{:S(2)}, u32[]{:S(2)}) collective-permute-start(bf16[6,32,512]{2,1,0:T(8,128)(2,1)} %get-tuple-element.32), channel_id=1, source_target_pairs={{0,3},{1,4},{2,5},{3,6},{4,7},{5,0},{6,1},{7,2},{8,11},{9,12},{10,... | collective-permute-start | bytes 589832 | tf_op jit(solution)/shard_map/ppermute | solution.py:813
  80.8 24.2 %collective-permute-start.4 = (bf16[3,192,128]{2,1,0:T(8,128)(2,1)S(1)}, bf16[3,192,128]{2,1,0:T(8,128)(2,1)S(1)}, u32[]{:S(2)}, u32[]{:S(2)}) collective-permute-start(bf16[3,192,128]{2,1,0:T(8,128)(2,1)S(1)} %copy-done.10), channel_id=1, source_target_pairs={{0,1},{1,2},{2,3},{3,4},{4,5},{5,6},{6,7},{7,0},{8,9},{9,10},{10,1... | collective-permute-start | bytes 442376 | tf_op jit(solution)/shard_map/ppermute | solution.py:45
  83.6 23.2 %collective-permute-start.5 = (bf16[3,192,128]{2,1,0:T(8,128)(2,1)S(1)}, bf16[3,192,128]{2,1,0:T(8,128)(2,1)S(1)}, u32[]{:S(2)}, u32[]{:S(2)}) collective-permute-start(bf16[3,192,128]{2,1,0:T(8,128)(2,1)S(1)} %copy-done.9), channel_id=1, source_target_pairs={{1,0},{2,1},{3,2},{4,3},{5,4},{6,5},{7,6},{0,7},{9,8},{10,9},{11,1... | collective-permute-start | bytes 442376 | tf_op jit(solution)/shard_map/ppermute | solution.py:45
  83.6 45.4 %collective-permute-start.8 = (bf16[6,32,512]{2,1,0:T(8,128)(2,1)}, bf16[6,32,512]{2,1,0:T(8,128)(2,1)S(1)}, u32[]{:S(2)}, u32[]{:S(2)}) collective-permute-start(bf16[6,32,512]{2,1,0:T(8,128)(2,1)} %get-tuple-element.33), channel_id=1, source_target_pairs={{0,5},{1,6},{2,7},{3,0},{4,1},{5,2},{6,3},{7,4},{8,13},{9,14},{10,... | collective-permute-start | bytes 589832 | tf_op jit(solution)/shard_map/ppermute | solution.py:813
  104.9 4.5 %copy-start.5 = (bf16[3,192,128]{2,1,0:T(8,128)(2,1)}, bf16[3,192,128]{2,1,0:T(8,128)(2,1)S(1)}, u32[]{:S(2)}) copy-start(bf16[3,192,128]{2,1,0:T(8,128)(2,1)S(1)} %collective-permute-done.4.ul_hbm) | copy-start | bytes 442372
  104.9 24.1 %collective-permute-start.9 = (bf16[6,32,512]{2,1,0:T(8,128)(2,1)}, bf16[6,32,512]{2,1,0:T(8,128)(2,1)S(1)}, u32[]{:S(2)}, u32[]{:S(2)}) collective-permute-start(bf16[6,32,512]{2,1,0:T(8,128)(2,1)} %get-tuple-element.34), channel_id=1, source_target_pairs={{0,2},{1,3},{2,4},{3,5},{4,6},{5,7},{6,0},{7,1},{8,10},{9,11},{10,... | collective-permute-start | bytes 589832 | tf_op jit(solution)/shard_map/ppermute | solution.py:813
  106.8 2.6 %copy-start.6 = (bf16[3,192,128]{2,1,0:T(8,128)(2,1)}, bf16[3,192,128]{2,1,0:T(8,128)(2,1)S(1)}, u32[]{:S(2)}) copy-start(bf16[3,192,128]{2,1,0:T(8,128)(2,1)S(1)} %collective-permute-done.5.uh_hbm) | copy-start | bytes 442372
  106.9 22.2 %collective-permute-start.10 = (bf16[6,32,512]{2,1,0:T(8,128)(2,1)}, bf16[6,32,512]{2,1,0:T(8,128)(2,1)S(1)}, u32[]{:S(2)}, u32[]{:S(2)}) collective-permute-start(bf16[6,32,512]{2,1,0:T(8,128)(2,1)} %get-tuple-element.35), channel_id=1, source_target_pairs={{0,6},{1,7},{2,0},{3,1},{4,2},{5,3},{6,4},{7,5},{8,14},{9,15},{10,... | collective-permute-start | bytes 589832 | tf_op jit(solution)/shard_map/ppermute | solution.py:813
  106.9 22.2 %collective-permute-start.11 = (bf16[6,32,512]{2,1,0:T(8,128)(2,1)}, bf16[6,32,512]{2,1,0:T(8,128)(2,1)S(1)}, u32[]{:S(2)}, u32[]{:S(2)}) collective-permute-start(bf16[6,32,512]{2,1,0:T(8,128)(2,1)} %get-tuple-element.36), channel_id=1, source_target_pairs={{0,1},{1,2},{2,3},{3,4},{4,5},{5,6},{6,7},{7,0},{8,9},{9,10},{10,1... | collective-permute-start | bytes 589832 | tf_op jit(solution)/shard_map/ppermute | solution.py:813
  109.5 19.6 %collective-permute-start.12 = (bf16[6,32,512]{2,1,0:T(8,128)(2,1)}, bf16[6,32,512]{2,1,0:T(8,128)(2,1)S(1)}, u32[]{:S(2)}, u32[]{:S(2)}) collective-permute-start(bf16[6,32,512]{2,1,0:T(8,128)(2,1)} %get-tuple-element.37), channel_id=1, source_target_pairs={{0,7},{1,0},{2,1},{3,2},{4,3},{5,4},{6,5},{7,6},{8,15},{9,8},{10,9... | collective-permute-start | bytes 589832 | tf_op jit(solution)/shard_map/ppermute | solution.py:813
  128.1 1.1 copy-start
